TPU v7x, 256 devices: a whole 4x4x8 slice. The times are simulated.
256 devices in a mesh: tgt: 32 (over z_hi, y, x), lat: 8 (over z_lo, core).
Axes of the slice: x: 4, y: 4, z: 8 (z_hi: 2, z_lo: 4; z = z_hi * 4 + z_lo), core: 2. Of those that a mesh axis runs over, the one named last changes fastest.
Arguments:
- code_index: int32 [2, 512, 64], P(None, 'tgt'), may hold values from 0 to 16383, all different within a row
- code_value: bfloat16 [2, 512, 64], P(None, 'tgt'), may hold values from 0.5 to 4
- decoder: bfloat16 [2, 16384, 28672], P(None, 'lat', 'tgt'), may hold values from -0.25 to 0.25
- mlp_out: bfloat16 [512, 28672], P('lat', 'tgt'), may hold values from -6 to 6
Outputs:
- error: float32 [512, 28672], P('lat', 'tgt')
- code_grad: float32 [2, 512, 64], P(None, ('tgt', 'lat'))
Inputs may be any that keep to these rules, and one draw needn't show every extreme that they name: `code_index`: within one source layer, the 64 latent numbers of a token are all different.
All inputs are finite; a program needn't handle non-finite values.
Results may differ from a plain program's by a relative error of at most 0.0004.
Values may be sent and summed in bfloat16 or wider, within the bound.
No kernel may reach another device: no remote copies, remote signals or barrier semaphores. Data moves between devices by JAX's collectives and lax.ppermute only.
A program may use at most 64 MiB of HBM per device.

v0:
```python
import jax
import jax.numpy as jnp
from jax import lax
from jax.sharding import PartitionSpec as P

TARGETS = 8


def densify(index, value, lat_start, lat_width):
    sources, rows, active = index.shape
    local = index - lat_start
    inside = (local >= 0) & (local < lat_width)
    local = jnp.where(inside, local, lat_width)
    row_ids = jnp.broadcast_to(jnp.arange(rows, dtype=jnp.int32)[None, :, None], index.shape)
    source_ids = jnp.broadcast_to(jnp.arange(sources, dtype=jnp.int32)[:, None, None], index.shape)
    dense = jnp.zeros((rows, sources, lat_width), jnp.bfloat16)
    return dense.at[row_ids, source_ids, local].add(value, mode="drop")


def pick_grads(grads, index, lat_start, lat_width):
    sources = index.shape[0]
    rows = grads.shape[0]
    local = index - lat_start
    inside = (local >= 0) & (local < lat_width)
    local = jnp.clip(local, 0, lat_width - 1)
    shaped = grads.reshape(rows, sources, lat_width)
    taken = jnp.take_along_axis(shaped, jnp.transpose(local, (1, 0, 2)), axis=2)
    taken = jnp.transpose(taken, (1, 0, 2))
    return jnp.where(inside, taken, 0.0)


def body(code_index, code_value, decoder, mlp_out):
    sources, lat_width, col_width = decoder.shape
    lat_start = lax.axis_index("lat") * lat_width
    total_rows = code_index.shape[1] * lax.axis_size("tgt")
    own_block = densify(code_index, code_value, lat_start, lat_width)
    dense = lax.all_gather(own_block, "tgt", axis=0, tiled=True)
    flat_codes = dense.reshape(total_rows, sources * lat_width)
    w_flat = decoder.reshape(sources * lat_width, col_width)
    block = flat_codes
    recon_own = lax.psum_scatter(
        jnp.dot(block, w_flat, preferred_element_type=jnp.float32),
        "lat",
        scatter_dimension=0,
        tiled=True,
    )
    error = recon_own - mlp_out.astype(jnp.float32)
    error_all = lax.all_gather(error, "lat", axis=0, tiled=True)
    block = error_all
    grads_own = lax.psum_scatter(
        jnp.dot(
            block, w_flat.T, precision=lax.Precision.HIGHEST, preferred_element_type=jnp.float32
        ),
        "tgt",
        scatter_dimension=0,
        tiled=True,
    )
    picked = pick_grads(grads_own, code_index, lat_start, lat_width)
    summed = lax.psum_scatter(picked, "lat", scatter_dimension=1, tiled=True)
    return (error, summed / TARGETS)


def solution(mesh):
    placed = (P(None, "tgt", None), P(None, "tgt", None), P(None, "lat", "tgt"), P("lat", "tgt"))
    return jax.shard_map(
        body,
        mesh=mesh,
        in_specs=placed,
        out_specs=(P("lat", "tgt"), P(None, ("tgt", "lat"), None)),
        check_vma=False,
    )
```

profile of v0, /device:TPU:1, one launch (start us, length us, event | category | flops | bytes accessed | tf_op | source)
XLA Modules:
  0.0 570.0 jit_solution(16276096870627105844)
XLA Ops:
  7.2 0.0 all-gather.3.cloned.1.call-start
  7.2 0.7 fusion.3
  8.0 0.8 multiply_reduce_fusion
  8.8 0.8 and_reduce_fusion
  9.6 0.1 reshape.33
  9.6 0.8 reshape.35
  10.4 14.7 %scatter_custom_fusion = bf16[65536]{0:T(1024)(128)(2,1)S(1)} fusion(s32[2048]{0:T(1024)S(1)} %reshape.33, bf16[2048]{0:T(1024)(128)(2,1)S(1)} %reshape.35, bf16[]{:T(256)} %constant.10.clone.1), kind=kCustom, calls=%fused_computation.5 | custom fusion | flops 2048 | bytes 131074
  25.1 0.7 copy.14
  25.8 0.0 all-gather.3.cloned.1.call-update
  25.9 0.0 copy-start.1
  25.9 0.0 reduce-scatter.3.cloned.1.call-start
  25.9 108.9 %all-gather.3.cloned.1.call-done = bf16[512,2,2048]{2,0,1:T(8,128)(2,1)} async-done(((bf16[16,2,2048]{2,0,1:T(8,128)(2,1)}), bf16[512,2,2048]{2,0,1:T(8,128)(2,1)}) %all-gather.3.cloned.1.call-update) | async-done | bytes 4194320 | tf_op jit(solution)/shard_map/all_gather | solution.py:37
  134.9 10.1 %convolution_bitcast_fusion = f32[512,896]{1,0:T(8,128)} fusion(bf16[512,2,2048]{2,0,1:T(8,128)(2,1)} %all-gather.3.cloned.1.call-done, bf16[2,2048,896]{2,1,0:T(8,128)(2,1)} %param.6), kind=kOutput, calls=%fused_computation.2 | convolution fusion | flops 3758096384 | bytes 13369344 | tf_op jit(solution)/shard_map/dot_general | solution.py:42
  145.0 0.0 reduce-scatter.3.cloned.1.call-update
  145.0 0.0 all-gather.5.cloned.1.call-start
  145.0 38.7 %reduce-scatter.3.cloned.1.call-done = f32[64,896]{1,0:T(8,128)} async-done(((f32[512,896]{1,0:T(8,128)}), f32[64,896]{1,0:T(8,128)}) %reduce-scatter.3.cloned.1.call-update) | async-done | bytes 229392 | tf_op jit(solution)/shard_map/reduce_scatter | solution.py:41
  183.8 0.0 copy-done.1
  183.8 1.6 convert_subtract_fusion
  185.4 0.0 all-gather.5.cloned.1.call-update
  185.5 0.2 reduce-scatter.5.cloned.1.call-start
  185.7 38.0 %all-gather.5.cloned.1.call-done = f32[512,896]{1,0:T(8,128)} async-done(((f32[64,896]{1,0:T(8,128)}), f32[512,896]{1,0:T(8,128)}) %all-gather.5.cloned.1.call-update) | async-done | bytes 1835024 | tf_op jit(solution)/shard_map/all_gather | solution.py:48
  223.6 18.1 %fusion.8 = f32[512,4096]{1,0:T(8,128)} fusion(f32[512,896]{1,0:T(8,128)} %all-gather.5.cloned.1.call-done, bf16[4096,896]{1,0:T(8,128)(2,1)} %bitcast.20), kind=kOutput, calls=%fused_computation.23 | convolution fusion | flops 22548578304 | bytes 17563648 | tf_op jit(solution)/shard_map/dot_general | solution.py:51
  241.7 0.0 copy-start
  241.7 0.0 copy-start.2
  241.7 0.0 reduce-scatter.5.cloned.1.call-update
  241.7 0.7 copy-done
  242.5 0.1 reshape.27
  242.5 0.0 copy-done.2
  242.5 0.6 dynamic-slice
  243.8 265.0 %reduce-scatter.5.cloned.1.call-done = f32[16,4096]{1,0:T(8,128)} async-done(((f32[512,4096]{1,0:T(8,128)}), f32[16,4096]{1,0:T(8,128)}) %reduce-scatter.5.cloned.1.call-update) | async-done | bytes 262160 | tf_op jit(solution)/shard_map/reduce_scatter | solution.py:50
  508.8 1.2 reshape.21
  510.0 20.5 %gather_fusion = f32[2048]{0:T(1024)S(1)} fusion(f32[16,2,2048]{2,1,0:T(2,128)S(1)} %reshape.21, s32[2048]{0:T(1024)S(1)} %reshape.27), kind=kCustom, calls=%fused_computation | custom fusion | bytes 40960 | tf_op jit(solution)/shard_map/jit(take_along_axis)/gather | solution.py:27
  530.5 0.1 reshape.30
  530.6 32.3 %all-reduce = f32[2,16,64]{2,0,1:T(2,128)S(1)} all-reduce(f32[2,16,64]{2,0,1:T(2,128)S(1)} %fusion.2), channel_id=4, replica_groups=mesh['tgt'=32,'lat'=8] {'lat'}, use_global_device_ids=true, to_apply=%region_3.4.clone | all-reduce | flops 2048 | bytes 16384
  562.9 0.6 copy.15
  (8 shorter events, 0.1 us)
Async XLA Ops:
  7.2 127.7 %all-gather.3.cloned.1.call-start = ((), (), s32[]{:S(2)}) async-start(), calls=%async_computation.2 | async-start | bytes 4325376 | tf_op jit(solution)/shard_map/all_gather | solution.py:37
  25.9 157.9 %copy-start.1 = (bf16[64,896]{1,0:T(8,128)(2,1)S(1)}, bf16[64,896]{1,0:T(8,128)(2,1)}, u32[]{:S(2)}) copy-start(bf16[64,896]{1,0:T(8,128)(2,1)} %param.7) | copy-start | bytes 344068
  25.9 157.9 %reduce-scatter.3.cloned.1.call-start = ((), (), s32[]{:S(2)}) async-start(), calls=%async_computation.3 | async-start | bytes 2064384 | tf_op jit(solution)/shard_map/reduce_scatter | solution.py:41
  145.0 78.6 %all-gather.5.cloned.1.call-start = ((), (), s32[]{:S(2)}) async-start(), calls=%async_computation.4 | async-start | bytes 2064384 | tf_op jit(solution)/shard_map/all_gather | solution.py:48
  185.5 323.4 %reduce-scatter.5.cloned.1.call-start = ((), (), s32[]{:S(2)}) async-start(), calls=%async_computation.5 | async-start | bytes 8650752 | tf_op jit(solution)/shard_map/reduce_scatter | solution.py:50
  241.7 0.7 copy-start
  241.7 0.8 copy-start.2
Sparse Core Ops, SparseCore 0:
  26.0 108.8 all-gather.2
  145.1 38.6 reduce-scatter.2
  186.1 37.4 all-gather.4
  241.8 266.9 reduce-scatter.4
where the time goes:
time: 571 us; the launch traced here: 570 us
  waiting for transfers between devices  451 us (79%)
  blocking collectives  32.3 us (6%)
  matrix products  28.2 us (5%)
  local copies, waits for them, and re-layouts  25.3 us (4%)
  other arithmetic  18.7 us (3%)
  between operations  14.5 us (3%)
    reduce_scatter x1, waiting for transfers between devices, body(): lax.psum_scatter(jnp.dot(block, w_flat.T, precision=lax.Precision.HIGHEST...  265 us
    all_gather x1, waiting for transfers between devices, body(): dense = lax.all_gather(own_block, 'tgt', axis=0, tiled=True)  109 us
    reduce_scatter x1, waiting for transfers between devices, body(): lax.psum_scatter(jnp.dot(block, w_flat, preferred_element_type=jnp.float3...  38.7 us
    all_gather x1, waiting for transfers between devices, body(): error_all = lax.all_gather(error, 'lat', axis=0, tiled=True)  38 us
    unnamed x1, blocking collectives  32.3 us
    gather x3, local copies, waits for them, and re-layouts, pick_grads(): taken = jnp.take_along_axis(shaped, jnp.transpose(local, (1, 0, 2)), axis=2)  20.6 us
    dot_general x1, matrix products, body(): jnp.dot(block, w_flat.T, precision=lax.Precision.HIGHEST, preferred_eleme...  18.1 us
    unnamed x4, other arithmetic  16.2 us
  transfers between devices with their start and end apart: 4, of which 4 were waited for; matrix products, arithmetic and copies ran while one was open for 0% of the time, Pallas kernels for 0%

commit v1 on v0

v1 whole, which is shorter than its diff:
```python
import jax
import jax.numpy as jnp
from jax import lax
from jax.experimental import pallas as pl
from jax.experimental.pallas import tpu as pltpu
from jax.sharding import PartitionSpec as P

TARGETS = 8
LO = 128
NT = (((1,), (1,)), ((), ()))


def tgt_shift(zh):
    return [(t, t ^ (zh << 4)) for t in range(32)]


def lat_xor(d):
    return [(i, i ^ d) for i in range(8)]


def decode_kernel(x_ref, w_hbm, mine_ref, theirs_ref, codes_ref, w_ref, acc_ref, sem):
    chunks = codes_ref.shape[0]
    per_source = chunks // 2
    width = per_source * LO
    lat = lax.axis_index("lat")
    core = lat % 2
    start = lat * width
    steps = 8
    rows_w = w_hbm.shape[0] // steps
    for i in range(steps):
        part = pl.ds(i * rows_w, rows_w)
        pltpu.make_async_copy(w_hbm.at[part], w_ref.at[part], sem.at[i]).start()

    half_lane = lax.broadcasted_iota(jnp.int32, (1, 128), 1) < 64
    row_hi = lax.broadcasted_iota(jnp.int32, (per_source * 8, 128), 0)
    row_lo = lax.broadcasted_iota(jnp.int32, (LO, 128), 0)

    def densify(b, carry):
        block = x_ref[b]
        local = block[0:16].astype(jnp.int32) - start
        inside = (local >= 0) & (local < width)
        hi = jnp.where(inside, (local >> 7) * 8, -1024)
        lo = local & (LO - 1)
        val = block[16:32]
        rolled = [pltpu.roll(a, 64, 1) for a in (hi, lo, val)]

        def pair(i, t, source):
            plain = (hi, lo, val)[i]
            turned = rolled[i]
            first, second = (plain, turned) if source == 0 else (turned, plain)
            return jnp.where(half_lane, first[t : t + 1], second[t + 1 : t + 2])

        yx = b // 2
        zh = b % 2
        token = pl.multiple_of(zh * 256 + yx * 16, 16)
        for source in range(2):
            halves = []
            for t0 in (0, 8):
                lhs, rhs = [], []
                for j in range(4):
                    t = t0 + 2 * j
                    slot = jnp.where(half_lane, 2 * j, 2 * j + 1)
                    key = pair(0, t, source) + slot
                    lhs.append(jnp.where(row_hi == key, pair(2, t, source), 0.0).astype(jnp.bfloat16))
                    rhs.append(jnp.where(row_lo == pair(1, t, source), 1.0, 0.0).astype(jnp.bfloat16))
                dense = lax.dot_general(
                    jnp.concatenate(lhs, axis=1),
                    jnp.concatenate(rhs, axis=1),
                    NT,
                    preferred_element_type=jnp.float32,
                )
                halves.append(dense.reshape(per_source, 8, LO))
            both = jnp.concatenate(halves, axis=1).astype(jnp.bfloat16)
            codes_ref[source * per_source : (source + 1) * per_source, pl.ds(token, 16), :] = both
        return carry

    lax.fori_loop(0, x_ref.shape[0], densify, 0)

    per_step = chunks // steps
    for i in range(steps):
        part = pl.ds(i * rows_w, rows_w)
        pltpu.make_async_copy(w_hbm.at[part], w_ref.at[part], sem.at[i]).wait()
        lhs = jnp.concatenate([codes_ref[i * per_step + j] for j in range(per_step)], axis=1)
        out = jnp.dot(lhs, w_ref[i * rows_w : (i + 1) * rows_w, :], preferred_element_type=jnp.float32)
        if i == 0:
            acc_ref[...] = out
        else:
            acc_ref[...] += out
    for z in range(4):
        mine_ref[z] = acc_ref[pl.ds(pl.multiple_of(z * 128 + core * 64, 64), 64), :]
        theirs_ref[z] = acc_ref[pl.ds(pl.multiple_of(z * 128 + (1 - core) * 64, 64), 64), :]


def decode(x, w):
    tokens, cols = 512, w.shape[1]
    part = jax.ShapeDtypeStruct((4, tokens // 8, cols), jnp.float32)
    return pl.pallas_call(
        decode_kernel,
        out_shape=(part, part),
        in_specs=[pl.BlockSpec(memory_space=pltpu.VMEM), pl.BlockSpec(memory_space=pl.ANY)],
        out_specs=(pl.BlockSpec(memory_space=pltpu.VMEM), pl.BlockSpec(memory_space=pltpu.VMEM)),
        scratch_shapes=[
            pltpu.VMEM((w.shape[0] // LO, tokens, LO), jnp.bfloat16),
            pltpu.VMEM(w.shape, jnp.bfloat16),
            pltpu.VMEM((tokens, cols), jnp.float32),
            pltpu.SemaphoreType.DMA((8,)),
        ],
        compiler_params=pltpu.CompilerParams(vmem_limit_bytes=48 << 20),
        name="decode",
    )(x, w)


def grads_kernel(x_ref, *refs):
    blocks = refs[:8]
    w_ref, out_ref, err_ref, key_ref, lo_ref = refs[8:]
    step = pl.program_id(0)
    per_step = w_ref.shape[0] // LO
    per_source = per_step * pl.num_programs(0) // 2
    tokens = out_ref.shape[0]
    lat = lax.axis_index("lat")

    @pl.when(step == 0)
    def _():
        core = lat % 2
        z = lat // 2
        for n, ref in enumerate(blocks):
            d, side = n % 4, n // 4
            c = core if side == 0 else 1 - core
            row = pl.multiple_of((z ^ d) * 128 + c * 64, 64)
            e = ref[...]
            high = e.astype(jnp.bfloat16)
            err_ref[pl.ds(row, 64), :] = high
            err_ref[pl.ds(pl.multiple_of(tokens + row, 64), 64), :] = (e - high.astype(jnp.float32)).astype(jnp.bfloat16)
        width = per_source * LO
        source = lax.broadcasted_iota(jnp.int32, (16, 128), 1) // 64
        for b in range(32):
            local = x_ref[b, 0:16, :].astype(jnp.int32) - lat * width
            inside = (local >= 0) & (local < width)
            row = (b % 2) * 256 + (b // 2) * 16
            key_ref[row : row + 16, :] = jnp.where(inside, (local >> 7) + source * per_source, -1)
            lo_ref[row : row + 16, :] = local & (LO - 1)
        out_ref[...] = jnp.zeros_like(out_ref)

    grads = lax.dot_general(err_ref[...], w_ref[...], NT, preferred_element_type=jnp.float32)
    grads = grads[:tokens] + grads[tokens:]
    key = key_ref[...]
    lo = lo_ref[...]
    picked = out_ref[...]
    for j in range(per_step):
        found = jnp.take_along_axis(grads[:, j * LO : (j + 1) * LO], lo, axis=1)
        picked = jnp.where(key == step * per_step + j, found, picked)
    out_ref[...] = picked


def grads(x, blocks, w):
    tokens, cols = 512, w.shape[1]
    tile = 256
    whole = lambda a: pl.BlockSpec(a.shape, lambda i: (0,) * a.ndim)
    return pl.pallas_call(
        grads_kernel,
        out_shape=jax.ShapeDtypeStruct((tokens, 128), jnp.float32),
        grid=(w.shape[0] // tile,),
        in_specs=[whole(x)] + [whole(b) for b in blocks] + [pl.BlockSpec((tile, cols), lambda i: (i, 0))],
        out_specs=pl.BlockSpec((tokens, 128), lambda i: (0, 0)),
        scratch_shapes=[
            pltpu.VMEM((2 * tokens, cols), jnp.bfloat16),
            pltpu.VMEM((tokens, 128), jnp.int32),
            pltpu.VMEM((tokens, 128), jnp.int32),
        ],
        compiler_params=pltpu.CompilerParams(vmem_limit_bytes=48 << 20),
        name="grads",
    )(x, *blocks, w)


def body(code_index, code_value, decoder, mlp_out):
    sources, lat_width, cols = decoder.shape
    w = decoder.reshape(sources * lat_width, cols)
    rows = code_index.shape[1]
    lat = lax.axis_index("lat")
    z = lat // 2
    zh = lax.axis_index("tgt") // 16

    index = jnp.transpose(code_index, (1, 0, 2)).reshape(rows, 128).astype(jnp.float32)
    value = jnp.transpose(code_value, (1, 0, 2)).reshape(rows, 128).astype(jnp.float32)
    own = jnp.concatenate([index, value], axis=0)
    other = lax.ppermute(own, "tgt", tgt_shift(1))
    both = jnp.where(zh == 0, jnp.stack([own, other]), jnp.stack([other, own]))
    groups = [[a * 16 + i for i in range(16)] for a in range(2)]
    sent = jnp.broadcast_to(both[None], (16,) + both.shape).reshape(32, 2 * rows, 128)
    x = lax.all_to_all(sent, "tgt", 0, 0, tiled=True, axis_index_groups=groups)

    mine, theirs = decode(x, w)
    chip = mine + lax.ppermute(theirs, "lat", lat_xor(1))
    near = [
        lax.ppermute(lax.dynamic_index_in_dim(chip, z ^ d, 0, keepdims=False), "lat", lat_xor(2 * d))
        for d in (1, 2, 3)
    ]
    error = lax.dynamic_index_in_dim(chip, z, 0, keepdims=False) + near[0] + near[1] + near[2]
    error = error - mlp_out.astype(jnp.float32)

    blocks = [error] + [lax.ppermute(error, "lat", lat_xor(2 * d)) for d in (1, 2, 3)]
    blocks = blocks + [lax.ppermute(b, "lat", lat_xor(1)) for b in blocks]
    picked = grads(x, blocks, w)
    parts = lax.all_to_all(picked, ("tgt", "lat"), 0, 0, tiled=True)
    total = jnp.sum(parts.reshape(256, 2, sources, 64), axis=0)
    return (error, jnp.transpose(total, (1, 0, 2)) / TARGETS)


def solution(mesh):
    placed = (P(None, "tgt", None), P(None, "tgt", None), P(None, "lat", "tgt"), P("lat", "tgt"))
    return jax.shard_map(
        body,
        mesh=mesh,
        in_specs=placed,
        out_specs=(P("lat", "tgt"), P(None, ("tgt", "lat"), None)),
        check_vma=False,
    )
```

time: 571 us -> 140 us (0.25)
  waiting for transfers between devices: 451 us -> 27.9 us
  Pallas kernels: 0 us -> 35.1 us
  starting transfers between devices: 0.34 us -> 29.9 us
  matrix products: 28.2 us -> 0 us
  local copies, waits for them, and re-layouts: 25.3 us -> 0.98 us
  other arithmetic: 18.7 us -> 1.89 us
  between operations: 14.5 us -> 0.72 us
  blocking collectives: 32.3 us -> 42.6 us
    reduce_scatter x2 -> x0, waiting for transfers between devices: 304 us -> none  [the longest x1 265 us: body(): lax.psum_scatter(jnp.dot(block, w_flat.T, precision=lax.Precision.HIGHEST...]
    all_gather x2 -> x0, waiting for transfers between devices: 147 us -> none  [the longest x1 109 us: body(): dense = lax.all_gather(own_block, 'tgt', axis=0, tiled=True)]
    all_to_all x0 -> x2, blocking collectives: none -> 42.6 us  [the longest x1 26.1 us: body(): parts = lax.all_to_all(picked, ('tgt', 'lat'), 0, 0, tiled=True)]
    pallas_call x0 -> x2, Pallas kernels: none -> 35.1 us  [the longest x1 17.7 us: decode(): pl.pallas_call(decode_kernel, out_shape=(part, part), in_specs=[pl.BlockS...]
    unnamed x1 -> x0, blocking collectives: 32.3 us -> none
    ppermute x0 -> x12, starting transfers between devices: none -> 29.9 us  [the longest x4 12.2 us: body(): blocks = blocks + [lax.ppermute(b, 'lat', lat_xor(1)) for b in blocks]]
    dot_general x2 -> x0, matrix products: 28.2 us -> none  [the longest x1 18.1 us: body(): jnp.dot(block, w_flat.T, precision=lax.Precision.HIGHEST, preferred_eleme...]
    ppermute x0 -> x12, waiting for transfers between devices: none -> 27.9 us  [the longest x3 18.4 us: body(): lax.ppermute(lax.dynamic_index_in_dim(chip, z ^ d, 0, keepdims=False), 'l...]
  transfers between devices with their start and end apart: 4 -> 12, of which waited for: 4 -> 7; matrix products, arithmetic and copies ran while one was open for 0% -> 0% of each run, Pallas kernels for 0% -> 0%
where the time goes in v1:
time: 140 us; the launch traced here: 139 us
  blocking collectives  42.6 us (30%)
  Pallas kernels  35.1 us (25%)
  starting transfers between devices  29.9 us (21%)
  waiting for transfers between devices  27.9 us (20%)
  other arithmetic  1.89 us (1%)
    all_to_all x1, blocking collectives, body(): parts = lax.all_to_all(picked, ('tgt', 'lat'), 0, 0, tiled=True)  26.1 us
    ppermute x3, waiting for transfers between devices, body(): lax.ppermute(lax.dynamic_index_in_dim(chip, z ^ d, 0, keepdims=False), 'l...  18.4 us
    pallas_call x1, Pallas kernels, decode(): pl.pallas_call(decode_kernel, out_shape=(part, part), in_specs=[pl.BlockS...  17.7 us
    pallas_call x1, Pallas kernels, grads(): pl.pallas_call(grads_kernel, out_shape=jax.ShapeDtypeStruct((tokens, 128)...  17.4 us
    all_to_all x1, blocking collectives, body(): x = lax.all_to_all(sent, 'tgt', 0, 0, tiled=True, axis_index_groups=groups)  16.6 us
    ppermute x4, starting transfers between devices, body(): blocks = blocks + [lax.ppermute(b, 'lat', lat_xor(1)) for b in blocks]  12.2 us
    ppermute x1, starting transfers between devices, body(): other = lax.ppermute(own, 'tgt', tgt_shift(1))  7.76 us
    ppermute x3, waiting for transfers between devices, body(): lax.ppermute(error, 'lat', lat_xor(2 * d))  4.75 us
  transfers between devices with their start and end apart: 12, of which 7 were waited for; matrix products, arithmetic and copies ran while one was open for 0% of the time, Pallas kernels for 0%

profile of v1, /device:TPU:1, one launch (start us, length us, event | category | flops | bytes accessed | tf_op | source)
XLA Modules:
  0.0 139.1 jit_solution(10041967275735471037)
XLA Ops:
  0.6 0.0 copy-start.1
  0.6 0.8 convert_bitcast_fusion.1
  1.4 0.1 convert_element_type.23
  1.5 0.7 convert_bitcast_fusion
  2.2 0.1 reshape.57
  2.3 7.8 %collective-permute-start = (f32[32,128]{1,0:T(8,128)S(1)}, f32[32,128]{1,0:T(8,128)S(1)}, u32[]{:S(2)}, u32[]{:S(2)}) collective-permute-start(f32[32,128]{1,0:T(8,128)S(1)} %constant_dynamic-update-slice_fusion), channel_id=1, source_target_pairs={{0,128},{8,136},{16,144},{24,152},{32,160},{40,168},{48,176},{56,1... | collective-permute-start | bytes 49160 | tf_op jit(solution)/shard_map/ppermute | solution.py:186
  10.1 1.1 collective-permute-done
  11.2 0.1 broadcast_in_dim.2
  11.2 16.6 %all_to_all.14.x_ref = f32[32,32,128]{2,1,0:T(8,128)S(1)} all-to-all(f32[32,32,128]{2,1,0:T(8,128)S(1)} %bitcast.27), channel_id=1, replica_groups={{0,8,16,24,32,40,48,56,64,72,80,88,96,104,112,120},{128,136,144,152,160..., dimensions={0} | all-to-all | bytes 1048576 | tf_op jit(solution)/shard_map/all_to_all | solution.py:190
  27.8 17.7 %decode.1 = (f32[4,64,896]{2,1,0:T(8,128)S(1)}, f32[4,64,896]{2,1,0:T(8,128)S(1)}) custom-call(f32[32,32,128]{2,1,0:T(8,128)S(1)} %all_to_all.14.x_ref, bf16[4096,896]{1,0:T(8,128)(2,1)} %bitcast.25), custom_call_target="tpu_custom_call" | custom-call | tf_op jit(solution)/shard_map/decode/pallas_call | solution.py:97
  45.5 2.6 %collective-permute-start.1 = (f32[4,64,896]{2,1,0:T(8,128)S(1)}, f32[4,64,896]{2,1,0:T(8,128)S(1)}, u32[]{:S(2)}, u32[]{:S(2)}) collective-permute-start(f32[4,64,896]{2,1,0:T(8,128)S(1)} %get-tuple-element.5), channel_id=1, source_target_pairs={{0,1},{1,0},{2,3},{3,2},{4,5},{5,4},{6,7},{7,6},{8,9},{9,8},{10,11... | collective-permute-start | bytes 2752520 | tf_op jit(solution)/shard_map/ppermute | solution.py:193
  48.1 2.1 %collective-permute-done.1 = f32[4,64,896]{2,1,0:T(8,128)S(1)} collective-permute-done((f32[4,64,896]{2,1,0:T(8,128)S(1)}, f32[4,64,896]{2,1,0:T(8,128)S(1)}, u32[]{:S(2)}, u32[]{:S(2)}) %collective-permute-start.1) | collective-permute-done | bytes 917536 | tf_op jit(solution)/shard_map/ppermute | solution.py:193
  50.2 0.1 add.27
  50.3 0.1 dynamic-slice_bitcast_fusion.2
  50.4 2.9 %collective-permute-start.4 = (f32[64,896]{1,0:T(8,128)S(1)}, f32[64,896]{1,0:T(8,128)S(1)}, u32[]{:S(2)}, u32[]{:S(2)}) collective-permute-start(f32[64,896]{1,0:T(8,128)S(1)} %get-tuple-element.9), channel_id=1, source_target_pairs={{0,6},{1,7},{2,4},{3,5},{4,2},{5,3},{6,0},{7,1},{8,14},{9,15},{10,... | collective-permute-start | bytes 688136 | tf_op jit(solution)/shard_map/ppermute | solution.py:195
  53.3 0.0 collective-permute-start.3
  53.3 0.7 collective-permute-start.2
  54.0 5.1 %collective-permute-done.4 = f32[64,896]{1,0:T(8,128)S(1)} collective-permute-done((f32[64,896]{1,0:T(8,128)S(1)}, f32[64,896]{1,0:T(8,128)S(1)}, u32[]{:S(2)}, u32[]{:S(2)}) %collective-permute-start.4) | collective-permute-done | bytes 229408 | tf_op jit(solution)/shard_map/ppermute | solution.py:195
  59.1 13.3 %collective-permute-done.3 = f32[64,896]{1,0:T(8,128)S(1)} collective-permute-done((f32[64,896]{1,0:T(8,128)S(1)}, f32[64,896]{1,0:T(8,128)S(1)}, u32[]{:S(2)}, u32[]{:S(2)}) %collective-permute-start.3) | collective-permute-done | bytes 229408 | tf_op jit(solution)/shard_map/ppermute | solution.py:195
  72.5 0.0 collective-permute-done.2
  72.5 0.0 copy-done.1
  72.5 0.1 fusion.2.refs_0_
  72.5 0.0 copy-start
  72.5 0.1 collective-permute-start.5
  72.6 2.2 %collective-permute-start.6 = (f32[64,896]{1,0:T(8,128)S(1)}, f32[64,896]{1,0:T(8,128)S(1)}, u32[]{:S(2)}, u32[]{:S(2)}) collective-permute-start(f32[64,896]{1,0:T(8,128)S(1)} %fusion.2.refs_0_), channel_id=1, source_target_pairs={{0,4},{1,5},{2,6},{3,7},{4,0},{5,1},{6,2},{7,3},{8,12},{9,13},{10,... | collective-permute-start | bytes 688136 | tf_op jit(solution)/shard_map/ppermute | solution.py:201
  74.8 1.4 collective-permute-start.7
  76.2 2.1 %collective-permute-start.8 = (f32[64,896]{1,0:T(8,128)S(1)}, f32[64,896]{1,0:T(8,128)S(1)}, u32[]{:S(2)}, u32[]{:S(2)}) collective-permute-start(f32[64,896]{1,0:T(8,128)S(1)} %fusion.2.refs_0_), channel_id=1, source_target_pairs={{0,1},{1,0},{2,3},{3,2},{4,5},{5,4},{6,7},{7,6},{8,9},{9,8},{10,11... | collective-permute-start | bytes 688136 | tf_op jit(solution)/shard_map/ppermute | solution.py:202
  78.2 4.7 %collective-permute-done.5.refs_1_ = f32[64,896]{1,0:T(8,128)S(1)} collective-permute-done((f32[64,896]{1,0:T(8,128)S(1)}, f32[64,896]{1,0:T(8,128)S(1)}, u32[]{:S(2)}, u32[]{:S(2)}) %collective-permute-start.5) | collective-permute-done | bytes 229408 | tf_op jit(solution)/shard_map/ppermute | solution.py:201
  83.0 1.5 %collective-permute-start.9 = (f32[64,896]{1,0:T(8,128)S(1)}, f32[64,896]{1,0:T(8,128)S(1)}, u32[]{:S(2)}, u32[]{:S(2)}) collective-permute-start(f32[64,896]{1,0:T(8,128)S(1)} %collective-permute-done.5.refs_1_), channel_id=1, source_target_pairs={{0,1},{1,0},{2,3},{3,2},{4,5},{5,4},{6,7},{7,6},{8,9},{9,8},{10,11... | collective-permute-start | bytes 688136 | tf_op jit(solution)/shard_map/ppermute | solution.py:202
  84.5 0.0 collective-permute-done.6.refs_2_
  84.5 8.7 %collective-permute-start.10 = (f32[64,896]{1,0:T(8,128)S(1)}, f32[64,896]{1,0:T(8,128)S(1)}, u32[]{:S(2)}, u32[]{:S(2)}) collective-permute-start(f32[64,896]{1,0:T(8,128)S(1)} %collective-permute-done.6.refs_2_), channel_id=1, source_target_pairs={{0,1},{1,0},{2,3},{3,2},{4,5},{5,4},{6,7},{7,6},{8,9},{9,8},{10,11... | collective-permute-start | bytes 688136 | tf_op jit(solution)/shard_map/ppermute | solution.py:202
  93.2 0.0 collective-permute-done.7.refs_3_
  93.2 0.0 collective-permute-start.11
  93.2 0.0 collective-permute-done.8.refs_4_
  93.2 0.0 collective-permute-done.9.refs_5_
  93.2 1.1 collective-permute-done.10.refs_6_
  94.3 0.4 collective-permute-done.11.refs_7_
  94.6 17.4 %grads.1 = f32[512,128]{1,0:T(8,128)S(1)} custom-call(f32[32,32,128]{2,1,0:T(8,128)S(1)} %all_to_all.14.x_ref, f32[64,896]{1,0:T(8,128)S(1)} %fusion.2.refs_0_, f32[64,896]{1,0:T(8,128)S(1)} %collective-permute-done.5.refs_1_, f32[64,896]{1,0:T(8,128)S(1)} %collective-permute-done.6.refs_2_, f32[64,896]{1,0:T(8,128)S(1)} %collective-permute-done.7.refs_3_, ...), custom_call_target="tpu_custom_call" | custom-call | tf_op jit(solution)/shard_map/grads/pallas_call | solution.py:159
  112.0 26.1 %all_to_all.15 = f32[256,2,128]{2,1,0:T(2,128)S(1)} all-to-all(f32[256,2,128]{2,1,0:T(2,128)S(1)} %bitcast.24), channel_id=1, replica_groups=mesh['tgt'=32,'lat'=8] {'tgt','lat'}, dimensions={0} | all-to-all | bytes 524288 | tf_op jit(solution)/shard_map/all_to_all | solution.py:204
  138.1 0.3 reduce_sum.9
  138.4 0.1 div.33
  138.5 0.6 copy.8
  139.1 0.0 copy-done
  (6 shorter events, 0.0 us)
Async XLA Ops:
  0.6 71.8 %copy-start.1 = (bf16[64,896]{1,0:T(8,128)(2,1)S(1)}, bf16[64,896]{1,0:T(8,128)(2,1)}, u32[]{:S(2)}) copy-start(bf16[64,896]{1,0:T(8,128)(2,1)} %param.7) | copy-start | bytes 344068
  2.3 8.9 %collective-permute-start = (f32[32,128]{1,0:T(8,128)S(1)}, f32[32,128]{1,0:T(8,128)S(1)}, u32[]{:S(2)}, u32[]{:S(2)}) collective-permute-start(f32[32,128]{1,0:T(8,128)S(1)} %constant_dynamic-update-slice_fusion), channel_id=1, source_target_pairs={{0,128},{8,136},{16,144},{24,152},{32,160},{40,168},{48,176},{56,1... | collective-permute-start | bytes 49160 | tf_op jit(solution)/shard_map/ppermute | solution.py:186
  45.5 4.7 %collective-permute-start.1 = (f32[4,64,896]{2,1,0:T(8,128)S(1)}, f32[4,64,896]{2,1,0:T(8,128)S(1)}, u32[]{:S(2)}, u32[]{:S(2)}) collective-permute-start(f32[4,64,896]{2,1,0:T(8,128)S(1)} %get-tuple-element.5), channel_id=1, source_target_pairs={{0,1},{1,0},{2,3},{3,2},{4,5},{5,4},{6,7},{7,6},{8,9},{9,8},{10,11... | collective-permute-start | bytes 2752520 | tf_op jit(solution)/shard_map/ppermute | solution.py:193
  50.4 8.8 %collective-permute-start.4 = (f32[64,896]{1,0:T(8,128)S(1)}, f32[64,896]{1,0:T(8,128)S(1)}, u32[]{:S(2)}, u32[]{:S(2)}) collective-permute-start(f32[64,896]{1,0:T(8,128)S(1)} %get-tuple-element.9), channel_id=1, source_target_pairs={{0,6},{1,7},{2,4},{3,5},{4,2},{5,3},{6,0},{7,1},{8,14},{9,15},{10,... | collective-permute-start | bytes 688136 | tf_op jit(solution)/shard_map/ppermute | solution.py:195
  53.3 19.2 %collective-permute-start.3 = (f32[64,896]{1,0:T(8,128)S(1)}, f32[64,896]{1,0:T(8,128)S(1)}, u32[]{:S(2)}, u32[]{:S(2)}) collective-permute-start(f32[64,896]{1,0:T(8,128)S(1)} %get-tuple-element.10), channel_id=1, source_target_pairs={{0,4},{1,5},{2,6},{3,7},{4,0},{5,1},{6,2},{7,3},{8,12},{9,13},{10,... | collective-permute-start | bytes 688136 | tf_op jit(solution)/shard_map/ppermute | solution.py:195
  53.3 19.2 %collective-permute-start.2 = (f32[64,896]{1,0:T(8,128)S(1)}, f32[64,896]{1,0:T(8,128)S(1)}, u32[]{:S(2)}, u32[]{:S(2)}) collective-permute-start(f32[64,896]{1,0:T(8,128)S(1)} %get-tuple-element.8), channel_id=1, source_target_pairs={{0,2},{1,3},{2,0},{3,1},{4,6},{5,7},{6,4},{7,5},{8,10},{9,11},{10,... | collective-permute-start | bytes 688136 | tf_op jit(solution)/shard_map/ppermute | solution.py:195
  72.5 66.5 %copy-start = (f32[64,896]{1,0:T(8,128)}, f32[64,896]{1,0:T(8,128)S(1)}, u32[]{:S(2)}) copy-start(f32[64,896]{1,0:T(8,128)S(1)} %fusion.2.refs_0_) | copy-start | bytes 688132
  72.5 10.4 %collective-permute-start.5 = (f32[64,896]{1,0:T(8,128)S(1)}, f32[64,896]{1,0:T(8,128)S(1)}, u32[]{:S(2)}, u32[]{:S(2)}) collective-permute-start(f32[64,896]{1,0:T(8,128)S(1)} %fusion.2.refs_0_), channel_id=1, source_target_pairs={{0,2},{1,3},{2,0},{3,1},{4,6},{5,7},{6,4},{7,5},{8,10},{9,11},{10,... | collective-permute-start | bytes 688136 | tf_op jit(solution)/shard_map/ppermute | solution.py:201
  72.6 11.8 %collective-permute-start.6 = (f32[64,896]{1,0:T(8,128)S(1)}, f32[64,896]{1,0:T(8,128)S(1)}, u32[]{:S(2)}, u32[]{:S(2)}) collective-permute-start(f32[64,896]{1,0:T(8,128)S(1)} %fusion.2.refs_0_), channel_id=1, source_target_pairs={{0,4},{1,5},{2,6},{3,7},{4,0},{5,1},{6,2},{7,3},{8,12},{9,13},{10,... | collective-permute-start | bytes 688136 | tf_op jit(solution)/shard_map/ppermute | solution.py:201
  74.8 18.4 %collective-permute-start.7 = (f32[64,896]{1,0:T(8,128)S(1)}, f32[64,896]{1,0:T(8,128)S(1)}, u32[]{:S(2)}, u32[]{:S(2)}) collective-permute-start(f32[64,896]{1,0:T(8,128)S(1)} %fusion.2.refs_0_), channel_id=1, source_target_pairs={{0,6},{1,7},{2,4},{3,5},{4,2},{5,3},{6,0},{7,1},{8,14},{9,15},{10,... | collective-permute-start | bytes 688136 | tf_op jit(solution)/shard_map/ppermute | solution.py:201
  76.2 17.0 %collective-permute-start.8 = (f32[64,896]{1,0:T(8,128)S(1)}, f32[64,896]{1,0:T(8,128)S(1)}, u32[]{:S(2)}, u32[]{:S(2)}) collective-permute-start(f32[64,896]{1,0:T(8,128)S(1)} %fusion.2.refs_0_), channel_id=1, source_target_pairs={{0,1},{1,0},{2,3},{3,2},{4,5},{5,4},{6,7},{7,6},{8,9},{9,8},{10,11... | collective-permute-start | bytes 688136 | tf_op jit(solution)/shard_map/ppermute | solution.py:202
  83.0 10.2 %collective-permute-start.9 = (f32[64,896]{1,0:T(8,128)S(1)}, f32[64,896]{1,0:T(8,128)S(1)}, u32[]{:S(2)}, u32[]{:S(2)}) collective-permute-start(f32[64,896]{1,0:T(8,128)S(1)} %collective-permute-done.5.refs_1_), channel_id=1, source_target_pairs={{0,1},{1,0},{2,3},{3,2},{4,5},{5,4},{6,7},{7,6},{8,9},{9,8},{10,11... | collective-permute-start | bytes 688136 | tf_op jit(solution)/shard_map/ppermute | solution.py:202
  84.5 9.8 %collective-permute-start.10 = (f32[64,896]{1,0:T(8,128)S(1)}, f32[64,896]{1,0:T(8,128)S(1)}, u32[]{:S(2)}, u32[]{:S(2)}) collective-permute-start(f32[64,896]{1,0:T(8,128)S(1)} %collective-permute-done.6.refs_2_), channel_id=1, source_target_pairs={{0,1},{1,0},{2,3},{3,2},{4,5},{5,4},{6,7},{7,6},{8,9},{9,8},{10,11... | collective-permute-start | bytes 688136 | tf_op jit(solution)/shard_map/ppermute | solution.py:202
  93.2 1.5 %collective-permute-start.11 = (f32[64,896]{1,0:T(8,128)S(1)}, f32[64,896]{1,0:T(8,128)S(1)}, u32[]{:S(2)}, u32[]{:S(2)}) collective-permute-start(f32[64,896]{1,0:T(8,128)S(1)} %collective-permute-done.7.refs_3_), channel_id=1, source_target_pairs={{0,1},{1,0},{2,3},{3,2},{4,5},{5,4},{6,7},{7,6},{8,9},{9,8},{10,11... | collective-permute-start | bytes 688136 | tf_op jit(solution)/shard_map/ppermute | solution.py:202

commit v2 on v1

v2 whole, which is shorter than its diff:
```python
import jax
import jax.numpy as jnp
from jax import lax
from jax.experimental import pallas as pl
from jax.experimental.pallas import tpu as pltpu
from jax.sharding import PartitionSpec as P

TARGETS = 8
PARTS = 1
LO = 128
NT = (((1,), (1,)), ((), ()))
VALUE_SCALE = 256.0
TOP = 32000.0
STEPS = 64.0
VMEM_SPEC = pl.BlockSpec(memory_space=pltpu.VMEM)
ANY_SPEC = pl.BlockSpec(memory_space=pl.ANY)
PARAMS = pltpu.CompilerParams(vmem_limit_bytes=40 << 20)


def tgt_shift(zh):
    return [(t, t ^ (zh << 4)) for t in range(32)]


def lat_xor(d):
    return [(i, i ^ d) for i in range(8)]


def start_weights(w_hbm, w_ref, sem, steps):
    rows = w_hbm.shape[0] // steps
    copies = []
    for i in range(steps):
        part = pl.ds(i * rows, rows)
        copies.append(pltpu.make_async_copy(w_hbm.at[part], w_ref.at[part], sem.at[i]))
        copies[-1].start()
    return copies


def encode(x):
    cols = x.shape[1] // 128
    parts = [x[:, c * 128 : (c + 1) * 128] for c in range(cols)]
    top = jnp.abs(parts[0])
    for p in parts[1:]:
        top = jnp.maximum(top, jnp.abs(p))
    level = jnp.ceil(jnp.log2(jnp.maximum(top, 1e-30)) * STEPS)
    inverse = jnp.exp2(level * (-1.0 / STEPS)) * TOP
    codes = [jnp.round(p * inverse).astype(jnp.int32).astype(jnp.int16) for p in parts]
    return jnp.concatenate(codes + [level.astype(jnp.int32).astype(jnp.int16)], axis=1)


def decoded(q):
    cols = q.shape[1] // 128 - 1
    wide = q.astype(jnp.int32).astype(jnp.float32)
    scale = jnp.exp2(wide[:, cols * 128 :] * (1.0 / STEPS)) * (1.0 / TOP)
    return jnp.concatenate([wide[:, c * 128 : (c + 1) * 128] * scale for c in range(cols)], axis=1)


def decode_kernel(part, x_ref, w_hbm, mine_ref, theirs_ref, codes_ref, w_ref, acc_ref, sem):
    chunks, tokens = codes_ref.shape[:2]
    his = chunks // 2
    width = his * LO
    group = tokens // 8
    blocks = group // 16
    lat = lax.axis_index("lat")
    core = lat % 2
    start = lat * width
    steps = 8
    rows_w = w_hbm.shape[0] // steps
    copies = start_weights(w_hbm, w_ref, sem, steps)

    half_lane = lax.broadcasted_iota(jnp.int32, (1, 128), 1) < 64
    shape = (his * 8 // 16, 16, 128)
    rows = lax.broadcasted_iota(jnp.int32, shape, 0) * 16 + lax.broadcasted_iota(jnp.int32, shape, 1)
    rows = rows.astype(jnp.float32).astype(jnp.bfloat16)
    zero = jnp.zeros((), jnp.bfloat16)
    one = jnp.ones((), jnp.bfloat16)

    def densify(i, carry):
        zy = i // blocks
        xl = i % blocks
        y = zy % 4
        block = x_ref[(y * 4 + part * blocks + xl) * 2 + zy // 4].astype(jnp.int32)
        local = block[0:16] - start
        inside = (local >= 0) & (local < width)
        hi = jnp.where(inside, (local >> 7) * 8, -1024).astype(jnp.float32)
        lo = (local & (LO - 1)).astype(jnp.float32)
        val = block[16:32].astype(jnp.float32) * (1.0 / VALUE_SCALE)
        both = [(a, pltpu.roll(a, 64, 1)) for a in (hi, lo, val)]

        def pair(n, t, source, extra=None):
            first, second = both[n] if source == 0 else both[n][::-1]
            row = jnp.where(half_lane, first[t : t + 1], second[t + 1 : t + 2])
            if extra is not None:
                row = row + extra
            return jnp.broadcast_to(row, (16, 128)).astype(jnp.bfloat16)[None]

        row = pl.multiple_of(i * 16, 16)
        for source in range(2):
            halves = []
            for t0 in (0, 8):
                lhs, rhs = [], []
                for j in range(4):
                    t = t0 + 2 * j
                    slot = jnp.where(half_lane, 2.0 * j, 2.0 * j + 1)
                    key = pair(0, t, source, slot)
                    lhs.append(jnp.where(rows == key, pair(2, t, source), zero).reshape(his * 8, 128))
                    rhs.append(jnp.where(rows == pair(1, t, source), one, zero).reshape(LO, 128))
                dense = lax.dot_general(
                    jnp.concatenate(lhs, axis=1),
                    jnp.concatenate(rhs, axis=1),
                    NT,
                    preferred_element_type=jnp.float32,
                )
                halves.append(dense.reshape(his, 8, LO))
            dense = jnp.concatenate(halves, axis=1).astype(jnp.bfloat16)
            codes_ref[source * his : (source + 1) * his, pl.ds(row, 16), :] = dense
        return carry

    lax.fori_loop(0, tokens // 16, densify, 0, unroll=8)

    per_step = chunks // steps
    for i in range(steps):
        copies[i].wait()
        lhs = jnp.concatenate([codes_ref[i * per_step + j] for j in range(per_step)], axis=1)
        out = jnp.dot(lhs, w_ref[i * rows_w : (i + 1) * rows_w, :], preferred_element_type=jnp.float32)
        if i == 0:
            acc_ref[...] = out
        else:
            acc_ref[...] += out
    for z in range(4):
        row = pl.multiple_of((z * 2 + core) * group, group)
        mine_ref[z] = acc_ref[pl.ds(row, group), :]
        row = pl.multiple_of((z * 2 + 1 - core) * group, group)
        theirs_ref[z] = acc_ref[pl.ds(row, group), :]


def decode(x, w, part):
    tokens, cols = 512 // PARTS, w.shape[1]
    shape = jax.ShapeDtypeStruct((4, tokens // 8, cols), jnp.float32)
    return pl.pallas_call(
        lambda *refs: decode_kernel(part, *refs),
        out_shape=(shape, shape),
        in_specs=[VMEM_SPEC, ANY_SPEC],
        out_specs=(VMEM_SPEC, VMEM_SPEC),
        scratch_shapes=[
            pltpu.VMEM((w.shape[0] // LO, tokens, LO), jnp.bfloat16),
            pltpu.VMEM(w.shape, jnp.bfloat16),
            pltpu.VMEM((tokens, cols), jnp.float32),
            pltpu.SemaphoreType.DMA((8,)),
        ],
        compiler_params=PARAMS,
        cost_estimate=pl.CostEstimate(
            flops=4 * tokens * w.shape[0] * cols, transcendentals=0, bytes_accessed=2 * w.size
        ),
        name=f"decode{part}",
    )(x, w)


def pack_kernel(mine_ref, recv_ref, own_ref, *near_refs):
    z = lax.axis_index("lat") // 2
    own_ref[...] = mine_ref[z] + recv_ref[z]
    for d in (1, 2, 3):
        near_refs[d - 1][...] = encode(mine_ref[z ^ d] + recv_ref[z ^ d])


def pack(mine, recv, part):
    _, rows, cols = mine.shape
    coded = jax.ShapeDtypeStruct((rows, cols + 128), jnp.int16)
    return pl.pallas_call(
        pack_kernel,
        out_shape=(jax.ShapeDtypeStruct((rows, cols), jnp.float32), coded, coded, coded),
        in_specs=[VMEM_SPEC] * 2,
        out_specs=(VMEM_SPEC,) * 4,
        compiler_params=PARAMS,
        name=f"pack{part}",
    )(mine, recv)


def error_kernel(part, own_ref, a_ref, b_ref, c_ref, mlp_ref, error_ref, code_ref):
    rows = own_ref.shape[0]
    total = own_ref[...] + decoded(a_ref[...]) + decoded(b_ref[...]) + decoded(c_ref[...])
    error = total - mlp_ref[part * rows : (part + 1) * rows, :].astype(jnp.float32)
    error_ref[...] = error
    code_ref[...] = encode(error)


def error_of(own, near, mlp, part):
    rows, cols = own.shape
    return pl.pallas_call(
        lambda *refs: error_kernel(part, *refs),
        out_shape=(
            jax.ShapeDtypeStruct((rows, cols), jnp.float32),
            jax.ShapeDtypeStruct((rows, cols + 128), jnp.int16),
        ),
        in_specs=[VMEM_SPEC] * 5,
        out_specs=(VMEM_SPEC,) * 2,
        compiler_params=PARAMS,
        name=f"error{part}",
    )(own, *near, mlp)


def grads_kernel(part, x_ref, *refs):
    coded = refs[:8]
    w_hbm, out_ref, err_ref, w_ref, sem = refs[8:]
    steps = 8
    rows_w = w_hbm.shape[0] // steps
    copies = start_weights(w_hbm, w_ref, sem, steps)
    tokens = out_ref.shape[0]
    group = tokens // 8
    blocks = group // 16
    lat = lax.axis_index("lat")
    core = lat % 2
    z = lat // 2
    for n, ref in enumerate(coded):
        d, side = n % 4, n // 4
        c = core if side == 0 else 1 - core
        row = pl.multiple_of(((z ^ d) * 2 + c) * group, group)
        e = decoded(ref[...])
        high = e.astype(jnp.bfloat16)
        err_ref[pl.ds(row, group), :] = high
        err_ref[pl.ds(pl.multiple_of(tokens + row, group), group), :] = (e - high.astype(jnp.float32)).astype(
            jnp.bfloat16
        )
    chunks = w_hbm.shape[0] // LO
    his = chunks // 2
    width = his * LO
    source = lax.broadcasted_iota(jnp.int32, (16, 128), 1) // 64
    keys, los = [], []
    for i in range(tokens // 16):
        zy = i // blocks
        b = ((zy % 4) * 4 + part * blocks + i % blocks) * 2 + zy // 4
        local = x_ref[b, 0:16, :].astype(jnp.int32) - lat * width
        inside = (local >= 0) & (local < width)
        keys.append(jnp.where(inside, (local >> 7) + source * his, -1))
        los.append(local & (LO - 1))
    key = jnp.concatenate(keys, axis=0)
    lo = jnp.concatenate(los, axis=0)
    picked = jnp.zeros(out_ref.shape, jnp.float32)
    for i in range(steps):
        copies[i].wait()
        grads = lax.dot_general(
            err_ref[...], w_ref[i * rows_w : (i + 1) * rows_w, :], NT, preferred_element_type=jnp.float32
        )
        grads = grads[:tokens] + grads[tokens:]
        for j in range(rows_w // LO):
            found = jnp.take_along_axis(grads[:, j * LO : (j + 1) * LO], lo, axis=1)
            picked = jnp.where(key == i * (rows_w // LO) + j, found, picked)
    out_ref[...] = picked


def grads(x, coded, w, part):
    tokens, cols = 512 // PARTS, w.shape[1]
    return pl.pallas_call(
        lambda *refs: grads_kernel(part, *refs),
        out_shape=jax.ShapeDtypeStruct((tokens, 128), jnp.float32),
        in_specs=[VMEM_SPEC] * 9 + [ANY_SPEC],
        out_specs=VMEM_SPEC,
        scratch_shapes=[
            pltpu.VMEM((2 * tokens, cols), jnp.bfloat16),
            pltpu.VMEM(w.shape, jnp.bfloat16),
            pltpu.SemaphoreType.DMA((8,)),
        ],
        compiler_params=PARAMS,
        cost_estimate=pl.CostEstimate(
            flops=4 * tokens * w.shape[0] * cols, transcendentals=0, bytes_accessed=2 * w.size
        ),
        name=f"grads{part}",
    )(x, *coded, w)


def body(code_index, code_value, decoder, mlp_out):
    sources, lat_width, cols = decoder.shape
    w = decoder.reshape(sources * lat_width, cols)
    rows = code_index.shape[1]
    zh = lax.axis_index("tgt") // 16

    value = (code_value.astype(jnp.float32) * VALUE_SCALE).astype(jnp.int32)
    own = jnp.stack([code_index, value]).astype(jnp.int16)
    own = jnp.transpose(own, (0, 2, 1, 3)).reshape(2 * rows, 128)
    other = lax.ppermute(own, "tgt", tgt_shift(1))
    both = jnp.where(zh == 0, jnp.stack([own, other]), jnp.stack([other, own]))
    groups = [[a * 16 + i for i in range(16)] for a in range(2)]
    sent = jnp.broadcast_to(both[None], (16,) + both.shape).reshape(32, 2 * rows, 128)
    x = lax.all_to_all(sent, "tgt", 0, 0, tiled=True, axis_index_groups=groups)

    errors, picks = [], []
    for part in range(PARTS):
        mine, theirs = decode(x, w, part)
        recv = lax.ppermute(theirs, "lat", lat_xor(1))
        own_sum, *near = pack(mine, recv, part)
        near = [lax.ppermute(near[d - 1], "lat", lat_xor(2 * d)) for d in (1, 2, 3)]
        error, coded = error_of(own_sum, near, mlp_out, part)
        errors.append(error)
        coded = [coded] + [lax.ppermute(coded, "lat", lat_xor(2 * d)) for d in (1, 2, 3)]
        coded = coded + [lax.ppermute(c, "lat", lat_xor(1)) for c in coded]
        picks.append(grads(x, coded, w, part).reshape(8, 64 // PARTS, 128))
    error = jnp.concatenate(errors, axis=0)
    picked = jnp.concatenate(picks, axis=1).reshape(512, 128)
    parts = lax.all_to_all(picked, ("tgt", "lat"), 0, 0, tiled=True)
    total = jnp.sum(parts.reshape(256, 2, sources, 64), axis=0)
    return (error, jnp.transpose(total, (1, 0, 2)) / TARGETS)


def solution(mesh):
    placed = (P(None, "tgt", None), P(None, "tgt", None), P(None, "lat", "tgt"), P("lat", "tgt"))
    return jax.shard_map(
        body,
        mesh=mesh,
        in_specs=placed,
        out_specs=(P("lat", "tgt"), P(None, ("tgt", "lat"), None)),
        check_vma=False,
    )
```

time: 140 us -> 117 us (0.84)
  waiting for transfers between devices: 27.9 us -> 17.6 us
  Pallas kernels: 35.1 us -> 29.4 us
  blocking collectives: 42.6 us -> 37.5 us
  starting transfers between devices: 29.9 us -> 25.9 us
  local copies, waits for them, and re-layouts: 0.98 us -> 4.01 us
    ppermute x11, waiting for transfers between devices: 26.8 us -> 16.7 us  [the longest x3 8.61 us: body(): near = [lax.ppermute(near[d - 1], 'lat', lat_xor(2 * d)) for d in (1, 2, 3)]]
    pallas_call x2 -> x4, Pallas kernels: 35.1 us -> 29.4 us  [the longest x1 16 us: grads(): pl.pallas_call(lambda *refs: grads_kernel(part, *refs), out_shape=jax.Sha...]
    ppermute x11, starting transfers between devices: 22.1 us -> 18.1 us  [the longest x4 7.06 us: body(): coded = coded + [lax.ppermute(c, 'lat', lat_xor(1)) for c in coded]]
    unnamed x6 -> x7, local copies, waits for them, and re-layouts: 0.6 us -> 3.7 us
    all_to_all x1, blocking collectives: 26.1 us -> 23.3 us  [body(): parts = lax.all_to_all(picked, ('tgt', 'lat'), 0, 0, tiled=True)]
    all_to_all x1, blocking collectives: 16.6 us -> 14.2 us  [body(): x = lax.all_to_all(sent, 'tgt', 0, 0, tiled=True, axis_index_groups=groups)]
    convert_element_type x2 -> x0, other arithmetic: 1.45 us -> none  [the longest x1 0.76 us: body(): jnp.transpose(code_index, (1, 0, 2)).reshape(rows, 128).astype(jnp.float32)]
    another operation x0 -> x2, other arithmetic: none -> 1.42 us  [body(): own = jnp.stack([code_index, value]).astype(jnp.int16)]
  transfers between devices with their start and end apart: 12 -> 12, of which waited for: 7 -> 8; matrix products, arithmetic and copies ran while one was open for 0% -> 0% of each run, Pallas kernels for 0% -> 0%
where the time goes in v2:
time: 117 us
  blocking collectives  37.5 us (32%)
  Pallas kernels  29.4 us (25%)
  starting transfers between devices  25.9 us (22%)
  waiting for transfers between devices  17.6 us (15%)
  local copies, waits for them, and re-layouts  4.01 us (3%)
  other arithmetic  1.73 us (1%)
    all_to_all x1, blocking collectives, body(): parts = lax.all_to_all(picked, ('tgt', 'lat'), 0, 0, tiled=True)  23.3 us
    pallas_call x1, Pallas kernels, grads(): pl.pallas_call(lambda *refs: grads_kernel(part, *refs), out_shape=jax.Sha...  16 us
    all_to_all x1, blocking collectives, body(): x = lax.all_to_all(sent, 'tgt', 0, 0, tiled=True, axis_index_groups=groups)  14.2 us
    pallas_call x1, Pallas kernels, decode(): pl.pallas_call(lambda *refs: decode_kernel(part, *refs), out_shape=(shape...  12.3 us
    ppermute x3, waiting for transfers between devices, body(): near = [lax.ppermute(near[d - 1], 'lat', lat_xor(2 * d)) for d in (1, 2, 3)]  8.61 us
    ppermute x1, starting transfers between devices, body(): other = lax.ppermute(own, 'tgt', tgt_shift(1))  7.76 us
    ppermute x4, starting transfers between devices, body(): coded = coded + [lax.ppermute(c, 'lat', lat_xor(1)) for c in coded]  7.06 us
    ppermute x3, waiting for transfers between devices, body(): lax.ppermute(coded, 'lat', lat_xor(2 * d))  4.61 us
  transfers between devices with their start and end apart: 12, of which 8 were waited for; matrix products, arithmetic and copies ran while one was open for 0% of the time, Pallas kernels for 0%

profile of v2, /device:TPU:1, one launch (start us, length us, event | category | flops | bytes accessed | tf_op | source)
XLA Modules:
  0.0 116.8 jit_solution(8263410238691954645)
XLA Ops:
  0.6 0.7 convert_bitcast_fusion
  1.4 0.7 fusion
  2.1 0.1 reshape.53
  2.2 7.8 %collective-permute-start = (s16[32,128]{1,0:T(8,128)(2,1)S(1)}, s16[32,128]{1,0:T(8,128)(2,1)S(1)}, u32[]{:S(2)}, u32[]{:S(2)}) collective-permute-start(s16[32,128]{1,0:T(8,128)(2,1)S(1)} %reshape.53), channel_id=1, source_target_pairs={{0,128},{8,136},{16,144},{24,152},{32,160},{40,168},{48,176},{56,1... | collective-permute-start | bytes 24584 | tf_op jit(solution)/shard_map/ppermute | solution.py:279
  9.9 0.1 stack.27
  10.0 1.0 collective-permute-done
  11.0 14.2 %all_to_all.14.refs_0_ = s16[32,32,128]{2,1,0:T(8,128)(2,1)S(1)} all-to-all(s16[32,32,128]{2,1,0:T(8,128)(2,1)S(1)} %bitcast.14), channel_id=1, replica_groups={{0,8,16,24,32,40,48,56,64,72,80,88,96,104,112,120},{128,136,144,152,160..., dimensions={0} | all-to-all | bytes 524288 | tf_op jit(solution)/shard_map/all_to_all | solution.py:283
  25.2 0.0 copy-start.1
  25.2 3.1 %copy-done.1 = bf16[2,2048,896]{2,1,0:T(8,128)(2,1)S(1)} copy-done((bf16[2,2048,896]{2,1,0:T(8,128)(2,1)S(1)}, bf16[2,2048,896]{2,1,0:T(8,128)(2,1)}, u32[]{:S(2)}) %copy-start.1) | copy-done | bytes 7340056
  28.3 0.0 copy-start
  28.3 0.0 copy-start.2
  28.3 12.3 %decode0.1 = (f32[4,64,896]{2,1,0:T(8,128)S(1)}, f32[4,64,896]{2,1,0:T(8,128)S(1)}) custom-call(s16[32,32,128]{2,1,0:T(8,128)(2,1)S(1)} %all_to_all.14.refs_0_, bf16[4096,896]{1,0:T(8,128)(2,1)S(1)} %bitcast.12), custom_call_target="tpu_custom_call" | custom-call | flops 7516192768 | bytes 7340032 | tf_op jit(solution)/shard_map/decode0/pallas_call | solution.py:139
  40.6 3.0 %collective-permute-start.1 = (f32[4,64,896]{2,1,0:T(8,128)S(1)}, f32[4,64,896]{2,1,0:T(8,128)S(1)}, u32[]{:S(2)}, u32[]{:S(2)}) collective-permute-start(f32[4,64,896]{2,1,0:T(8,128)S(1)} %get-tuple-element.11), channel_id=1, source_target_pairs={{0,1},{1,0},{2,3},{3,2},{4,5},{5,4},{6,7},{7,6},{8,9},{9,8},{10,11... | collective-permute-start | bytes 2752520 | tf_op jit(solution)/shard_map/ppermute | solution.py:288
  43.6 2.1 %collective-permute-done.1.recv_ref = f32[4,64,896]{2,1,0:T(8,128)S(1)} collective-permute-done((f32[4,64,896]{2,1,0:T(8,128)S(1)}, f32[4,64,896]{2,1,0:T(8,128)S(1)}, u32[]{:S(2)}, u32[]{:S(2)}) %collective-permute-start.1) | collective-permute-done | bytes 917536 | tf_op jit(solution)/shard_map/ppermute | solution.py:288
  45.7 0.2 pack0.1
  45.9 0.8 collective-permute-start.2
  46.7 2.6 %collective-permute-start.3 = (s16[64,1024]{1,0:T(8,128)(2,1)S(1)}, s16[64,1024]{1,0:T(8,128)(2,1)S(1)}, u32[]{:S(2)}, u32[]{:S(2)}) collective-permute-start(s16[64,1024]{1,0:T(8,128)(2,1)S(1)} %get-tuple-element.14), channel_id=1, source_target_pairs={{0,4},{1,5},{2,6},{3,7},{4,0},{5,1},{6,2},{7,3},{8,12},{9,13},{10,... | collective-permute-start | bytes 393224 | tf_op jit(solution)/shard_map/ppermute | solution.py:290
  49.3 0.2 collective-permute-start.4
  49.5 1.1 collective-permute-done.2.refs_1_
  50.7 2.1 %collective-permute-done.3.refs_2_ = s16[64,1024]{1,0:T(8,128)(2,1)S(1)} collective-permute-done((s16[64,1024]{1,0:T(8,128)(2,1)S(1)}, s16[64,1024]{1,0:T(8,128)(2,1)S(1)}, u32[]{:S(2)}, u32[]{:S(2)}) %collective-permute-start.3) | collective-permute-done | bytes 131104 | tf_op jit(solution)/shard_map/ppermute | solution.py:290
  52.7 5.4 %collective-permute-done.4.refs_3_ = s16[64,1024]{1,0:T(8,128)(2,1)S(1)} collective-permute-done((s16[64,1024]{1,0:T(8,128)(2,1)S(1)}, s16[64,1024]{1,0:T(8,128)(2,1)S(1)}, u32[]{:S(2)}, u32[]{:S(2)}) %collective-permute-start.4) | collective-permute-done | bytes 131104 | tf_op jit(solution)/shard_map/ppermute | solution.py:290
  58.1 0.0 copy-done
  58.1 0.9 error0.1
  59.0 2.3 %collective-permute-start.7 = (s16[64,1024]{1,0:T(8,128)(2,1)S(1)}, s16[64,1024]{1,0:T(8,128)(2,1)S(1)}, u32[]{:S(2)}, u32[]{:S(2)}) collective-permute-start(s16[64,1024]{1,0:T(8,128)(2,1)S(1)} %get-tuple-element.17.refs_1_), channel_id=1, source_target_pairs={{0,6},{1,7},{2,4},{3,5},{4,2},{5,3},{6,0},{7,1},{8,14},{9,15},{10,... | collective-permute-start | bytes 393224 | tf_op jit(solution)/shard_map/ppermute | solution.py:293
  61.3 2.1 %collective-permute-start.6 = (s16[64,1024]{1,0:T(8,128)(2,1)S(1)}, s16[64,1024]{1,0:T(8,128)(2,1)S(1)}, u32[]{:S(2)}, u32[]{:S(2)}) collective-permute-start(s16[64,1024]{1,0:T(8,128)(2,1)S(1)} %get-tuple-element.17.refs_1_), channel_id=1, source_target_pairs={{0,4},{1,5},{2,6},{3,7},{4,0},{5,1},{6,2},{7,3},{8,12},{9,13},{10,... | collective-permute-start | bytes 393224 | tf_op jit(solution)/shard_map/ppermute | solution.py:293
  63.4 0.1 collective-permute-start.5
  63.5 2.1 %collective-permute-start.8 = (s16[64,1024]{1,0:T(8,128)(2,1)S(1)}, s16[64,1024]{1,0:T(8,128)(2,1)S(1)}, u32[]{:S(2)}, u32[]{:S(2)}) collective-permute-start(s16[64,1024]{1,0:T(8,128)(2,1)S(1)} %get-tuple-element.17.refs_1_), channel_id=1, source_target_pairs={{0,1},{1,0},{2,3},{3,2},{4,5},{5,4},{6,7},{7,6},{8,9},{9,8},{10,11... | collective-permute-start | bytes 393224 | tf_op jit(solution)/shard_map/ppermute | solution.py:294
  65.6 0.0 collective-permute-done.7.refs_4_
  65.6 3.2 %collective-permute-start.11 = (s16[64,1024]{1,0:T(8,128)(2,1)S(1)}, s16[64,1024]{1,0:T(8,128)(2,1)S(1)}, u32[]{:S(2)}, u32[]{:S(2)}) collective-permute-start(s16[64,1024]{1,0:T(8,128)(2,1)S(1)} %collective-permute-done.7.refs_4_), channel_id=1, source_target_pairs={{0,1},{1,0},{2,3},{3,2},{4,5},{5,4},{6,7},{7,6},{8,9},{9,8},{10,11... | collective-permute-start | bytes 393224 | tf_op jit(solution)/shard_map/ppermute | solution.py:294
  68.8 4.6 %collective-permute-done.6.refs_3_ = s16[64,1024]{1,0:T(8,128)(2,1)S(1)} collective-permute-done((s16[64,1024]{1,0:T(8,128)(2,1)S(1)}, s16[64,1024]{1,0:T(8,128)(2,1)S(1)}, u32[]{:S(2)}, u32[]{:S(2)}) %collective-permute-start.6) | collective-permute-done | bytes 131104 | tf_op jit(solution)/shard_map/ppermute | solution.py:293
  73.4 1.7 %collective-permute-start.10 = (s16[64,1024]{1,0:T(8,128)(2,1)S(1)}, s16[64,1024]{1,0:T(8,128)(2,1)S(1)}, u32[]{:S(2)}, u32[]{:S(2)}) collective-permute-start(s16[64,1024]{1,0:T(8,128)(2,1)S(1)} %collective-permute-done.6.refs_3_), channel_id=1, source_target_pairs={{0,1},{1,0},{2,3},{3,2},{4,5},{5,4},{6,7},{7,6},{8,9},{9,8},{10,11... | collective-permute-start | bytes 393224 | tf_op jit(solution)/shard_map/ppermute | solution.py:294
  75.1 0.0 collective-permute-done.5.refs_2_
  75.1 0.0 collective-permute-start.9
  75.1 0.0 collective-permute-done.8.refs_5_
  75.2 0.0 collective-permute-done.11.refs_8_
  75.2 1.0 collective-permute-done.10.refs_7_
  76.1 0.4 collective-permute-done.9.refs_6_
  76.5 0.0 copy-done.2
  76.5 16.0 %grads0.1 = f32[512,128]{1,0:T(8,128)S(1)} custom-call(s16[32,32,128]{2,1,0:T(8,128)(2,1)S(1)} %all_to_all.14.refs_0_, s16[64,1024]{1,0:T(8,128)(2,1)S(1)} %get-tuple-element.17.refs_1_, s16[64,1024]{1,0:T(8,128)(2,1)S(1)} %collective-permute-done.5.refs_2_, s16[64,1024]{1,0:T(8,128)(2,1)S(1)} %collective-permute-done.6.refs_3_, ...), custom_call_target="tpu_custom_call" | custom-call | flops 7516192768 | bytes 7340032 | tf_op jit(solution)/shard_map/grads0/pallas_call | solution.py:252
  92.5 23.3 %all_to_all.15 = f32[256,2,128]{2,1,0:T(2,128)S(1)} all-to-all(f32[256,2,128]{2,1,0:T(2,128)S(1)} %bitcast.11), channel_id=1, replica_groups=mesh['tgt'=32,'lat'=8] {'tgt','lat'}, dimensions={0} | all-to-all | bytes 524288 | tf_op jit(solution)/shard_map/all_to_all | solution.py:298
  115.9 0.3 reduce_sum.9
  116.2 0.1 div.23
  116.2 0.6 copy.8
  (5 shorter events, 0.1 us)
Async XLA Ops:
  2.2 8.8 %collective-permute-start = (s16[32,128]{1,0:T(8,128)(2,1)S(1)}, s16[32,128]{1,0:T(8,128)(2,1)S(1)}, u32[]{:S(2)}, u32[]{:S(2)}) collective-permute-start(s16[32,128]{1,0:T(8,128)(2,1)S(1)} %reshape.53), channel_id=1, source_target_pairs={{0,128},{8,136},{16,144},{24,152},{32,160},{40,168},{48,176},{56,1... | collective-permute-start | bytes 24584 | tf_op jit(solution)/shard_map/ppermute | solution.py:279
  25.2 3.1 %copy-start.1 = (bf16[2,2048,896]{2,1,0:T(8,128)(2,1)S(1)}, bf16[2,2048,896]{2,1,0:T(8,128)(2,1)}, u32[]{:S(2)}) copy-start(bf16[2,2048,896]{2,1,0:T(8,128)(2,1)} %param.6) | copy-start | bytes 22020100
  28.3 29.8 %copy-start = (bf16[64,896]{1,0:T(8,128)(2,1)S(1)}, bf16[64,896]{1,0:T(8,128)(2,1)}, u32[]{:S(2)}) copy-start(bf16[64,896]{1,0:T(8,128)(2,1)} %refs_4_.1) | copy-start | bytes 344068
  28.3 48.2 %copy-start.2 = (bf16[2,2048,896]{2,1,0:T(8,128)(2,1)S(1)}, bf16[2,2048,896]{2,1,0:T(8,128)(2,1)}, u32[]{:S(2)}) copy-start(bf16[2,2048,896]{2,1,0:T(8,128)(2,1)} %param.6) | copy-start | bytes 22020100
  40.6 5.1 %collective-permute-start.1 = (f32[4,64,896]{2,1,0:T(8,128)S(1)}, f32[4,64,896]{2,1,0:T(8,128)S(1)}, u32[]{:S(2)}, u32[]{:S(2)}) collective-permute-start(f32[4,64,896]{2,1,0:T(8,128)S(1)} %get-tuple-element.11), channel_id=1, source_target_pairs={{0,1},{1,0},{2,3},{3,2},{4,5},{5,4},{6,7},{7,6},{8,9},{9,8},{10,11... | collective-permute-start | bytes 2752520 | tf_op jit(solution)/shard_map/ppermute | solution.py:288
  45.9 4.8 %collective-permute-start.2 = (s16[64,1024]{1,0:T(8,128)(2,1)S(1)}, s16[64,1024]{1,0:T(8,128)(2,1)S(1)}, u32[]{:S(2)}, u32[]{:S(2)}) collective-permute-start(s16[64,1024]{1,0:T(8,128)(2,1)S(1)} %get-tuple-element.13), channel_id=1, source_target_pairs={{0,2},{1,3},{2,0},{3,1},{4,6},{5,7},{6,4},{7,5},{8,10},{9,11},{10,... | collective-permute-start | bytes 393224 | tf_op jit(solution)/shard_map/ppermute | solution.py:290
  46.7 6.0 %collective-permute-start.3 = (s16[64,1024]{1,0:T(8,128)(2,1)S(1)}, s16[64,1024]{1,0:T(8,128)(2,1)S(1)}, u32[]{:S(2)}, u32[]{:S(2)}) collective-permute-start(s16[64,1024]{1,0:T(8,128)(2,1)S(1)} %get-tuple-element.14), channel_id=1, source_target_pairs={{0,4},{1,5},{2,6},{3,7},{4,0},{5,1},{6,2},{7,3},{8,12},{9,13},{10,... | collective-permute-start | bytes 393224 | tf_op jit(solution)/shard_map/ppermute | solution.py:290
  49.3 8.8 %collective-permute-start.4 = (s16[64,1024]{1,0:T(8,128)(2,1)S(1)}, s16[64,1024]{1,0:T(8,128)(2,1)S(1)}, u32[]{:S(2)}, u32[]{:S(2)}) collective-permute-start(s16[64,1024]{1,0:T(8,128)(2,1)S(1)} %get-tuple-element.15), channel_id=1, source_target_pairs={{0,6},{1,7},{2,4},{3,5},{4,2},{5,3},{6,0},{7,1},{8,14},{9,15},{10,... | collective-permute-start | bytes 393224 | tf_op jit(solution)/shard_map/ppermute | solution.py:290
  59.0 6.6 %collective-permute-start.7 = (s16[64,1024]{1,0:T(8,128)(2,1)S(1)}, s16[64,1024]{1,0:T(8,128)(2,1)S(1)}, u32[]{:S(2)}, u32[]{:S(2)}) collective-permute-start(s16[64,1024]{1,0:T(8,128)(2,1)S(1)} %get-tuple-element.17.refs_1_), channel_id=1, source_target_pairs={{0,6},{1,7},{2,4},{3,5},{4,2},{5,3},{6,0},{7,1},{8,14},{9,15},{10,... | collective-permute-start | bytes 393224 | tf_op jit(solution)/shard_map/ppermute | solution.py:293
  61.3 12.1 %collective-permute-start.6 = (s16[64,1024]{1,0:T(8,128)(2,1)S(1)}, s16[64,1024]{1,0:T(8,128)(2,1)S(1)}, u32[]{:S(2)}, u32[]{:S(2)}) collective-permute-start(s16[64,1024]{1,0:T(8,128)(2,1)S(1)} %get-tuple-element.17.refs_1_), channel_id=1, source_target_pairs={{0,4},{1,5},{2,6},{3,7},{4,0},{5,1},{6,2},{7,3},{8,12},{9,13},{10,... | collective-permute-start | bytes 393224 | tf_op jit(solution)/shard_map/ppermute | solution.py:293
  63.4 11.8 %collective-permute-start.5 = (s16[64,1024]{1,0:T(8,128)(2,1)S(1)}, s16[64,1024]{1,0:T(8,128)(2,1)S(1)}, u32[]{:S(2)}, u32[]{:S(2)}) collective-permute-start(s16[64,1024]{1,0:T(8,128)(2,1)S(1)} %get-tuple-element.17.refs_1_), channel_id=1, source_target_pairs={{0,2},{1,3},{2,0},{3,1},{4,6},{5,7},{6,4},{7,5},{8,10},{9,11},{10,... | collective-permute-start | bytes 393224 | tf_op jit(solution)/shard_map/ppermute | solution.py:293
  63.5 11.7 %collective-permute-start.8 = (s16[64,1024]{1,0:T(8,128)(2,1)S(1)}, s16[64,1024]{1,0:T(8,128)(2,1)S(1)}, u32[]{:S(2)}, u32[]{:S(2)}) collective-permute-start(s16[64,1024]{1,0:T(8,128)(2,1)S(1)} %get-tuple-element.17.refs_1_), channel_id=1, source_target_pairs={{0,1},{1,0},{2,3},{3,2},{4,5},{5,4},{6,7},{7,6},{8,9},{9,8},{10,11... | collective-permute-start | bytes 393224 | tf_op jit(solution)/shard_map/ppermute | solution.py:294
  65.6 9.6 %collective-permute-start.11 = (s16[64,1024]{1,0:T(8,128)(2,1)S(1)}, s16[64,1024]{1,0:T(8,128)(2,1)S(1)}, u32[]{:S(2)}, u32[]{:S(2)}) collective-permute-start(s16[64,1024]{1,0:T(8,128)(2,1)S(1)} %collective-permute-done.7.refs_4_), channel_id=1, source_target_pairs={{0,1},{1,0},{2,3},{3,2},{4,5},{5,4},{6,7},{7,6},{8,9},{9,8},{10,11... | collective-permute-start | bytes 393224 | tf_op jit(solution)/shard_map/ppermute | solution.py:294
  73.4 2.7 %collective-permute-start.10 = (s16[64,1024]{1,0:T(8,128)(2,1)S(1)}, s16[64,1024]{1,0:T(8,128)(2,1)S(1)}, u32[]{:S(2)}, u32[]{:S(2)}) collective-permute-start(s16[64,1024]{1,0:T(8,128)(2,1)S(1)} %collective-permute-done.6.refs_3_), channel_id=1, source_target_pairs={{0,1},{1,0},{2,3},{3,2},{4,5},{5,4},{6,7},{7,6},{8,9},{9,8},{10,11... | collective-permute-start | bytes 393224 | tf_op jit(solution)/shard_map/ppermute | solution.py:294
  75.1 1.3 %collective-permute-start.9 = (s16[64,1024]{1,0:T(8,128)(2,1)S(1)}, s16[64,1024]{1,0:T(8,128)(2,1)S(1)}, u32[]{:S(2)}, u32[]{:S(2)}) collective-permute-start(s16[64,1024]{1,0:T(8,128)(2,1)S(1)} %collective-permute-done.5.refs_2_), channel_id=1, source_target_pairs={{0,1},{1,0},{2,3},{3,2},{4,5},{5,4},{6,7},{7,6},{8,9},{9,8},{10,11... | collective-permute-start | bytes 393224 | tf_op jit(solution)/shard_map/ppermute | solution.py:294

commit v3 on v2

--- a/solution.py
+++ b/solution.py
@@ -6,7 +6,7 @@
 from jax.sharding import PartitionSpec as P
 
 TARGETS = 8
-PARTS = 1
+PARTS = 2
 LO = 128
 NT = (((1,), (1,)), ((), ()))
 VALUE_SCALE = 256.0
@@ -14,6 +14,7 @@
 STEPS = 64.0
 VMEM_SPEC = pl.BlockSpec(memory_space=pltpu.VMEM)
 ANY_SPEC = pl.BlockSpec(memory_space=pl.ANY)
+HBM_SPEC = pl.BlockSpec(memory_space=pltpu.HBM)
 PARAMS = pltpu.CompilerParams(vmem_limit_bytes=40 << 20)
 
 
@@ -133,13 +134,13 @@
         theirs_ref[z] = acc_ref[pl.ds(row, group), :]
 
 
-def decode(x, w, part):
+def decode(x, w, part, after):
     tokens, cols = 512 // PARTS, w.shape[1]
     shape = jax.ShapeDtypeStruct((4, tokens // 8, cols), jnp.float32)
     return pl.pallas_call(
-        lambda *refs: decode_kernel(part, *refs),
+        lambda x_ref, w_ref, *refs: decode_kernel(part, x_ref, w_ref, *refs[len(after) :]),
         out_shape=(shape, shape),
-        in_specs=[VMEM_SPEC, ANY_SPEC],
+        in_specs=[VMEM_SPEC, HBM_SPEC] + [ANY_SPEC] * len(after),
         out_specs=(VMEM_SPEC, VMEM_SPEC),
         scratch_shapes=[
             pltpu.VMEM((w.shape[0] // LO, tokens, LO), jnp.bfloat16),
@@ -151,8 +152,7 @@
         cost_estimate=pl.CostEstimate(
             flops=4 * tokens * w.shape[0] * cols, transcendentals=0, bytes_accessed=2 * w.size
         ),
-        name=f"decode{part}",
-    )(x, w)
+    )(x, w, *after)
 
 
 def pack_kernel(mine_ref, recv_ref, own_ref, *near_refs):
@@ -162,7 +162,7 @@
         near_refs[d - 1][...] = encode(mine_ref[z ^ d] + recv_ref[z ^ d])
 
 
-def pack(mine, recv, part):
+def pack(mine, recv):
     _, rows, cols = mine.shape
     coded = jax.ShapeDtypeStruct((rows, cols + 128), jnp.int16)
     return pl.pallas_call(
@@ -171,7 +171,6 @@
         in_specs=[VMEM_SPEC] * 2,
         out_specs=(VMEM_SPEC,) * 4,
         compiler_params=PARAMS,
-        name=f"pack{part}",
     )(mine, recv)
 
 
@@ -194,16 +193,15 @@
         in_specs=[VMEM_SPEC] * 5,
         out_specs=(VMEM_SPEC,) * 2,
         compiler_params=PARAMS,
-        name=f"error{part}",
     )(own, *near, mlp)
 
 
 def grads_kernel(part, x_ref, *refs):
     coded = refs[:8]
-    w_hbm, out_ref, err_ref, w_ref, sem = refs[8:]
-    steps = 8
-    rows_w = w_hbm.shape[0] // steps
-    copies = start_weights(w_hbm, w_ref, sem, steps)
+    w_ref, out_ref, err_ref = refs[8:]
+    steps = 4
+    rows_w = w_ref.shape[0] // steps
+    cols = w_ref.shape[1]
     tokens = out_ref.shape[0]
     group = tokens // 8
     blocks = group // 16
@@ -216,11 +214,9 @@
         row = pl.multiple_of(((z ^ d) * 2 + c) * group, group)
         e = decoded(ref[...])
         high = e.astype(jnp.bfloat16)
-        err_ref[pl.ds(row, group), :] = high
-        err_ref[pl.ds(pl.multiple_of(tokens + row, group), group), :] = (e - high.astype(jnp.float32)).astype(
-            jnp.bfloat16
-        )
-    chunks = w_hbm.shape[0] // LO
+        err_ref[pl.ds(row, group), :cols] = high
+        err_ref[pl.ds(row, group), cols:] = (e - high.astype(jnp.float32)).astype(jnp.bfloat16)
+    chunks = w_ref.shape[0] // LO
     his = chunks // 2
     width = his * LO
     source = lax.broadcasted_iota(jnp.int32, (16, 128), 1) // 64
@@ -236,38 +232,36 @@
     lo = jnp.concatenate(los, axis=0)
     picked = jnp.zeros(out_ref.shape, jnp.float32)
     for i in range(steps):
-        copies[i].wait()
+        w = w_ref[i * rows_w : (i + 1) * rows_w, :]
         grads = lax.dot_general(
-            err_ref[...], w_ref[i * rows_w : (i + 1) * rows_w, :], NT, preferred_element_type=jnp.float32
+            err_ref[...], jnp.concatenate([w, w], axis=1), NT, preferred_element_type=jnp.float32
         )
-        grads = grads[:tokens] + grads[tokens:]
         for j in range(rows_w // LO):
             found = jnp.take_along_axis(grads[:, j * LO : (j + 1) * LO], lo, axis=1)
             picked = jnp.where(key == i * (rows_w // LO) + j, found, picked)
     out_ref[...] = picked
 
 
-def grads(x, coded, w, part):
+def grads(x, coded, w, part, after):
     tokens, cols = 512 // PARTS, w.shape[1]
     return pl.pallas_call(
-        lambda *refs: grads_kernel(part, *refs),
+        lambda *refs: grads_kernel(part, *refs[:10], *refs[10 + len(after) :]),
         out_shape=jax.ShapeDtypeStruct((tokens, 128), jnp.float32),
-        in_specs=[VMEM_SPEC] * 9 + [ANY_SPEC],
+        in_specs=[VMEM_SPEC] * 10 + [ANY_SPEC] * len(after),
         out_specs=VMEM_SPEC,
-        scratch_shapes=[
-            pltpu.VMEM((2 * tokens, cols), jnp.bfloat16),
-            pltpu.VMEM(w.shape, jnp.bfloat16),
-            pltpu.SemaphoreType.DMA((8,)),
-        ],
+        scratch_shapes=[pltpu.VMEM((tokens, 2 * cols), jnp.bfloat16)],
         compiler_params=PARAMS,
         cost_estimate=pl.CostEstimate(
             flops=4 * tokens * w.shape[0] * cols, transcendentals=0, bytes_accessed=2 * w.size
         ),
-        name=f"grads{part}",
-    )(x, *coded, w)
-
-
-def body(code_index, code_value, decoder, mlp_out):
+    )(x, *coded, w, *after)
+
+
+def shift_z(x, d):
+    return lax.ppermute(x, "lat", lat_xor(2 * d))
+
+
+def layer(code_index, code_value, decoder, mlp_out):
     sources, lat_width, cols = decoder.shape
     w = decoder.reshape(sources * lat_width, cols)
     rows = code_index.shape[1]
@@ -282,17 +276,24 @@
     sent = jnp.broadcast_to(both[None], (16,) + both.shape).reshape(32, 2 * rows, 128)
     x = lax.all_to_all(sent, "tgt", 0, 0, tiled=True, axis_index_groups=groups)
 
-    errors, picks = [], []
+    near_of, own_of, after = [], [], []
     for part in range(PARTS):
-        mine, theirs = decode(x, w, part)
+        mine, theirs = decode(x, pltpu.with_memory_space_constraint(w, pltpu.HBM), part, after)
         recv = lax.ppermute(theirs, "lat", lat_xor(1))
-        own_sum, *near = pack(mine, recv, part)
-        near = [lax.ppermute(near[d - 1], "lat", lat_xor(2 * d)) for d in (1, 2, 3)]
-        error, coded = error_of(own_sum, near, mlp_out, part)
+        own_sum, *after = pack(mine, recv)
+        own_of.append(own_sum)
+        near_of.append([shift_z(after[d - 1], d) for d in (1, 2, 3)])
+    errors, coded_of, picks = [], [], []
+    for part in range(PARTS):
+        error, coded = error_of(own_of[part], near_of[part], mlp_out, part)
         errors.append(error)
-        coded = [coded] + [lax.ppermute(coded, "lat", lat_xor(2 * d)) for d in (1, 2, 3)]
+        coded_of.append([coded] + [shift_z(coded, d) for d in (1, 2, 3)])
+    for part in range(PARTS):
+        coded = coded_of[part]
         coded = coded + [lax.ppermute(c, "lat", lat_xor(1)) for c in coded]
-        picks.append(grads(x, coded, w, part).reshape(8, 64 // PARTS, 128))
+        after = [coded_of[-1][0]] if part + 1 < PARTS else []
+        picked = grads(x, coded, w, part, after)
+        picks.append(picked.reshape(8, 64 // PARTS, 128))
     error = jnp.concatenate(errors, axis=0)
     picked = jnp.concatenate(picks, axis=1).reshape(512, 128)
     parts = lax.all_to_all(picked, ("tgt", "lat"), 0, 0, tiled=True)
@@ -303,7 +304,7 @@
 def solution(mesh):
     placed = (P(None, "tgt", None), P(None, "tgt", None), P(None, "lat", "tgt"), P("lat", "tgt"))
     return jax.shard_map(
-        body,
+        layer,
         mesh=mesh,
         in_specs=placed,
         out_specs=(P("lat", "tgt"), P(None, ("tgt", "lat"), None)),

time: 117 us -> 112 us (0.957)
  blocking collectives: 37.5 us -> 14.2 us
  starting transfers between devices: 25.9 us -> 48.2 us
  Pallas kernels: 29.4 us -> 22 us
  waiting for transfers between devices: 17.6 us -> 22.2 us
  local copies, waits for them, and re-layouts: 4.01 us -> 0.91 us
  other arithmetic: 1.73 us -> 3.14 us
    all_to_all x2 -> x1, blocking collectives: 37.5 us -> 14.2 us  [layer(): x = lax.all_to_all(sent, 'tgt', 0, 0, tiled=True, axis_index_groups=groups)]
    all_to_all x0 -> x1, waiting for transfers between devices: none -> 14.9 us  [layer(): parts = lax.all_to_all(picked, ('tgt', 'lat'), 0, 0, tiled=True)]
    ppermute x12 -> x23, starting transfers between devices: 25.9 us -> 39.5 us  [the longest x12 15.2 us: shift_z(): return lax.ppermute(x, 'lat', lat_xor(2 * d))]
    ppermute x12 -> x23, waiting for transfers between devices: 17.6 us -> 7.28 us  [the longest x12 4.86 us: shift_z(): return lax.ppermute(x, 'lat', lat_xor(2 * d))]
    all_to_all x0 -> x1, starting transfers between devices: none -> 8.73 us  [layer(): parts = lax.all_to_all(picked, ('tgt', 'lat'), 0, 0, tiled=True)]
    pallas_call x2 -> x4, Pallas kernels: 28.3 us -> 21.6 us  [the longest x2 12.7 us: decode(): pl.pallas_call(lambda x_ref, w_ref, *refs: decode_kernel(part, x_ref, w_r...]
    unnamed x7, local copies, waits for them, and re-layouts: 3.7 us -> 0.6 us
    concatenate x0 -> x2, other arithmetic: none -> 1.41 us  [the longest x1 0.71 us: layer(): picked = jnp.concatenate(picks, axis=1).reshape(512, 128)]
  transfers between devices with their start and end apart: 12 -> 24, of which waited for: 8 -> 5; matrix products, arithmetic and copies ran while one was open for 0% -> 1% of each run, Pallas kernels for 0% -> 4%
where the time goes in v3:
time: 112 us; the launch traced here: 111 us
  starting transfers between devices  48.2 us (43%)
  waiting for transfers between devices  22.2 us (20%)
  Pallas kernels  22 us (20%)
  blocking collectives  14.2 us (13%)
  other arithmetic  3.14 us (3%)
    ppermute x12, starting transfers between devices, shift_z(): return lax.ppermute(x, 'lat', lat_xor(2 * d))  15.2 us
    all_to_all x1, waiting for transfers between devices, layer(): parts = lax.all_to_all(picked, ('tgt', 'lat'), 0, 0, tiled=True)  14.9 us
    all_to_all x1, blocking collectives, layer(): x = lax.all_to_all(sent, 'tgt', 0, 0, tiled=True, axis_index_groups=groups)  14.2 us
    ppermute x8, starting transfers between devices, layer(): coded = coded + [lax.ppermute(c, 'lat', lat_xor(1)) for c in coded]  13.1 us
    pallas_call x2, Pallas kernels, decode(): pl.pallas_call(lambda x_ref, w_ref, *refs: decode_kernel(part, x_ref, w_r...  12.7 us
    pallas_call x2, Pallas kernels, grads(): pl.pallas_call(lambda *refs: grads_kernel(part, *refs[:10], *refs[10 + le...  8.89 us
    all_to_all x1, starting transfers between devices, layer(): parts = lax.all_to_all(picked, ('tgt', 'lat'), 0, 0, tiled=True)  8.73 us
    ppermute x1, starting transfers between devices, layer(): other = lax.ppermute(own, 'tgt', tgt_shift(1))  7.76 us
  transfers between devices with their start and end apart: 24, of which 5 were waited for; matrix products, arithmetic and copies ran while one was open for 1% of the time, Pallas kernels for 4%

profile of v3, /device:TPU:1, one launch (start us, length us, event | category | flops | bytes accessed | tf_op | source)
XLA Modules:
  0.0 111.4 jit_solution(15440813855130358157)
XLA Ops:
  0.6 0.7 fusion
  1.3 0.7 convert_bitcast_fusion
  2.1 0.1 reshape.61
  2.2 7.8 %collective-permute-start = (s16[32,128]{1,0:T(8,128)(2,1)S(1)}, s16[32,128]{1,0:T(8,128)(2,1)S(1)}, u32[]{:S(2)}, u32[]{:S(2)}) collective-permute-start(s16[32,128]{1,0:T(8,128)(2,1)S(1)} %reshape.61), channel_id=1, source_target_pairs={{0,128},{8,136},{16,144},{24,152},{32,160},{40,168},{48,176},{56,1... | collective-permute-start | bytes 24584 | tf_op jit(solution)/shard_map/ppermute | solution.py:273
  9.9 0.1 stack.27
  10.0 1.0 collective-permute-done
  11.0 14.2 %all_to_all.14.x_ref.refs_0_ = s16[32,32,128]{2,1,0:T(8,128)(2,1)S(1)} all-to-all(s16[32,32,128]{2,1,0:T(8,128)(2,1)S(1)} %bitcast.21), channel_id=1, replica_groups={{0,8,16,24,32,40,48,56,64,72,80,88,96,104,112,120},{128,136,144,152,160..., dimensions={0} | all-to-all | bytes 524288 | tf_op jit(solution)/shard_map/all_to_all | solution.py:277
  25.2 6.4 %shard_map.59 = (f32[4,32,896]{2,1,0:T(8,128)S(1)}, f32[4,32,896]{2,1,0:T(8,128)S(1)}) custom-call(s16[32,32,128]{2,1,0:T(8,128)(2,1)S(1)} %all_to_all.14.x_ref.refs_0_, bf16[4096,896]{1,0:T(8,128)(2,1)} %bitcast.15), custom_call_target="tpu_custom_call" | custom-call | flops 3758096384 | bytes 7340032 | tf_op jit(solution)/shard_map/pallas_call | solution.py:140
  31.6 3.0 %collective-permute-start.1 = (f32[4,32,896]{2,1,0:T(8,128)S(1)}, f32[4,32,896]{2,1,0:T(8,128)S(1)}, u32[]{:S(2)}, u32[]{:S(2)}) collective-permute-start(f32[4,32,896]{2,1,0:T(8,128)S(1)} %get-tuple-element.19), channel_id=1, source_target_pairs={{0,1},{1,0},{2,3},{3,2},{4,5},{5,4},{6,7},{7,6},{8,9},{9,8},{10,11... | collective-permute-start | bytes 1376264 | tf_op jit(solution)/shard_map/ppermute | solution.py:282
  34.6 1.4 %collective-permute-done.1.recv_ref = f32[4,32,896]{2,1,0:T(8,128)S(1)} collective-permute-done((f32[4,32,896]{2,1,0:T(8,128)S(1)}, f32[4,32,896]{2,1,0:T(8,128)S(1)}, u32[]{:S(2)}, u32[]{:S(2)}) %collective-permute-start.1) | collective-permute-done | bytes 458784 | tf_op jit(solution)/shard_map/ppermute | solution.py:282
  36.0 0.1 shard_map.60
  36.1 0.0 slice-start.1
  36.1 6.4 %shard_map.62 = (f32[4,32,896]{2,1,0:T(8,128)S(1)}, f32[4,32,896]{2,1,0:T(8,128)S(1)}) custom-call(s16[32,32,128]{2,1,0:T(8,128)(2,1)S(1)} %all_to_all.14.x_ref.refs_0_, bf16[4096,896]{1,0:T(8,128)(2,1)} %bitcast.16, s16[32,1024]{1,0:T(8,128)(2,1)S(1)} %get-tuple-element.21.refs_0_, s16[32,1024]{1,0:T(8,128)(2,1)S(1)} %get-tuple-element.22.refs_1_, ...), custom_call_target="tpu_custom_call" | custom-call | flops 3758096384 | bytes 7340032 | tf_op jit(solution)/shard_map/pallas_call | solution.py:140
  42.5 0.5 collective-permute-start.5
  43.0 0.7 collective-permute-start.2
  43.7 2.6 %collective-permute-start.3 = (s16[32,1024]{1,0:T(8,128)(2,1)S(1)}, s16[32,1024]{1,0:T(8,128)(2,1)S(1)}, u32[]{:S(2)}, u32[]{:S(2)}) collective-permute-start(s16[32,1024]{1,0:T(8,128)(2,1)S(1)} %get-tuple-element.22.refs_1_), channel_id=1, source_target_pairs={{0,4},{1,5},{2,6},{3,7},{4,0},{5,1},{6,2},{7,3},{8,12},{9,13},{10,... | collective-permute-start | bytes 196616 | tf_op jit(solution)/shard_map/ppermute | solution.py:261
  46.3 0.2 collective-permute-start.4
  46.5 0.0 collective-permute-done.2.refs_1_
  46.5 2.0 %collective-permute-done.3.refs_2_ = s16[32,1024]{1,0:T(8,128)(2,1)S(1)} collective-permute-done((s16[32,1024]{1,0:T(8,128)(2,1)S(1)}, s16[32,1024]{1,0:T(8,128)(2,1)S(1)}, u32[]{:S(2)}, u32[]{:S(2)}) %collective-permute-start.3) | collective-permute-done | bytes 65568 | tf_op jit(solution)/shard_map/ppermute | solution.py:261
  48.5 2.9 %collective-permute-done.4.refs_3_ = s16[32,1024]{1,0:T(8,128)(2,1)S(1)} collective-permute-done((s16[32,1024]{1,0:T(8,128)(2,1)S(1)}, s16[32,1024]{1,0:T(8,128)(2,1)S(1)}, u32[]{:S(2)}, u32[]{:S(2)}) %collective-permute-start.4) | collective-permute-done | bytes 65568 | tf_op jit(solution)/shard_map/ppermute | solution.py:261
  51.4 0.1 shard_map.61
  51.5 1.9 %collective-permute-start.9 = (s16[32,1024]{1,0:T(8,128)(2,1)S(1)}, s16[32,1024]{1,0:T(8,128)(2,1)S(1)}, u32[]{:S(2)}, u32[]{:S(2)}) collective-permute-start(s16[32,1024]{1,0:T(8,128)(2,1)S(1)} %get-tuple-element.32.refs_1_), channel_id=1, source_target_pairs={{0,2},{1,3},{2,0},{3,1},{4,6},{5,7},{6,4},{7,5},{8,10},{9,11},{10,... | collective-permute-start | bytes 196616 | tf_op jit(solution)/shard_map/ppermute | solution.py:261
  53.4 0.5 collective-permute-start.10
  53.9 0.0 collective-permute-done.5.recv_ref
  53.9 0.1 shard_map.63
  54.0 1.5 %collective-permute-start.6 = (s16[32,1024]{1,0:T(8,128)(2,1)S(1)}, s16[32,1024]{1,0:T(8,128)(2,1)S(1)}, u32[]{:S(2)}, u32[]{:S(2)}) collective-permute-start(s16[32,1024]{1,0:T(8,128)(2,1)S(1)} %get-tuple-element.28), channel_id=1, source_target_pairs={{0,2},{1,3},{2,0},{3,1},{4,6},{5,7},{6,4},{7,5},{8,10},{9,11},{10,... | collective-permute-start | bytes 196616 | tf_op jit(solution)/shard_map/ppermute | solution.py:261
  55.4 0.6 collective-permute-start.7
  56.1 1.6 %collective-permute-start.8 = (s16[32,1024]{1,0:T(8,128)(2,1)S(1)}, s16[32,1024]{1,0:T(8,128)(2,1)S(1)}, u32[]{:S(2)}, u32[]{:S(2)}) collective-permute-start(s16[32,1024]{1,0:T(8,128)(2,1)S(1)} %get-tuple-element.30), channel_id=1, source_target_pairs={{0,6},{1,7},{2,4},{3,5},{4,2},{5,3},{6,0},{7,1},{8,14},{9,15},{10,... | collective-permute-start | bytes 196616 | tf_op jit(solution)/shard_map/ppermute | solution.py:261
  57.6 0.0 collective-permute-done.9.refs_2_
  57.6 1.7 %collective-permute-start.11 = (s16[32,1024]{1,0:T(8,128)(2,1)S(1)}, s16[32,1024]{1,0:T(8,128)(2,1)S(1)}, u32[]{:S(2)}, u32[]{:S(2)}) collective-permute-start(s16[32,1024]{1,0:T(8,128)(2,1)S(1)} %get-tuple-element.32.refs_1_), channel_id=1, source_target_pairs={{0,6},{1,7},{2,4},{3,5},{4,2},{5,3},{6,0},{7,1},{8,14},{9,15},{10,... | collective-permute-start | bytes 196616 | tf_op jit(solution)/shard_map/ppermute | solution.py:261
  59.3 0.0 collective-permute-done.10.refs_3_
  59.3 3.1 %collective-permute-start.12 = (s16[32,1024]{1,0:T(8,128)(2,1)S(1)}, s16[32,1024]{1,0:T(8,128)(2,1)S(1)}, u32[]{:S(2)}, u32[]{:S(2)}) collective-permute-start(s16[32,1024]{1,0:T(8,128)(2,1)S(1)} %get-tuple-element.32.refs_1_), channel_id=1, source_target_pairs={{0,1},{1,0},{2,3},{3,2},{4,5},{5,4},{6,7},{7,6},{8,9},{9,8},{10,11... | collective-permute-start | bytes 196616 | tf_op jit(solution)/shard_map/ppermute | solution.py:293
  62.5 0.0 collective-permute-done.6.refs_1_
  62.5 0.1 collective-permute-start.13
  62.6 0.0 collective-permute-done.7.refs_2_
  62.6 3.5 %collective-permute-start.14 = (s16[32,1024]{1,0:T(8,128)(2,1)S(1)}, s16[32,1024]{1,0:T(8,128)(2,1)S(1)}, u32[]{:S(2)}, u32[]{:S(2)}) collective-permute-start(s16[32,1024]{1,0:T(8,128)(2,1)S(1)} %collective-permute-done.10.refs_3_), channel_id=1, source_target_pairs={{0,1},{1,0},{2,3},{3,2},{4,5},{5,4},{6,7},{7,6},{8,9},{9,8},{10,11... | collective-permute-start | bytes 196616 | tf_op jit(solution)/shard_map/ppermute | solution.py:293
  66.1 0.0 collective-permute-done.8.refs_3_
  66.1 0.1 shard_map.64
  66.2 0.1 collective-permute-start.16
  66.3 0.0 collective-permute-done.11.refs_4_
  66.3 3.0 %collective-permute-start.17 = (s16[32,1024]{1,0:T(8,128)(2,1)S(1)}, s16[32,1024]{1,0:T(8,128)(2,1)S(1)}, u32[]{:S(2)}, u32[]{:S(2)}) collective-permute-start(s16[32,1024]{1,0:T(8,128)(2,1)S(1)} %get-tuple-element.33.refs_10_.refs_1_), channel_id=1, source_target_pairs={{0,4},{1,5},{2,6},{3,7},{4,0},{5,1},{6,2},{7,3},{8,12},{9,13},{10,... | collective-permute-start | bytes 196616 | tf_op jit(solution)/shard_map/ppermute | solution.py:261
  69.2 0.0 collective-permute-done.12.refs_5_
  69.2 0.8 collective-permute-start.18
  70.1 0.0 collective-permute-done.13.refs_6_
  70.1 1.7 %collective-permute-start.15 = (s16[32,1024]{1,0:T(8,128)(2,1)S(1)}, s16[32,1024]{1,0:T(8,128)(2,1)S(1)}, u32[]{:S(2)}, u32[]{:S(2)}) collective-permute-start(s16[32,1024]{1,0:T(8,128)(2,1)S(1)} %collective-permute-done.11.refs_4_), channel_id=1, source_target_pairs={{0,1},{1,0},{2,3},{3,2},{4,5},{5,4},{6,7},{7,6},{8,9},{9,8},{10,11... | collective-permute-start | bytes 196616 | tf_op jit(solution)/shard_map/ppermute | solution.py:293
  71.8 0.0 collective-permute-done.14.refs_7_
  71.8 0.1 collective-permute-start.19
  71.9 0.0 collective-permute-done.16.refs_2_
  71.9 0.4 collective-permute-start.20
  72.3 0.0 collective-permute-done.17.refs_3_
  72.3 3.2 %collective-permute-start.21 = (s16[32,1024]{1,0:T(8,128)(2,1)S(1)}, s16[32,1024]{1,0:T(8,128)(2,1)S(1)}, u32[]{:S(2)}, u32[]{:S(2)}) collective-permute-start(s16[32,1024]{1,0:T(8,128)(2,1)S(1)} %collective-permute-done.17.refs_3_), channel_id=1, source_target_pairs={{0,1},{1,0},{2,3},{3,2},{4,5},{5,4},{6,7},{7,6},{8,9},{9,8},{10,11... | collective-permute-start | bytes 196616 | tf_op jit(solution)/shard_map/ppermute | solution.py:293
  75.5 1.0 collective-permute-start.22
  76.5 4.4 %shard_map.65 = f32[256,128]{1,0:T(8,128)S(1)} custom-call(s16[32,32,128]{2,1,0:T(8,128)(2,1)S(1)} %all_to_all.14.x_ref.refs_0_, s16[32,1024]{1,0:T(8,128)(2,1)S(1)} %get-tuple-element.32.refs_1_, s16[32,1024]{1,0:T(8,128)(2,1)S(1)} %collective-permute-done.9.refs_2_, s16[32,1024]{1,0:T(8,128)(2,1)S(1)} %collective-permute-done.10.refs_3_, ...), custom_call_target="tpu_custom_call" | custom-call | flops 3758096384 | bytes 7340032 | tf_op jit(solution)/shard_map/pallas_call | solution.py:247
  80.9 0.0 collective-permute-done.19.refs_5_
  80.9 0.0 collective-permute-done.20.refs_6_
  81.0 0.0 collective-permute-done.22.refs_8_
  81.0 4.4 %shard_map.66 = f32[256,128]{1,0:T(8,128)S(1)} custom-call(s16[32,32,128]{2,1,0:T(8,128)(2,1)S(1)} %all_to_all.14.x_ref.refs_0_, s16[32,1024]{1,0:T(8,128)(2,1)S(1)} %get-tuple-element.33.refs_10_.refs_1_, s16[32,1024]{1,0:T(8,128)(2,1)S(1)} %collective-permute-done.16.refs_2_, s16[32,1024]{1,0:T(8,128)(2,1)S(1)} %collective-permute-done.17.refs_3_, ...), custom_call_target="tpu_custom_call" | custom-call | flops 3758096384 | bytes 7340032 | tf_op jit(solution)/shard_map/pallas_call | solution.py:247
  85.4 0.7 pad_maximum_fusion
  86.1 8.7 %all-to-all-start.1 = ((f32[256,2,128]{2,1,0:T(2,128)}), f32[256,2,128]{2,1,0:T(2,128)S(1)}, u32[]{:S(2)}, u32[]{:S(2)}) async-start(f32[256,2,128]{2,1,0:T(2,128)} %bitcast.8), calls=%async_computation.1 | async-start | bytes 524288 | tf_op jit(solution)/shard_map/all_to_all | solution.py:299
  94.9 0.7 pad_maximum_fusion.1
  95.6 14.9 %all-to-all-done.1 = f32[256,2,128]{2,1,0:T(2,128)S(1)} async-done(((f32[256,2,128]{2,1,0:T(2,128)}), f32[256,2,128]{2,1,0:T(2,128)S(1)}, u32[]{:S(2)}, u32[]{:S(2)}) %all-to-all-start.1) | async-done | bytes 262176 | tf_op jit(solution)/shard_map/all_to_all | solution.py:299
  110.5 0.3 reduce_sum.9
  110.7 0.1 div.23
  110.8 0.6 copy.8
  (14 shorter events, 0.1 us)
Async XLA Ops:
  2.2 8.8 %collective-permute-start = (s16[32,128]{1,0:T(8,128)(2,1)S(1)}, s16[32,128]{1,0:T(8,128)(2,1)S(1)}, u32[]{:S(2)}, u32[]{:S(2)}) collective-permute-start(s16[32,128]{1,0:T(8,128)(2,1)S(1)} %reshape.61), channel_id=1, source_target_pairs={{0,128},{8,136},{16,144},{24,152},{32,160},{40,168},{48,176},{56,1... | collective-permute-start | bytes 24584 | tf_op jit(solution)/shard_map/ppermute | solution.py:273
  31.6 4.4 %collective-permute-start.1 = (f32[4,32,896]{2,1,0:T(8,128)S(1)}, f32[4,32,896]{2,1,0:T(8,128)S(1)}, u32[]{:S(2)}, u32[]{:S(2)}) collective-permute-start(f32[4,32,896]{2,1,0:T(8,128)S(1)} %get-tuple-element.19), channel_id=1, source_target_pairs={{0,1},{1,0},{2,3},{3,2},{4,5},{5,4},{6,7},{7,6},{8,9},{9,8},{10,11... | collective-permute-start | bytes 1376264 | tf_op jit(solution)/shard_map/ppermute | solution.py:282
  36.0 15.3 %copy-start = (bf16[64,896]{1,0:T(8,128)(2,1)S(1)}, bf16[64,896]{1,0:T(8,128)(2,1)}, u32[]{:S(2)}) copy-start(bf16[64,896]{1,0:T(8,128)(2,1)} %refs_4_.3) | copy-start | bytes 344068
  36.0 40.5 %slice-start = ((s8[7340032]{0:T(1024)(128)(4,1)}), s8[4194304]{0:T(1024)(128)(4,1)S(1)}, s32[]{:S(2)}) async-start(s8[7340032]{0:T(1024)(128)(4,1)} %bitcast.17), calls=%async_computation.2 | async-start | bytes 8388608
  36.1 40.4 %slice-start.1 = ((s8[7340032]{0:T(1024)(128)(4,1)}), s8[3145728]{0:T(1024)(128)(4,1)S(1)}, s32[]{:S(2)}) async-start(s8[7340032]{0:T(1024)(128)(4,1)} %bitcast.17), calls=%async_computation.3 | async-start | bytes 6291456
  42.5 11.4 %collective-permute-start.5 = (f32[4,32,896]{2,1,0:T(8,128)S(1)}, f32[4,32,896]{2,1,0:T(8,128)S(1)}, u32[]{:S(2)}, u32[]{:S(2)}) collective-permute-start(f32[4,32,896]{2,1,0:T(8,128)S(1)} %get-tuple-element.26), channel_id=1, source_target_pairs={{0,1},{1,0},{2,3},{3,2},{4,5},{5,4},{6,7},{7,6},{8,9},{9,8},{10,11... | collective-permute-start | bytes 1376264 | tf_op jit(solution)/shard_map/ppermute | solution.py:282
  43.0 3.6 %collective-permute-start.2 = (s16[32,1024]{1,0:T(8,128)(2,1)S(1)}, s16[32,1024]{1,0:T(8,128)(2,1)S(1)}, u32[]{:S(2)}, u32[]{:S(2)}) collective-permute-start(s16[32,1024]{1,0:T(8,128)(2,1)S(1)} %get-tuple-element.21.refs_0_), channel_id=1, source_target_pairs={{0,2},{1,3},{2,0},{3,1},{4,6},{5,7},{6,4},{7,5},{8,10},{9,11},{10,... | collective-permute-start | bytes 196616 | tf_op jit(solution)/shard_map/ppermute | solution.py:261
  43.7 4.8 %collective-permute-start.3 = (s16[32,1024]{1,0:T(8,128)(2,1)S(1)}, s16[32,1024]{1,0:T(8,128)(2,1)S(1)}, u32[]{:S(2)}, u32[]{:S(2)}) collective-permute-start(s16[32,1024]{1,0:T(8,128)(2,1)S(1)} %get-tuple-element.22.refs_1_), channel_id=1, source_target_pairs={{0,4},{1,5},{2,6},{3,7},{4,0},{5,1},{6,2},{7,3},{8,12},{9,13},{10,... | collective-permute-start | bytes 196616 | tf_op jit(solution)/shard_map/ppermute | solution.py:261
  46.3 5.0 %collective-permute-start.4 = (s16[32,1024]{1,0:T(8,128)(2,1)S(1)}, s16[32,1024]{1,0:T(8,128)(2,1)S(1)}, u32[]{:S(2)}, u32[]{:S(2)}) collective-permute-start(s16[32,1024]{1,0:T(8,128)(2,1)S(1)} %get-tuple-element.23.refs_2_), channel_id=1, source_target_pairs={{0,6},{1,7},{2,4},{3,5},{4,2},{5,3},{6,0},{7,1},{8,14},{9,15},{10,... | collective-permute-start | bytes 196616 | tf_op jit(solution)/shard_map/ppermute | solution.py:261
  51.5 6.1 %collective-permute-start.9 = (s16[32,1024]{1,0:T(8,128)(2,1)S(1)}, s16[32,1024]{1,0:T(8,128)(2,1)S(1)}, u32[]{:S(2)}, u32[]{:S(2)}) collective-permute-start(s16[32,1024]{1,0:T(8,128)(2,1)S(1)} %get-tuple-element.32.refs_1_), channel_id=1, source_target_pairs={{0,2},{1,3},{2,0},{3,1},{4,6},{5,7},{6,4},{7,5},{8,10},{9,11},{10,... | collective-permute-start | bytes 196616 | tf_op jit(solution)/shard_map/ppermute | solution.py:261
  53.4 5.9 %collective-permute-start.10 = (s16[32,1024]{1,0:T(8,128)(2,1)S(1)}, s16[32,1024]{1,0:T(8,128)(2,1)S(1)}, u32[]{:S(2)}, u32[]{:S(2)}) collective-permute-start(s16[32,1024]{1,0:T(8,128)(2,1)S(1)} %get-tuple-element.32.refs_1_), channel_id=1, source_target_pairs={{0,4},{1,5},{2,6},{3,7},{4,0},{5,1},{6,2},{7,3},{8,12},{9,13},{10,... | collective-permute-start | bytes 196616 | tf_op jit(solution)/shard_map/ppermute | solution.py:261
  54.0 8.5 %collective-permute-start.6 = (s16[32,1024]{1,0:T(8,128)(2,1)S(1)}, s16[32,1024]{1,0:T(8,128)(2,1)S(1)}, u32[]{:S(2)}, u32[]{:S(2)}) collective-permute-start(s16[32,1024]{1,0:T(8,128)(2,1)S(1)} %get-tuple-element.28), channel_id=1, source_target_pairs={{0,2},{1,3},{2,0},{3,1},{4,6},{5,7},{6,4},{7,5},{8,10},{9,11},{10,... | collective-permute-start | bytes 196616 | tf_op jit(solution)/shard_map/ppermute | solution.py:261
  55.4 7.1 %collective-permute-start.7 = (s16[32,1024]{1,0:T(8,128)(2,1)S(1)}, s16[32,1024]{1,0:T(8,128)(2,1)S(1)}, u32[]{:S(2)}, u32[]{:S(2)}) collective-permute-start(s16[32,1024]{1,0:T(8,128)(2,1)S(1)} %get-tuple-element.29), channel_id=1, source_target_pairs={{0,4},{1,5},{2,6},{3,7},{4,0},{5,1},{6,2},{7,3},{8,12},{9,13},{10,... | collective-permute-start | bytes 196616 | tf_op jit(solution)/shard_map/ppermute | solution.py:261
  56.1 10.0 %collective-permute-start.8 = (s16[32,1024]{1,0:T(8,128)(2,1)S(1)}, s16[32,1024]{1,0:T(8,128)(2,1)S(1)}, u32[]{:S(2)}, u32[]{:S(2)}) collective-permute-start(s16[32,1024]{1,0:T(8,128)(2,1)S(1)} %get-tuple-element.30), channel_id=1, source_target_pairs={{0,6},{1,7},{2,4},{3,5},{4,2},{5,3},{6,0},{7,1},{8,14},{9,15},{10,... | collective-permute-start | bytes 196616 | tf_op jit(solution)/shard_map/ppermute | solution.py:261
  57.6 8.7 %collective-permute-start.11 = (s16[32,1024]{1,0:T(8,128)(2,1)S(1)}, s16[32,1024]{1,0:T(8,128)(2,1)S(1)}, u32[]{:S(2)}, u32[]{:S(2)}) collective-permute-start(s16[32,1024]{1,0:T(8,128)(2,1)S(1)} %get-tuple-element.32.refs_1_), channel_id=1, source_target_pairs={{0,6},{1,7},{2,4},{3,5},{4,2},{5,3},{6,0},{7,1},{8,14},{9,15},{10,... | collective-permute-start | bytes 196616 | tf_op jit(solution)/shard_map/ppermute | solution.py:261
  59.3 9.9 %collective-permute-start.12 = (s16[32,1024]{1,0:T(8,128)(2,1)S(1)}, s16[32,1024]{1,0:T(8,128)(2,1)S(1)}, u32[]{:S(2)}, u32[]{:S(2)}) collective-permute-start(s16[32,1024]{1,0:T(8,128)(2,1)S(1)} %get-tuple-element.32.refs_1_), channel_id=1, source_target_pairs={{0,1},{1,0},{2,3},{3,2},{4,5},{5,4},{6,7},{7,6},{8,9},{9,8},{10,11... | collective-permute-start | bytes 196616 | tf_op jit(solution)/shard_map/ppermute | solution.py:293
  62.5 7.6 %collective-permute-start.13 = (s16[32,1024]{1,0:T(8,128)(2,1)S(1)}, s16[32,1024]{1,0:T(8,128)(2,1)S(1)}, u32[]{:S(2)}, u32[]{:S(2)}) collective-permute-start(s16[32,1024]{1,0:T(8,128)(2,1)S(1)} %collective-permute-done.9.refs_2_), channel_id=1, source_target_pairs={{0,1},{1,0},{2,3},{3,2},{4,5},{5,4},{6,7},{7,6},{8,9},{9,8},{10,11... | collective-permute-start | bytes 196616 | tf_op jit(solution)/shard_map/ppermute | solution.py:293
  62.6 9.2 %collective-permute-start.14 = (s16[32,1024]{1,0:T(8,128)(2,1)S(1)}, s16[32,1024]{1,0:T(8,128)(2,1)S(1)}, u32[]{:S(2)}, u32[]{:S(2)}) collective-permute-start(s16[32,1024]{1,0:T(8,128)(2,1)S(1)} %collective-permute-done.10.refs_3_), channel_id=1, source_target_pairs={{0,1},{1,0},{2,3},{3,2},{4,5},{5,4},{6,7},{7,6},{8,9},{9,8},{10,11... | collective-permute-start | bytes 196616 | tf_op jit(solution)/shard_map/ppermute | solution.py:293
  66.2 5.7 %collective-permute-start.16 = (s16[32,1024]{1,0:T(8,128)(2,1)S(1)}, s16[32,1024]{1,0:T(8,128)(2,1)S(1)}, u32[]{:S(2)}, u32[]{:S(2)}) collective-permute-start(s16[32,1024]{1,0:T(8,128)(2,1)S(1)} %get-tuple-element.33.refs_10_.refs_1_), channel_id=1, source_target_pairs={{0,2},{1,3},{2,0},{3,1},{4,6},{5,7},{6,4},{7,5},{8,10},{9,11},{10,... | collective-permute-start | bytes 196616 | tf_op jit(solution)/shard_map/ppermute | solution.py:261
  66.3 6.0 %collective-permute-start.17 = (s16[32,1024]{1,0:T(8,128)(2,1)S(1)}, s16[32,1024]{1,0:T(8,128)(2,1)S(1)}, u32[]{:S(2)}, u32[]{:S(2)}) collective-permute-start(s16[32,1024]{1,0:T(8,128)(2,1)S(1)} %get-tuple-element.33.refs_10_.refs_1_), channel_id=1, source_target_pairs={{0,4},{1,5},{2,6},{3,7},{4,0},{5,1},{6,2},{7,3},{8,12},{9,13},{10,... | collective-permute-start | bytes 196616 | tf_op jit(solution)/shard_map/ppermute | solution.py:261
  69.2 6.2 %collective-permute-start.18 = (s16[32,1024]{1,0:T(8,128)(2,1)S(1)}, s16[32,1024]{1,0:T(8,128)(2,1)S(1)}, u32[]{:S(2)}, u32[]{:S(2)}) collective-permute-start(s16[32,1024]{1,0:T(8,128)(2,1)S(1)} %get-tuple-element.33.refs_10_.refs_1_), channel_id=1, source_target_pairs={{0,6},{1,7},{2,4},{3,5},{4,2},{5,3},{6,0},{7,1},{8,14},{9,15},{10,... | collective-permute-start | bytes 196616 | tf_op jit(solution)/shard_map/ppermute | solution.py:261
  70.1 6.4 %collective-permute-start.15 = (s16[32,1024]{1,0:T(8,128)(2,1)S(1)}, s16[32,1024]{1,0:T(8,128)(2,1)S(1)}, u32[]{:S(2)}, u32[]{:S(2)}) collective-permute-start(s16[32,1024]{1,0:T(8,128)(2,1)S(1)} %collective-permute-done.11.refs_4_), channel_id=1, source_target_pairs={{0,1},{1,0},{2,3},{3,2},{4,5},{5,4},{6,7},{7,6},{8,9},{9,8},{10,11... | collective-permute-start | bytes 196616 | tf_op jit(solution)/shard_map/ppermute | solution.py:293
  71.8 9.2 %collective-permute-start.19 = (s16[32,1024]{1,0:T(8,128)(2,1)S(1)}, s16[32,1024]{1,0:T(8,128)(2,1)S(1)}, u32[]{:S(2)}, u32[]{:S(2)}) collective-permute-start(s16[32,1024]{1,0:T(8,128)(2,1)S(1)} %get-tuple-element.33.refs_10_.refs_1_), channel_id=1, source_target_pairs={{0,1},{1,0},{2,3},{3,2},{4,5},{5,4},{6,7},{7,6},{8,9},{9,8},{10,11... | collective-permute-start | bytes 196616 | tf_op jit(solution)/shard_map/ppermute | solution.py:293
  71.9 9.1 %collective-permute-start.20 = (s16[32,1024]{1,0:T(8,128)(2,1)S(1)}, s16[32,1024]{1,0:T(8,128)(2,1)S(1)}, u32[]{:S(2)}, u32[]{:S(2)}) collective-permute-start(s16[32,1024]{1,0:T(8,128)(2,1)S(1)} %collective-permute-done.16.refs_2_), channel_id=1, source_target_pairs={{0,1},{1,0},{2,3},{3,2},{4,5},{5,4},{6,7},{7,6},{8,9},{9,8},{10,11... | collective-permute-start | bytes 196616 | tf_op jit(solution)/shard_map/ppermute | solution.py:293
  72.3 8.7 %collective-permute-start.21 = (s16[32,1024]{1,0:T(8,128)(2,1)S(1)}, s16[32,1024]{1,0:T(8,128)(2,1)S(1)}, u32[]{:S(2)}, u32[]{:S(2)}) collective-permute-start(s16[32,1024]{1,0:T(8,128)(2,1)S(1)} %collective-permute-done.17.refs_3_), channel_id=1, source_target_pairs={{0,1},{1,0},{2,3},{3,2},{4,5},{5,4},{6,7},{7,6},{8,9},{9,8},{10,11... | collective-permute-start | bytes 196616 | tf_op jit(solution)/shard_map/ppermute | solution.py:293
  75.5 5.5 %collective-permute-start.22 = (s16[32,1024]{1,0:T(8,128)(2,1)S(1)}, s16[32,1024]{1,0:T(8,128)(2,1)S(1)}, u32[]{:S(2)}, u32[]{:S(2)}) collective-permute-start(s16[32,1024]{1,0:T(8,128)(2,1)S(1)} %collective-permute-done.18.refs_4_), channel_id=1, source_target_pairs={{0,1},{1,0},{2,3},{3,2},{4,5},{5,4},{6,7},{7,6},{8,9},{9,8},{10,11... | collective-permute-start | bytes 196616 | tf_op jit(solution)/shard_map/ppermute | solution.py:293
  86.1 24.3 %all-to-all-start.1 = ((f32[256,2,128]{2,1,0:T(2,128)}), f32[256,2,128]{2,1,0:T(2,128)S(1)}, u32[]{:S(2)}, u32[]{:S(2)}) async-start(f32[256,2,128]{2,1,0:T(2,128)} %bitcast.8), calls=%async_computation.1 | async-start | bytes 524288 | tf_op jit(solution)/shard_map/all_to_all | solution.py:299

commit v4 on v3

--- a/solution.py
+++ b/solution.py
@@ -18,8 +18,12 @@
 PARAMS = pltpu.CompilerParams(vmem_limit_bytes=40 << 20)
 
 
-def tgt_shift(zh):
-    return [(t, t ^ (zh << 4)) for t in range(32)]
+def mirror():
+    pairs = []
+    for t in range(32):
+        for i in range(8):
+            pairs.append((t * 8 + i, (t ^ 16) * 8 + ((3 - i // 2) * 2 + i % 2)))
+    return pairs
 
 
 def lat_xor(d):
@@ -55,18 +59,26 @@
     return jnp.concatenate([wide[:, c * 128 : (c + 1) * 128] * scale for c in range(cols)], axis=1)
 
 
-def decode_kernel(part, x_ref, w_hbm, mine_ref, theirs_ref, codes_ref, w_ref, acc_ref, sem):
+def own_rows(part):
+    lat = lax.axis_index("lat")
+    row = pl.multiple_of((lat // 2 % 2) * 128 + (lat % 2) * 64, 64)
+    zh = lax.axis_index("tgt") // 16
+    return row, lat // 4 == (zh + part) % 2
+
+
+def decode_kernel(part, x_ref, w_hbm, mlp_hbm, mine_ref, theirs_ref, codes_ref, w_ref, mlp_ref, acc_ref, sem):
     chunks, tokens = codes_ref.shape[:2]
     his = chunks // 2
     width = his * LO
     group = tokens // 8
-    blocks = group // 16
     lat = lax.axis_index("lat")
     core = lat % 2
     start = lat * width
     steps = 8
     rows_w = w_hbm.shape[0] // steps
     copies = start_weights(w_hbm, w_ref, sem, steps)
+    mlp_copy = pltpu.make_async_copy(mlp_hbm, mlp_ref, sem.at[steps])
+    mlp_copy.start()
 
     half_lane = lax.broadcasted_iota(jnp.int32, (1, 128), 1) < 64
     shape = (his * 8 // 16, 16, 128)
@@ -76,10 +88,7 @@
     one = jnp.ones((), jnp.bfloat16)
 
     def densify(i, carry):
-        zy = i // blocks
-        xl = i % blocks
-        y = zy % 4
-        block = x_ref[(y * 4 + part * blocks + xl) * 2 + zy // 4].astype(jnp.int32)
+        block = x_ref[i].astype(jnp.int32)
         local = block[0:16] - start
         inside = (local >= 0) & (local < width)
         hi = jnp.where(inside, (local >> 7) * 8, -1024).astype(jnp.float32)
@@ -127,6 +136,10 @@
             acc_ref[...] = out
         else:
             acc_ref[...] += out
+    mlp_copy.wait()
+    own, in_part = own_rows(part)
+    own_mlp = jnp.where(in_part, mlp_ref[...].astype(jnp.float32), 0.0)
+    acc_ref[pl.ds(own, 64), :] = acc_ref[pl.ds(own, 64), :] - own_mlp
     for z in range(4):
         row = pl.multiple_of((z * 2 + core) * group, group)
         mine_ref[z] = acc_ref[pl.ds(row, group), :]
@@ -134,25 +147,26 @@
         theirs_ref[z] = acc_ref[pl.ds(row, group), :]
 
 
-def decode(x, w, part, after):
+def decode(x, w, mlp, part, after):
     tokens, cols = 512 // PARTS, w.shape[1]
     shape = jax.ShapeDtypeStruct((4, tokens // 8, cols), jnp.float32)
     return pl.pallas_call(
-        lambda x_ref, w_ref, *refs: decode_kernel(part, x_ref, w_ref, *refs[len(after) :]),
+        lambda x_ref, w_ref, m_ref, *refs: decode_kernel(part, x_ref, w_ref, m_ref, *refs[len(after) :]),
         out_shape=(shape, shape),
-        in_specs=[VMEM_SPEC, HBM_SPEC] + [ANY_SPEC] * len(after),
+        in_specs=[VMEM_SPEC, HBM_SPEC, HBM_SPEC] + [ANY_SPEC] * len(after),
         out_specs=(VMEM_SPEC, VMEM_SPEC),
         scratch_shapes=[
             pltpu.VMEM((w.shape[0] // LO, tokens, LO), jnp.bfloat16),
             pltpu.VMEM(w.shape, jnp.bfloat16),
+            pltpu.VMEM(mlp.shape, jnp.bfloat16),
             pltpu.VMEM((tokens, cols), jnp.float32),
-            pltpu.SemaphoreType.DMA((8,)),
+            pltpu.SemaphoreType.DMA((9,)),
         ],
         compiler_params=PARAMS,
         cost_estimate=pl.CostEstimate(
             flops=4 * tokens * w.shape[0] * cols, transcendentals=0, bytes_accessed=2 * w.size
         ),
-    )(x, w, *after)
+    )(x, w, mlp, *after)
 
 
 def pack_kernel(mine_ref, recv_ref, own_ref, *near_refs):
@@ -174,37 +188,31 @@
     )(mine, recv)
 
 
-def error_kernel(part, own_ref, a_ref, b_ref, c_ref, mlp_ref, error_ref, code_ref):
-    rows = own_ref.shape[0]
-    total = own_ref[...] + decoded(a_ref[...]) + decoded(b_ref[...]) + decoded(c_ref[...])
-    error = total - mlp_ref[part * rows : (part + 1) * rows, :].astype(jnp.float32)
-    error_ref[...] = error
-    code_ref[...] = encode(error)
-
-
-def error_of(own, near, mlp, part):
+def error_kernel(own_ref, a_ref, b_ref, c_ref, code_ref):
+    code_ref[...] = encode(own_ref[...] + decoded(a_ref[...]) + decoded(b_ref[...]) + decoded(c_ref[...]))
+
+
+def error_of(own, near):
     rows, cols = own.shape
     return pl.pallas_call(
-        lambda *refs: error_kernel(part, *refs),
-        out_shape=(
-            jax.ShapeDtypeStruct((rows, cols), jnp.float32),
-            jax.ShapeDtypeStruct((rows, cols + 128), jnp.int16),
-        ),
-        in_specs=[VMEM_SPEC] * 5,
-        out_specs=(VMEM_SPEC,) * 2,
+        error_kernel,
+        out_shape=jax.ShapeDtypeStruct((rows, cols + 128), jnp.int16),
+        in_specs=[VMEM_SPEC] * 4,
+        out_specs=VMEM_SPEC,
         compiler_params=PARAMS,
-    )(own, *near, mlp)
+    )(own, *near)
 
 
 def grads_kernel(part, x_ref, *refs):
     coded = refs[:8]
-    w_ref, out_ref, err_ref = refs[8:]
+    w_ref = refs[8]
+    first = refs[9 : 9 + 2 * part]
+    error_ref, out_ref, err_ref, full_ref = refs[9 + 2 * part :]
     steps = 4
     rows_w = w_ref.shape[0] // steps
     cols = w_ref.shape[1]
-    tokens = out_ref.shape[0]
+    tokens = err_ref.shape[0]
     group = tokens // 8
-    blocks = group // 16
     lat = lax.axis_index("lat")
     core = lat % 2
     z = lat // 2
@@ -213,6 +221,7 @@
         c = core if side == 0 else 1 - core
         row = pl.multiple_of(((z ^ d) * 2 + c) * group, group)
         e = decoded(ref[...])
+        full_ref[pl.ds(row, group), :] = e
         high = e.astype(jnp.bfloat16)
         err_ref[pl.ds(row, group), :cols] = high
         err_ref[pl.ds(row, group), cols:] = (e - high.astype(jnp.float32)).astype(jnp.bfloat16)
@@ -222,15 +231,13 @@
     source = lax.broadcasted_iota(jnp.int32, (16, 128), 1) // 64
     keys, los = [], []
     for i in range(tokens // 16):
-        zy = i // blocks
-        b = ((zy % 4) * 4 + part * blocks + i % blocks) * 2 + zy // 4
-        local = x_ref[b, 0:16, :].astype(jnp.int32) - lat * width
+        local = x_ref[i, 0:16, :].astype(jnp.int32) - lat * width
         inside = (local >= 0) & (local < width)
         keys.append(jnp.where(inside, (local >> 7) + source * his, -1))
         los.append(local & (LO - 1))
     key = jnp.concatenate(keys, axis=0)
     lo = jnp.concatenate(los, axis=0)
-    picked = jnp.zeros(out_ref.shape, jnp.float32)
+    picked = jnp.zeros((tokens, LO), jnp.float32)
     for i in range(steps):
         w = w_ref[i * rows_w : (i + 1) * rows_w, :]
         grads = lax.dot_general(
@@ -239,22 +246,58 @@
         for j in range(rows_w // LO):
             found = jnp.take_along_axis(grads[:, j * LO : (j + 1) * LO], lo, axis=1)
             picked = jnp.where(key == i * (rows_w // LO) + j, found, picked)
-    out_ref[...] = picked
-
-
-def grads(x, coded, w, part, after):
+    own, in_part = own_rows(part)
+    error = full_ref[pl.ds(own, 64), :]
+    if part == 0:
+        error_ref[...] = error
+        out_ref[...] = picked
+    else:
+        error_ref[...] = jnp.where(in_part, error, first[0][...])
+        zh = lax.axis_index("tgt") // 16
+        out_ref[pl.ds(pl.multiple_of(zh * tokens, tokens), tokens), :] = first[1][...]
+        out_ref[pl.ds(pl.multiple_of((1 - zh) * tokens, tokens), tokens), :] = picked
+
+
+def grads(x, coded, w, part, first, after):
     tokens, cols = 512 // PARTS, w.shape[1]
+    args = (x, *coded, w, *first)
+    used = len(args)
     return pl.pallas_call(
-        lambda *refs: grads_kernel(part, *refs[:10], *refs[10 + len(after) :]),
-        out_shape=jax.ShapeDtypeStruct((tokens, 128), jnp.float32),
-        in_specs=[VMEM_SPEC] * 10 + [ANY_SPEC] * len(after),
-        out_specs=VMEM_SPEC,
-        scratch_shapes=[pltpu.VMEM((tokens, 2 * cols), jnp.bfloat16)],
+        lambda *refs: grads_kernel(part, *refs[:used], *refs[used + len(after) :]),
+        out_shape=(
+            jax.ShapeDtypeStruct((64, cols), jnp.float32),
+            jax.ShapeDtypeStruct((tokens * (part + 1), LO), jnp.float32),
+        ),
+        in_specs=[VMEM_SPEC] * used + [ANY_SPEC] * len(after),
+        out_specs=(VMEM_SPEC,) * 2,
+        scratch_shapes=[
+            pltpu.VMEM((tokens, 2 * cols), jnp.bfloat16),
+            pltpu.VMEM((tokens, cols), jnp.float32),
+        ],
         compiler_params=PARAMS,
         cost_estimate=pl.CostEstimate(
             flops=4 * tokens * w.shape[0] * cols, transcendentals=0, bytes_accessed=2 * w.size
         ),
-    )(x, *coded, w, *after)
+    )(*args, *after)
+
+
+def codes_kernel(index_ref, value_ref, out_ref):
+    index = jnp.concatenate([index_ref[0], index_ref[1]], axis=1)
+    value = jnp.concatenate([value_ref[0], value_ref[1]], axis=1).astype(jnp.float32) * VALUE_SCALE
+    both = jnp.concatenate([index, value.astype(jnp.int32)], axis=0).astype(jnp.int16)
+    for i in range(out_ref.shape[0]):
+        out_ref[i] = both
+
+
+def total_kernel(parts_ref, out_ref):
+    eight = parts_ref[0:8, :]
+    for i in range(1, parts_ref.shape[0] // 8):
+        eight = eight + parts_ref[8 * i : 8 * i + 8, :]
+    for j in range(2):
+        row = eight[j : j + 1] + eight[j + 2 : j + 3] + eight[j + 4 : j + 5] + eight[j + 6 : j + 7]
+        row = row * (1.0 / TARGETS)
+        for source in range(2):
+            out_ref[source, j : j + 1, :] = row[:, source * 64 : (source + 1) * 64]
 
 
 def shift_z(x, d):
@@ -265,40 +308,45 @@
     sources, lat_width, cols = decoder.shape
     w = decoder.reshape(sources * lat_width, cols)
     rows = code_index.shape[1]
-    zh = lax.axis_index("tgt") // 16
-
-    value = (code_value.astype(jnp.float32) * VALUE_SCALE).astype(jnp.int32)
-    own = jnp.stack([code_index, value]).astype(jnp.int16)
-    own = jnp.transpose(own, (0, 2, 1, 3)).reshape(2 * rows, 128)
-    other = lax.ppermute(own, "tgt", tgt_shift(1))
-    both = jnp.where(zh == 0, jnp.stack([own, other]), jnp.stack([other, own]))
+    sent = pl.pallas_call(
+        codes_kernel,
+        out_shape=jax.ShapeDtypeStruct((16, 2 * rows, 128), jnp.int16),
+        in_specs=[VMEM_SPEC] * 2,
+        out_specs=VMEM_SPEC,
+        name="codes",
+    )(code_index, code_value)
     groups = [[a * 16 + i for i in range(16)] for a in range(2)]
-    sent = jnp.broadcast_to(both[None], (16,) + both.shape).reshape(32, 2 * rows, 128)
-    x = lax.all_to_all(sent, "tgt", 0, 0, tiled=True, axis_index_groups=groups)
+    x = [lax.all_to_all(sent, "tgt", 0, 0, tiled=True, axis_index_groups=groups)]
+    x.append(lax.ppermute(x[0], ("tgt", "lat"), mirror()))
 
     near_of, own_of, after = [], [], []
     for part in range(PARTS):
-        mine, theirs = decode(x, pltpu.with_memory_space_constraint(w, pltpu.HBM), part, after)
+        w_hbm = pltpu.with_memory_space_constraint(w, pltpu.HBM)
+        mlp_hbm = pltpu.with_memory_space_constraint(mlp_out, pltpu.HBM)
+        mine, theirs = decode(x[part], w_hbm, mlp_hbm, part, after)
         recv = lax.ppermute(theirs, "lat", lat_xor(1))
         own_sum, *after = pack(mine, recv)
         own_of.append(own_sum)
         near_of.append([shift_z(after[d - 1], d) for d in (1, 2, 3)])
-    errors, coded_of, picks = [], [], []
+    coded_of, done = [], ()
     for part in range(PARTS):
-        error, coded = error_of(own_of[part], near_of[part], mlp_out, part)
-        errors.append(error)
+        coded = error_of(own_of[part], near_of[part])
         coded_of.append([coded] + [shift_z(coded, d) for d in (1, 2, 3)])
     for part in range(PARTS):
         coded = coded_of[part]
         coded = coded + [lax.ppermute(c, "lat", lat_xor(1)) for c in coded]
         after = [coded_of[-1][0]] if part + 1 < PARTS else []
-        picked = grads(x, coded, w, part, after)
-        picks.append(picked.reshape(8, 64 // PARTS, 128))
-    error = jnp.concatenate(errors, axis=0)
-    picked = jnp.concatenate(picks, axis=1).reshape(512, 128)
+        done = grads(x[part], coded, w, part, done, after)
+    error, picked = done
     parts = lax.all_to_all(picked, ("tgt", "lat"), 0, 0, tiled=True)
-    total = jnp.sum(parts.reshape(256, 2, sources, 64), axis=0)
-    return (error, jnp.transpose(total, (1, 0, 2)) / TARGETS)
+    total = pl.pallas_call(
+        total_kernel,
+        out_shape=jax.ShapeDtypeStruct((sources, 2, 64), jnp.float32),
+        in_specs=[VMEM_SPEC],
+        out_specs=VMEM_SPEC,
+        name="total",
+    )(parts)
+    return error, total
 
 
 def solution(mesh):

time: 112 us -> 111 us (level)
  blocking collectives: 14.2 us -> 37.8 us
  starting transfers between devices: 48.2 us -> 36.2 us
  waiting for transfers between devices: 22.2 us -> 10.5 us
  Pallas kernels: 22 us -> 25.8 us
  other arithmetic: 3.14 us -> 0.01 us
    all_to_all x1 -> x2, blocking collectives: 14.2 us -> 37.8 us  [the longest x1 23.4 us: layer(): parts = lax.all_to_all(picked, ('tgt', 'lat'), 0, 0, tiled=True)]
    all_to_all x1 -> x0, waiting for transfers between devices: 14.9 us -> none  [layer(): parts = lax.all_to_all(picked, ('tgt', 'lat'), 0, 0, tiled=True)]
    all_to_all x1 -> x0, starting transfers between devices: 8.73 us -> none  [layer(): parts = lax.all_to_all(picked, ('tgt', 'lat'), 0, 0, tiled=True)]
    ppermute x1, waiting for transfers between devices: 0.95 us -> 6.48 us  [layer(): x.append(lax.ppermute(x[0], ('tgt', 'lat'), mirror()))]
    pallas_call x6 -> x8, Pallas kernels: 21.8 us -> 25.6 us  [the longest x2 12.7 us: decode(): pl.pallas_call(lambda x_ref, w_ref, m_ref, *refs: decode_kernel(part, x_r...]
    ppermute x1, starting transfers between devices: 7.76 us -> 5.57 us  [layer(): x.append(lax.ppermute(x[0], ('tgt', 'lat'), mirror()))]
    ppermute x2, waiting for transfers between devices: 1.45 us -> 0.01 us  [layer(): recv = lax.ppermute(theirs, 'lat', lat_xor(1))]
    another operation x2 -> x0, other arithmetic: 1.42 us -> none  [layer(): own = jnp.stack([code_index, value]).astype(jnp.int16)]
  transfers between devices with their start and end apart: 24 -> 23, of which waited for: 5 -> 4; matrix products, arithmetic and copies ran while one was open for 1% -> 0% of each run, Pallas kernels for 4% -> 4%
where the time goes in v4:
time: 111 us
  blocking collectives  37.8 us (34%)
  starting transfers between devices  36.2 us (33%)
  Pallas kernels  25.8 us (23%)
  waiting for transfers between devices  10.5 us (9%)
    all_to_all x1, blocking collectives, layer(): parts = lax.all_to_all(picked, ('tgt', 'lat'), 0, 0, tiled=True)  23.4 us
    ppermute x12, starting transfers between devices, shift_z(): return lax.ppermute(x, 'lat', lat_xor(2 * d))  15.4 us
    all_to_all x1, blocking collectives, layer(): lax.all_to_all(sent, 'tgt', 0, 0, tiled=True, axis_index_groups=groups)  14.4 us
    pallas_call x2, Pallas kernels, decode(): pl.pallas_call(lambda x_ref, w_ref, m_ref, *refs: decode_kernel(part, x_r...  12.7 us
    ppermute x8, starting transfers between devices, layer(): coded = coded + [lax.ppermute(c, 'lat', lat_xor(1)) for c in coded]  12.3 us
    pallas_call x2, Pallas kernels, grads(): pl.pallas_call(lambda *refs: grads_kernel(part, *refs[:used], *refs[used...  9.57 us
    ppermute x1, waiting for transfers between devices, layer(): x.append(lax.ppermute(x[0], ('tgt', 'lat'), mirror()))  6.48 us
    ppermute x1, starting transfers between devices, layer(): x.append(lax.ppermute(x[0], ('tgt', 'lat'), mirror()))  5.57 us
  transfers between devices with their start and end apart: 23, of which 4 were waited for; matrix products, arithmetic and copies ran while one was open for 0% of the time, Pallas kernels for 4%

profile of v4, /device:TPU:1, one launch (start us, length us, event | category | flops | bytes accessed | tf_op | source)
XLA Modules:
  0.0 111.1 jit_solution(12390394116090309982)
XLA Ops:
  0.6 1.5 %codes.1 = s16[16,32,128]{2,1,0:T(8,128)(2,1)} custom-call(s32[2,16,64]{2,1,0:T(8,128)} %index_ref.1, bf16[2,16,64]{2,1,0:T(8,128)(2,1)} %value_ref.1), custom_call_target="tpu_custom_call" | custom-call | tf_op jit(solution)/shard_map/codes/pallas_call | solution.py:311
  2.1 14.4 %all_to_all.16.x_ref.refs_0_ = s16[16,32,128]{2,1,0:T(8,128)(2,1)S(1)} all-to-all(s16[16,32,128]{2,1,0:T(8,128)(2,1)} %codes.1), channel_id=1, replica_groups={{0,8,16,24,32,40,48,56,64,72,80,88,96,104,112,120},{128,136,144,152,160..., dimensions={0} | all-to-all | bytes 262144 | tf_op jit(solution)/shard_map/all_to_all | solution.py:319
  16.5 6.4 %shard_map.59 = (f32[4,32,896]{2,1,0:T(8,128)S(1)}, f32[4,32,896]{2,1,0:T(8,128)S(1)}) custom-call(s16[16,32,128]{2,1,0:T(8,128)(2,1)S(1)} %all_to_all.16.x_ref.refs_0_, bf16[4096,896]{1,0:T(8,128)(2,1)} %bitcast.4, bf16[64,896]{1,0:T(8,128)(2,1)} %m_ref.3), custom_call_target="tpu_custom_call" | custom-call | flops 3758096384 | bytes 7340032 | tf_op jit(solution)/shard_map/pallas_call | solution.py:153
  22.9 2.2 %collective-permute-start.1 = (f32[4,32,896]{2,1,0:T(8,128)S(1)}, f32[4,32,896]{2,1,0:T(8,128)S(1)}, u32[]{:S(2)}, u32[]{:S(2)}) collective-permute-start(f32[4,32,896]{2,1,0:T(8,128)S(1)} %get-tuple-element.19), channel_id=1, source_target_pairs={{0,1},{1,0},{2,3},{3,2},{4,5},{5,4},{6,7},{7,6},{8,9},{9,8},{10,11... | collective-permute-start | bytes 1376264 | tf_op jit(solution)/shard_map/ppermute | solution.py:327
  25.1 5.6 %collective-permute-start = (s16[16,32,128]{2,1,0:T(8,128)(2,1)S(1)}, s16[16,32,128]{2,1,0:T(8,128)(2,1)S(1)}, u32[]{:S(2)}, u32[]{:S(2)}) collective-permute-start(s16[16,32,128]{2,1,0:T(8,128)(2,1)S(1)} %all_to_all.16.x_ref.refs_0_), channel_id=1, source_target_pairs={{0,134},{1,135},{2,132},{3,133},{4,130},{5,131},{6,128},{7,129},{8... | collective-permute-start | bytes 393224 | tf_op jit(solution)/shard_map/ppermute | solution.py:320
  30.6 0.0 collective-permute-done.1.recv_ref
  30.6 0.0 slice-start
  30.7 0.1 shard_map.60
  30.7 6.5 %collective-permute-done.x_ref.refs_0_ = s16[16,32,128]{2,1,0:T(8,128)(2,1)S(1)} collective-permute-done((s16[16,32,128]{2,1,0:T(8,128)(2,1)S(1)}, s16[16,32,128]{2,1,0:T(8,128)(2,1)S(1)}, u32[]{:S(2)}, u32[]{:S(2)}) %collective-permute-start) | collective-permute-done | bytes 131104 | tf_op jit(solution)/shard_map/ppermute | solution.py:320
  37.2 0.0 slice-start.1
  37.2 6.4 %shard_map.61 = (f32[4,32,896]{2,1,0:T(8,128)S(1)}, f32[4,32,896]{2,1,0:T(8,128)S(1)}) custom-call(s16[16,32,128]{2,1,0:T(8,128)(2,1)S(1)} %collective-permute-done.x_ref.refs_0_, bf16[4096,896]{1,0:T(8,128)(2,1)} %bitcast.5, bf16[64,896]{1,0:T(8,128)(2,1)} %m_ref.3, s16[32,1024]{1,0:T(8,128)(2,1)S(1)} %get-tuple-element.20.refs_0_, ...), custom_call_target="tpu_custom_call" | custom-call | flops 3758096384 | bytes 7340032 | tf_op jit(solution)/shard_map/pallas_call | solution.py:153
  43.6 0.8 collective-permute-start.2
  44.4 0.0 collective-permute-start.13
  44.4 1.9 %collective-permute-start.14 = (s16[32,1024]{1,0:T(8,128)(2,1)S(1)}, s16[32,1024]{1,0:T(8,128)(2,1)S(1)}, u32[]{:S(2)}, u32[]{:S(2)}) collective-permute-start(s16[32,1024]{1,0:T(8,128)(2,1)S(1)} %get-tuple-element.21.refs_1_), channel_id=1, source_target_pairs={{0,4},{1,5},{2,6},{3,7},{4,0},{5,1},{6,2},{7,3},{8,12},{9,13},{10,... | collective-permute-start | bytes 196616 | tf_op jit(solution)/shard_map/ppermute | solution.py:304
  46.3 1.6 %collective-permute-start.15 = (s16[32,1024]{1,0:T(8,128)(2,1)S(1)}, s16[32,1024]{1,0:T(8,128)(2,1)S(1)}, u32[]{:S(2)}, u32[]{:S(2)}) collective-permute-start(s16[32,1024]{1,0:T(8,128)(2,1)S(1)} %get-tuple-element.22.refs_2_), channel_id=1, source_target_pairs={{0,6},{1,7},{2,4},{3,5},{4,2},{5,3},{6,0},{7,1},{8,14},{9,15},{10,... | collective-permute-start | bytes 196616 | tf_op jit(solution)/shard_map/ppermute | solution.py:304
  47.9 0.0 collective-permute-done.13.a_ref
  47.9 0.8 collective-permute-done.14.b_ref
  48.7 2.5 %collective-permute-done.15.c_ref = s16[32,1024]{1,0:T(8,128)(2,1)S(1)} collective-permute-done((s16[32,1024]{1,0:T(8,128)(2,1)S(1)}, s16[32,1024]{1,0:T(8,128)(2,1)S(1)}, u32[]{:S(2)}, u32[]{:S(2)}) %collective-permute-start.15) | collective-permute-done | bytes 65568 | tf_op jit(solution)/shard_map/ppermute | solution.py:304
  51.2 0.1 shard_map.64.refs_1_
  51.3 2.3 %collective-permute-start.16 = (s16[32,1024]{1,0:T(8,128)(2,1)S(1)}, s16[32,1024]{1,0:T(8,128)(2,1)S(1)}, u32[]{:S(2)}, u32[]{:S(2)}) collective-permute-start(s16[32,1024]{1,0:T(8,128)(2,1)S(1)} %shard_map.64.refs_1_), channel_id=1, source_target_pairs={{0,2},{1,3},{2,0},{3,1},{4,6},{5,7},{6,4},{7,5},{8,10},{9,11},{10,... | collective-permute-start | bytes 196616 | tf_op jit(solution)/shard_map/ppermute | solution.py:304
  53.6 0.5 collective-permute-start.17
  54.1 0.0 collective-permute-done.2.recv_ref
  54.1 0.1 shard_map.62
  54.2 1.5 %collective-permute-start.3 = (s16[32,1024]{1,0:T(8,128)(2,1)S(1)}, s16[32,1024]{1,0:T(8,128)(2,1)S(1)}, u32[]{:S(2)}, u32[]{:S(2)}) collective-permute-start(s16[32,1024]{1,0:T(8,128)(2,1)S(1)} %get-tuple-element.26), channel_id=1, source_target_pairs={{0,2},{1,3},{2,0},{3,1},{4,6},{5,7},{6,4},{7,5},{8,10},{9,11},{10,... | collective-permute-start | bytes 196616 | tf_op jit(solution)/shard_map/ppermute | solution.py:304
  55.7 0.6 collective-permute-start.4
  56.2 1.6 %collective-permute-start.5 = (s16[32,1024]{1,0:T(8,128)(2,1)S(1)}, s16[32,1024]{1,0:T(8,128)(2,1)S(1)}, u32[]{:S(2)}, u32[]{:S(2)}) collective-permute-start(s16[32,1024]{1,0:T(8,128)(2,1)S(1)} %get-tuple-element.28), channel_id=1, source_target_pairs={{0,6},{1,7},{2,4},{3,5},{4,2},{5,3},{6,0},{7,1},{8,14},{9,15},{10,... | collective-permute-start | bytes 196616 | tf_op jit(solution)/shard_map/ppermute | solution.py:304
  57.9 0.0 collective-permute-done.16.refs_2_
  57.9 1.6 %collective-permute-start.18 = (s16[32,1024]{1,0:T(8,128)(2,1)S(1)}, s16[32,1024]{1,0:T(8,128)(2,1)S(1)}, u32[]{:S(2)}, u32[]{:S(2)}) collective-permute-start(s16[32,1024]{1,0:T(8,128)(2,1)S(1)} %shard_map.64.refs_1_), channel_id=1, source_target_pairs={{0,6},{1,7},{2,4},{3,5},{4,2},{5,3},{6,0},{7,1},{8,14},{9,15},{10,... | collective-permute-start | bytes 196616 | tf_op jit(solution)/shard_map/ppermute | solution.py:304
  59.5 0.0 collective-permute-done.17.refs_3_
  59.5 4.6 %collective-permute-start.19 = (s16[32,1024]{1,0:T(8,128)(2,1)S(1)}, s16[32,1024]{1,0:T(8,128)(2,1)S(1)}, u32[]{:S(2)}, u32[]{:S(2)}) collective-permute-start(s16[32,1024]{1,0:T(8,128)(2,1)S(1)} %shard_map.64.refs_1_), channel_id=1, source_target_pairs={{0,1},{1,0},{2,3},{3,2},{4,5},{5,4},{6,7},{7,6},{8,9},{9,8},{10,11... | collective-permute-start | bytes 196616 | tf_op jit(solution)/shard_map/ppermute | solution.py:337
  64.1 0.0 collective-permute-done.3.a_ref
  64.1 0.0 collective-permute-start.20
  64.1 0.8 collective-permute-done.4.b_ref
  64.8 2.0 %collective-permute-start.21 = (s16[32,1024]{1,0:T(8,128)(2,1)S(1)}, s16[32,1024]{1,0:T(8,128)(2,1)S(1)}, u32[]{:S(2)}, u32[]{:S(2)}) collective-permute-start(s16[32,1024]{1,0:T(8,128)(2,1)S(1)} %collective-permute-done.17.refs_3_), channel_id=1, source_target_pairs={{0,1},{1,0},{2,3},{3,2},{4,5},{5,4},{6,7},{7,6},{8,9},{9,8},{10,11... | collective-permute-start | bytes 196616 | tf_op jit(solution)/shard_map/ppermute | solution.py:337
  66.9 0.0 collective-permute-done.5.c_ref
  66.9 0.1 shard_map.63.refs_10_.refs_1_
  67.0 0.4 collective-permute-start.6
  67.4 0.0 collective-permute-done.18.refs_4_
  67.4 1.7 %collective-permute-start.7 = (s16[32,1024]{1,0:T(8,128)(2,1)S(1)}, s16[32,1024]{1,0:T(8,128)(2,1)S(1)}, u32[]{:S(2)}, u32[]{:S(2)}) collective-permute-start(s16[32,1024]{1,0:T(8,128)(2,1)S(1)} %shard_map.63.refs_10_.refs_1_), channel_id=1, source_target_pairs={{0,4},{1,5},{2,6},{3,7},{4,0},{5,1},{6,2},{7,3},{8,12},{9,13},{10,... | collective-permute-start | bytes 196616 | tf_op jit(solution)/shard_map/ppermute | solution.py:304
  69.1 0.0 collective-permute-done.19.refs_5_
  69.1 1.6 %collective-permute-start.8 = (s16[32,1024]{1,0:T(8,128)(2,1)S(1)}, s16[32,1024]{1,0:T(8,128)(2,1)S(1)}, u32[]{:S(2)}, u32[]{:S(2)}) collective-permute-start(s16[32,1024]{1,0:T(8,128)(2,1)S(1)} %shard_map.63.refs_10_.refs_1_), channel_id=1, source_target_pairs={{0,6},{1,7},{2,4},{3,5},{4,2},{5,3},{6,0},{7,1},{8,14},{9,15},{10,... | collective-permute-start | bytes 196616 | tf_op jit(solution)/shard_map/ppermute | solution.py:304
  70.7 0.0 collective-permute-done.20.refs_6_
  70.7 1.4 %collective-permute-start.22 = (s16[32,1024]{1,0:T(8,128)(2,1)S(1)}, s16[32,1024]{1,0:T(8,128)(2,1)S(1)}, u32[]{:S(2)}, u32[]{:S(2)}) collective-permute-start(s16[32,1024]{1,0:T(8,128)(2,1)S(1)} %collective-permute-done.18.refs_4_), channel_id=1, source_target_pairs={{0,1},{1,0},{2,3},{3,2},{4,5},{5,4},{6,7},{7,6},{8,9},{9,8},{10,11... | collective-permute-start | bytes 196616 | tf_op jit(solution)/shard_map/ppermute | solution.py:337
  72.2 0.0 collective-permute-done.21.refs_7_
  72.2 0.1 collective-permute-start.9
  72.2 0.0 collective-permute-done.6.refs_2_
  72.2 0.4 collective-permute-start.10
  72.7 0.0 collective-permute-done.7.refs_3_
  72.7 3.7 %collective-permute-start.11 = (s16[32,1024]{1,0:T(8,128)(2,1)S(1)}, s16[32,1024]{1,0:T(8,128)(2,1)S(1)}, u32[]{:S(2)}, u32[]{:S(2)}) collective-permute-start(s16[32,1024]{1,0:T(8,128)(2,1)S(1)} %collective-permute-done.7.refs_3_), channel_id=1, source_target_pairs={{0,1},{1,0},{2,3},{3,2},{4,5},{5,4},{6,7},{7,6},{8,9},{9,8},{10,11... | collective-permute-start | bytes 196616 | tf_op jit(solution)/shard_map/ppermute | solution.py:337
  76.4 0.0 collective-permute-done.8.refs_4_
  76.4 0.0 collective-permute-start.12
  76.4 0.0 collective-permute-done.22.refs_8_
  76.4 0.0 slice-done
  76.4 0.0 slice-done.1
  76.4 4.5 %shard_map.65 = (f32[64,896]{1,0:T(8,128)S(1)}, f32[256,128]{1,0:T(8,128)S(1)}) custom-call(s16[16,32,128]{2,1,0:T(8,128)(2,1)S(1)} %all_to_all.16.x_ref.refs_0_, s16[32,1024]{1,0:T(8,128)(2,1)S(1)} %shard_map.64.refs_1_, s16[32,1024]{1,0:T(8,128)(2,1)S(1)} %collective-permute-done.16.refs_2_, s16[32,1024]{1,0:T(8,128)(2,1)S(1)} %collective-permute-done.17.refs_3_, ...), custom_call_target="tpu_custom_call" | custom-call | flops 3758096384 | bytes 7340032 | tf_op jit(solution)/shard_map/pallas_call | solution.py:265
  80.9 0.0 collective-permute-done.9.refs_5_
  80.9 0.0 collective-permute-done.10.refs_6_
  80.9 0.0 collective-permute-done.11.refs_7_
  80.9 0.0 collective-permute-done.12.refs_8_
  80.9 5.1 %shard_map.66 = (f32[64,896]{1,0:T(8,128)}, f32[512,128]{1,0:T(8,128)S(1)}) custom-call(s16[16,32,128]{2,1,0:T(8,128)(2,1)S(1)} %collective-permute-done.x_ref.refs_0_, s16[32,1024]{1,0:T(8,128)(2,1)S(1)} %shard_map.63.refs_10_.refs_1_, s16[32,1024]{1,0:T(8,128)(2,1)S(1)} %collective-permute-done.6.refs_2_, ...), custom_call_target="tpu_custom_call" | custom-call | flops 3758096384 | bytes 7340032 | tf_op jit(solution)/shard_map/pallas_call | solution.py:265
  86.0 23.4 %all_to_all.17 = f32[256,2,128]{2,1,0:T(2,128)} all-to-all(f32[256,2,128]{2,1,0:T(2,128)S(1)} %bitcast.3), channel_id=1, replica_groups=mesh['tgt'=32,'lat'=8] {'tgt','lat'}, dimensions={0} | all-to-all | bytes 524288 | tf_op jit(solution)/shard_map/all_to_all | solution.py:341
  109.4 1.7 %total.1 = f32[2,2,64]{2,1,0:T(2,128)} custom-call(f32[512,128]{1,0:T(8,128)} %bitcast.10), custom_call_target="tpu_custom_call" | custom-call | tf_op jit(solution)/shard_map/total/pallas_call | solution.py:342
  (1 shorter events, 0.0 us)
Async XLA Ops:
  22.9 7.7 %collective-permute-start.1 = (f32[4,32,896]{2,1,0:T(8,128)S(1)}, f32[4,32,896]{2,1,0:T(8,128)S(1)}, u32[]{:S(2)}, u32[]{:S(2)}) collective-permute-start(f32[4,32,896]{2,1,0:T(8,128)S(1)} %get-tuple-element.19), channel_id=1, source_target_pairs={{0,1},{1,0},{2,3},{3,2},{4,5},{5,4},{6,7},{7,6},{8,9},{9,8},{10,11... | collective-permute-start | bytes 1376264 | tf_op jit(solution)/shard_map/ppermute | solution.py:327
  25.1 12.1 %collective-permute-start = (s16[16,32,128]{2,1,0:T(8,128)(2,1)S(1)}, s16[16,32,128]{2,1,0:T(8,128)(2,1)S(1)}, u32[]{:S(2)}, u32[]{:S(2)}) collective-permute-start(s16[16,32,128]{2,1,0:T(8,128)(2,1)S(1)} %all_to_all.16.x_ref.refs_0_), channel_id=1, source_target_pairs={{0,134},{1,135},{2,132},{3,133},{4,130},{5,131},{6,128},{7,129},{8... | collective-permute-start | bytes 393224 | tf_op jit(solution)/shard_map/ppermute | solution.py:320
  30.6 45.7 %slice-start = ((s8[7340032]{0:T(1024)(128)(4,1)}), s8[4194304]{0:T(1024)(128)(4,1)S(1)}, s32[]{:S(2)}) async-start(s8[7340032]{0:T(1024)(128)(4,1)} %bitcast.6), calls=%async_computation.2 | async-start | bytes 8388608
  37.2 39.2 %slice-start.1 = ((s8[7340032]{0:T(1024)(128)(4,1)}), s8[3145728]{0:T(1024)(128)(4,1)S(1)}, s32[]{:S(2)}) async-start(s8[7340032]{0:T(1024)(128)(4,1)} %bitcast.6), calls=%async_computation.3 | async-start | bytes 6291456
  43.6 10.5 %collective-permute-start.2 = (f32[4,32,896]{2,1,0:T(8,128)S(1)}, f32[4,32,896]{2,1,0:T(8,128)S(1)}, u32[]{:S(2)}, u32[]{:S(2)}) collective-permute-start(f32[4,32,896]{2,1,0:T(8,128)S(1)} %get-tuple-element.24), channel_id=1, source_target_pairs={{0,1},{1,0},{2,3},{3,2},{4,5},{5,4},{6,7},{7,6},{8,9},{9,8},{10,11... | collective-permute-start | bytes 1376264 | tf_op jit(solution)/shard_map/ppermute | solution.py:327
  44.4 3.6 %collective-permute-start.13 = (s16[32,1024]{1,0:T(8,128)(2,1)S(1)}, s16[32,1024]{1,0:T(8,128)(2,1)S(1)}, u32[]{:S(2)}, u32[]{:S(2)}) collective-permute-start(s16[32,1024]{1,0:T(8,128)(2,1)S(1)} %get-tuple-element.20.refs_0_), channel_id=1, source_target_pairs={{0,2},{1,3},{2,0},{3,1},{4,6},{5,7},{6,4},{7,5},{8,10},{9,11},{10,... | collective-permute-start | bytes 196616 | tf_op jit(solution)/shard_map/ppermute | solution.py:304
  44.4 4.3 %collective-permute-start.14 = (s16[32,1024]{1,0:T(8,128)(2,1)S(1)}, s16[32,1024]{1,0:T(8,128)(2,1)S(1)}, u32[]{:S(2)}, u32[]{:S(2)}) collective-permute-start(s16[32,1024]{1,0:T(8,128)(2,1)S(1)} %get-tuple-element.21.refs_1_), channel_id=1, source_target_pairs={{0,4},{1,5},{2,6},{3,7},{4,0},{5,1},{6,2},{7,3},{8,12},{9,13},{10,... | collective-permute-start | bytes 196616 | tf_op jit(solution)/shard_map/ppermute | solution.py:304
  46.3 4.9 %collective-permute-start.15 = (s16[32,1024]{1,0:T(8,128)(2,1)S(1)}, s16[32,1024]{1,0:T(8,128)(2,1)S(1)}, u32[]{:S(2)}, u32[]{:S(2)}) collective-permute-start(s16[32,1024]{1,0:T(8,128)(2,1)S(1)} %get-tuple-element.22.refs_2_), channel_id=1, source_target_pairs={{0,6},{1,7},{2,4},{3,5},{4,2},{5,3},{6,0},{7,1},{8,14},{9,15},{10,... | collective-permute-start | bytes 196616 | tf_op jit(solution)/shard_map/ppermute | solution.py:304
  51.3 6.6 %collective-permute-start.16 = (s16[32,1024]{1,0:T(8,128)(2,1)S(1)}, s16[32,1024]{1,0:T(8,128)(2,1)S(1)}, u32[]{:S(2)}, u32[]{:S(2)}) collective-permute-start(s16[32,1024]{1,0:T(8,128)(2,1)S(1)} %shard_map.64.refs_1_), channel_id=1, source_target_pairs={{0,2},{1,3},{2,0},{3,1},{4,6},{5,7},{6,4},{7,5},{8,10},{9,11},{10,... | collective-permute-start | bytes 196616 | tf_op jit(solution)/shard_map/ppermute | solution.py:304
  53.6 5.9 %collective-permute-start.17 = (s16[32,1024]{1,0:T(8,128)(2,1)S(1)}, s16[32,1024]{1,0:T(8,128)(2,1)S(1)}, u32[]{:S(2)}, u32[]{:S(2)}) collective-permute-start(s16[32,1024]{1,0:T(8,128)(2,1)S(1)} %shard_map.64.refs_1_), channel_id=1, source_target_pairs={{0,4},{1,5},{2,6},{3,7},{4,0},{5,1},{6,2},{7,3},{8,12},{9,13},{10,... | collective-permute-start | bytes 196616 | tf_op jit(solution)/shard_map/ppermute | solution.py:304
  54.2 9.9 %collective-permute-start.3 = (s16[32,1024]{1,0:T(8,128)(2,1)S(1)}, s16[32,1024]{1,0:T(8,128)(2,1)S(1)}, u32[]{:S(2)}, u32[]{:S(2)}) collective-permute-start(s16[32,1024]{1,0:T(8,128)(2,1)S(1)} %get-tuple-element.26), channel_id=1, source_target_pairs={{0,2},{1,3},{2,0},{3,1},{4,6},{5,7},{6,4},{7,5},{8,10},{9,11},{10,... | collective-permute-start | bytes 196616 | tf_op jit(solution)/shard_map/ppermute | solution.py:304
  55.7 9.2 %collective-permute-start.4 = (s16[32,1024]{1,0:T(8,128)(2,1)S(1)}, s16[32,1024]{1,0:T(8,128)(2,1)S(1)}, u32[]{:S(2)}, u32[]{:S(2)}) collective-permute-start(s16[32,1024]{1,0:T(8,128)(2,1)S(1)} %get-tuple-element.27), channel_id=1, source_target_pairs={{0,4},{1,5},{2,6},{3,7},{4,0},{5,1},{6,2},{7,3},{8,12},{9,13},{10,... | collective-permute-start | bytes 196616 | tf_op jit(solution)/shard_map/ppermute | solution.py:304
  56.2 10.6 %collective-permute-start.5 = (s16[32,1024]{1,0:T(8,128)(2,1)S(1)}, s16[32,1024]{1,0:T(8,128)(2,1)S(1)}, u32[]{:S(2)}, u32[]{:S(2)}) collective-permute-start(s16[32,1024]{1,0:T(8,128)(2,1)S(1)} %get-tuple-element.28), channel_id=1, source_target_pairs={{0,6},{1,7},{2,4},{3,5},{4,2},{5,3},{6,0},{7,1},{8,14},{9,15},{10,... | collective-permute-start | bytes 196616 | tf_op jit(solution)/shard_map/ppermute | solution.py:304
  57.9 9.5 %collective-permute-start.18 = (s16[32,1024]{1,0:T(8,128)(2,1)S(1)}, s16[32,1024]{1,0:T(8,128)(2,1)S(1)}, u32[]{:S(2)}, u32[]{:S(2)}) collective-permute-start(s16[32,1024]{1,0:T(8,128)(2,1)S(1)} %shard_map.64.refs_1_), channel_id=1, source_target_pairs={{0,6},{1,7},{2,4},{3,5},{4,2},{5,3},{6,0},{7,1},{8,14},{9,15},{10,... | collective-permute-start | bytes 196616 | tf_op jit(solution)/shard_map/ppermute | solution.py:304
  59.5 9.6 %collective-permute-start.19 = (s16[32,1024]{1,0:T(8,128)(2,1)S(1)}, s16[32,1024]{1,0:T(8,128)(2,1)S(1)}, u32[]{:S(2)}, u32[]{:S(2)}) collective-permute-start(s16[32,1024]{1,0:T(8,128)(2,1)S(1)} %shard_map.64.refs_1_), channel_id=1, source_target_pairs={{0,1},{1,0},{2,3},{3,2},{4,5},{5,4},{6,7},{7,6},{8,9},{9,8},{10,11... | collective-permute-start | bytes 196616 | tf_op jit(solution)/shard_map/ppermute | solution.py:337
  64.1 6.6 %collective-permute-start.20 = (s16[32,1024]{1,0:T(8,128)(2,1)S(1)}, s16[32,1024]{1,0:T(8,128)(2,1)S(1)}, u32[]{:S(2)}, u32[]{:S(2)}) collective-permute-start(s16[32,1024]{1,0:T(8,128)(2,1)S(1)} %collective-permute-done.16.refs_2_), channel_id=1, source_target_pairs={{0,1},{1,0},{2,3},{3,2},{4,5},{5,4},{6,7},{7,6},{8,9},{9,8},{10,11... | collective-permute-start | bytes 196616 | tf_op jit(solution)/shard_map/ppermute | solution.py:337
  64.8 7.3 %collective-permute-start.21 = (s16[32,1024]{1,0:T(8,128)(2,1)S(1)}, s16[32,1024]{1,0:T(8,128)(2,1)S(1)}, u32[]{:S(2)}, u32[]{:S(2)}) collective-permute-start(s16[32,1024]{1,0:T(8,128)(2,1)S(1)} %collective-permute-done.17.refs_3_), channel_id=1, source_target_pairs={{0,1},{1,0},{2,3},{3,2},{4,5},{5,4},{6,7},{7,6},{8,9},{9,8},{10,11... | collective-permute-start | bytes 196616 | tf_op jit(solution)/shard_map/ppermute | solution.py:337
  67.0 5.3 %collective-permute-start.6 = (s16[32,1024]{1,0:T(8,128)(2,1)S(1)}, s16[32,1024]{1,0:T(8,128)(2,1)S(1)}, u32[]{:S(2)}, u32[]{:S(2)}) collective-permute-start(s16[32,1024]{1,0:T(8,128)(2,1)S(1)} %shard_map.63.refs_10_.refs_1_), channel_id=1, source_target_pairs={{0,2},{1,3},{2,0},{3,1},{4,6},{5,7},{6,4},{7,5},{8,10},{9,11},{10,... | collective-permute-start | bytes 196616 | tf_op jit(solution)/shard_map/ppermute | solution.py:304
  67.4 5.3 %collective-permute-start.7 = (s16[32,1024]{1,0:T(8,128)(2,1)S(1)}, s16[32,1024]{1,0:T(8,128)(2,1)S(1)}, u32[]{:S(2)}, u32[]{:S(2)}) collective-permute-start(s16[32,1024]{1,0:T(8,128)(2,1)S(1)} %shard_map.63.refs_10_.refs_1_), channel_id=1, source_target_pairs={{0,4},{1,5},{2,6},{3,7},{4,0},{5,1},{6,2},{7,3},{8,12},{9,13},{10,... | collective-permute-start | bytes 196616 | tf_op jit(solution)/shard_map/ppermute | solution.py:304
  69.1 7.3 %collective-permute-start.8 = (s16[32,1024]{1,0:T(8,128)(2,1)S(1)}, s16[32,1024]{1,0:T(8,128)(2,1)S(1)}, u32[]{:S(2)}, u32[]{:S(2)}) collective-permute-start(s16[32,1024]{1,0:T(8,128)(2,1)S(1)} %shard_map.63.refs_10_.refs_1_), channel_id=1, source_target_pairs={{0,6},{1,7},{2,4},{3,5},{4,2},{5,3},{6,0},{7,1},{8,14},{9,15},{10,... | collective-permute-start | bytes 196616 | tf_op jit(solution)/shard_map/ppermute | solution.py:304
  70.7 5.7 %collective-permute-start.22 = (s16[32,1024]{1,0:T(8,128)(2,1)S(1)}, s16[32,1024]{1,0:T(8,128)(2,1)S(1)}, u32[]{:S(2)}, u32[]{:S(2)}) collective-permute-start(s16[32,1024]{1,0:T(8,128)(2,1)S(1)} %collective-permute-done.18.refs_4_), channel_id=1, source_target_pairs={{0,1},{1,0},{2,3},{3,2},{4,5},{5,4},{6,7},{7,6},{8,9},{9,8},{10,11... | collective-permute-start | bytes 196616 | tf_op jit(solution)/shard_map/ppermute | solution.py:337
  72.2 8.7 %collective-permute-start.9 = (s16[32,1024]{1,0:T(8,128)(2,1)S(1)}, s16[32,1024]{1,0:T(8,128)(2,1)S(1)}, u32[]{:S(2)}, u32[]{:S(2)}) collective-permute-start(s16[32,1024]{1,0:T(8,128)(2,1)S(1)} %shard_map.63.refs_10_.refs_1_), channel_id=1, source_target_pairs={{0,1},{1,0},{2,3},{3,2},{4,5},{5,4},{6,7},{7,6},{8,9},{9,8},{10,11... | collective-permute-start | bytes 196616 | tf_op jit(solution)/shard_map/ppermute | solution.py:337
  72.2 8.6 %collective-permute-start.10 = (s16[32,1024]{1,0:T(8,128)(2,1)S(1)}, s16[32,1024]{1,0:T(8,128)(2,1)S(1)}, u32[]{:S(2)}, u32[]{:S(2)}) collective-permute-start(s16[32,1024]{1,0:T(8,128)(2,1)S(1)} %collective-permute-done.6.refs_2_), channel_id=1, source_target_pairs={{0,1},{1,0},{2,3},{3,2},{4,5},{5,4},{6,7},{7,6},{8,9},{9,8},{10,11... | collective-permute-start | bytes 196616 | tf_op jit(solution)/shard_map/ppermute | solution.py:337
  72.7 8.2 %collective-permute-start.11 = (s16[32,1024]{1,0:T(8,128)(2,1)S(1)}, s16[32,1024]{1,0:T(8,128)(2,1)S(1)}, u32[]{:S(2)}, u32[]{:S(2)}) collective-permute-start(s16[32,1024]{1,0:T(8,128)(2,1)S(1)} %collective-permute-done.7.refs_3_), channel_id=1, source_target_pairs={{0,1},{1,0},{2,3},{3,2},{4,5},{5,4},{6,7},{7,6},{8,9},{9,8},{10,11... | collective-permute-start | bytes 196616 | tf_op jit(solution)/shard_map/ppermute | solution.py:337
  76.4 4.5 %collective-permute-start.12 = (s16[32,1024]{1,0:T(8,128)(2,1)S(1)}, s16[32,1024]{1,0:T(8,128)(2,1)S(1)}, u32[]{:S(2)}, u32[]{:S(2)}) collective-permute-start(s16[32,1024]{1,0:T(8,128)(2,1)S(1)} %collective-permute-done.8.refs_4_), channel_id=1, source_target_pairs={{0,1},{1,0},{2,3},{3,2},{4,5},{5,4},{6,7},{7,6},{8,9},{9,8},{10,11... | collective-permute-start | bytes 196616 | tf_op jit(solution)/shard_map/ppermute | solution.py:337

commit v5 on v4

--- a/solution.py
+++ b/solution.py
@@ -207,7 +207,7 @@
     coded = refs[:8]
     w_ref = refs[8]
     first = refs[9 : 9 + 2 * part]
-    error_ref, out_ref, err_ref, full_ref = refs[9 + 2 * part :]
+    error_ref, out_ref, err_ref, full_ref, rows_ref, sem = refs[9 + 2 * part :]
     steps = 4
     rows_w = w_ref.shape[0] // steps
     cols = w_ref.shape[1]
@@ -225,6 +225,12 @@
         high = e.astype(jnp.bfloat16)
         err_ref[pl.ds(row, group), :cols] = high
         err_ref[pl.ds(row, group), cols:] = (e - high.astype(jnp.float32)).astype(jnp.bfloat16)
+    own, in_part = own_rows(part)
+    rows_ref[...] = full_ref[pl.ds(own, 64), :]
+    if part == 1:
+        rows_ref[...] = jnp.where(in_part, rows_ref[...], first[0][...])
+    error_copy = pltpu.make_async_copy(rows_ref, error_ref, sem)
+    error_copy.start()
     chunks = w_ref.shape[0] // LO
     his = chunks // 2
     width = his * LO
@@ -246,16 +252,13 @@
         for j in range(rows_w // LO):
             found = jnp.take_along_axis(grads[:, j * LO : (j + 1) * LO], lo, axis=1)
             picked = jnp.where(key == i * (rows_w // LO) + j, found, picked)
-    own, in_part = own_rows(part)
-    error = full_ref[pl.ds(own, 64), :]
     if part == 0:
-        error_ref[...] = error
         out_ref[...] = picked
     else:
-        error_ref[...] = jnp.where(in_part, error, first[0][...])
         zh = lax.axis_index("tgt") // 16
         out_ref[pl.ds(pl.multiple_of(zh * tokens, tokens), tokens), :] = first[1][...]
         out_ref[pl.ds(pl.multiple_of((1 - zh) * tokens, tokens), tokens), :] = picked
+    error_copy.wait()
 
 
 def grads(x, coded, w, part, first, after):
@@ -269,10 +272,12 @@
             jax.ShapeDtypeStruct((tokens * (part + 1), LO), jnp.float32),
         ),
         in_specs=[VMEM_SPEC] * used + [ANY_SPEC] * len(after),
-        out_specs=(VMEM_SPEC,) * 2,
+        out_specs=(ANY_SPEC, VMEM_SPEC),
         scratch_shapes=[
             pltpu.VMEM((tokens, 2 * cols), jnp.bfloat16),
             pltpu.VMEM((tokens, cols), jnp.float32),
+            pltpu.VMEM((64, cols), jnp.float32),
+            pltpu.SemaphoreType.DMA,
         ],
         compiler_params=PARAMS,
         cost_estimate=pl.CostEstimate(
@@ -287,17 +292,6 @@
     both = jnp.concatenate([index, value.astype(jnp.int32)], axis=0).astype(jnp.int16)
     for i in range(out_ref.shape[0]):
         out_ref[i] = both
-
-
-def total_kernel(parts_ref, out_ref):
-    eight = parts_ref[0:8, :]
-    for i in range(1, parts_ref.shape[0] // 8):
-        eight = eight + parts_ref[8 * i : 8 * i + 8, :]
-    for j in range(2):
-        row = eight[j : j + 1] + eight[j + 2 : j + 3] + eight[j + 4 : j + 5] + eight[j + 6 : j + 7]
-        row = row * (1.0 / TARGETS)
-        for source in range(2):
-            out_ref[source, j : j + 1, :] = row[:, source * 64 : (source + 1) * 64]
 
 
 def shift_z(x, d):
@@ -339,14 +333,8 @@
         done = grads(x[part], coded, w, part, done, after)
     error, picked = done
     parts = lax.all_to_all(picked, ("tgt", "lat"), 0, 0, tiled=True)
-    total = pl.pallas_call(
-        total_kernel,
-        out_shape=jax.ShapeDtypeStruct((sources, 2, 64), jnp.float32),
-        in_specs=[VMEM_SPEC],
-        out_specs=VMEM_SPEC,
-        name="total",
-    )(parts)
-    return error, total
+    total = jnp.sum(parts.reshape(256, 2, sources, 64), axis=0)
+    return error, jnp.transpose(total, (1, 0, 2)) / TARGETS
 
 
 def solution(mesh):

time: 111 us -> 111 us (level)
  Pallas kernels: 25.8 us -> 24.5 us
    pallas_call x1 -> x0, Pallas kernels: 1.67 us -> none  [layer(): pl.pallas_call(total_kernel, out_shape=jax.ShapeDtypeStruct((sources, 2,...]
  transfers between devices with their start and end apart: 23 -> 23, of which waited for: 4 -> 4; matrix products, arithmetic and copies ran while one was open for 0% -> 0% of each run, Pallas kernels for 4% -> 5%
where the time goes in v5:
time: 111 us; the launch traced here: 110 us
  blocking collectives  37.4 us (34%)
  starting transfers between devices  36.2 us (33%)
  Pallas kernels  24.5 us (22%)
  waiting for transfers between devices  10.5 us (9%)
    all_to_all x1, blocking collectives, layer(): parts = lax.all_to_all(picked, ('tgt', 'lat'), 0, 0, tiled=True)  23 us
    ppermute x12, starting transfers between devices, shift_z(): return lax.ppermute(x, 'lat', lat_xor(2 * d))  15.4 us
    all_to_all x1, blocking collectives, layer(): lax.all_to_all(sent, 'tgt', 0, 0, tiled=True, axis_index_groups=groups)  14.4 us
    pallas_call x2, Pallas kernels, decode(): pl.pallas_call(lambda x_ref, w_ref, m_ref, *refs: decode_kernel(part, x_r...  12.7 us
    ppermute x8, starting transfers between devices, layer(): coded = coded + [lax.ppermute(c, 'lat', lat_xor(1)) for c in coded]  12.3 us
    pallas_call x2, Pallas kernels, grads(): pl.pallas_call(lambda *refs: grads_kernel(part, *refs[:used], *refs[used...  9.94 us
    ppermute x1, waiting for transfers between devices, layer(): x.append(lax.ppermute(x[0], ('tgt', 'lat'), mirror()))  6.48 us
    ppermute x1, starting transfers between devices, layer(): x.append(lax.ppermute(x[0], ('tgt', 'lat'), mirror()))  5.57 us
  transfers between devices with their start and end apart: 23, of which 4 were waited for; matrix products, arithmetic and copies ran while one was open for 0% of the time, Pallas kernels for 5%

profile of v5, /device:TPU:1, one launch (start us, length us, event | category | flops | bytes accessed | tf_op | source)
XLA Modules:
  0.0 110.4 jit_solution(15221186975588546000)
XLA Ops:
  0.6 1.5 %codes.1 = s16[16,32,128]{2,1,0:T(8,128)(2,1)} custom-call(s32[2,16,64]{2,1,0:T(8,128)} %index_ref.1, bf16[2,16,64]{2,1,0:T(8,128)(2,1)} %value_ref.1), custom_call_target="tpu_custom_call" | custom-call | tf_op jit(solution)/shard_map/codes/pallas_call | solution.py:305
  2.1 14.4 %all_to_all.14.x_ref.refs_0_ = s16[16,32,128]{2,1,0:T(8,128)(2,1)S(1)} all-to-all(s16[16,32,128]{2,1,0:T(8,128)(2,1)} %codes.1), channel_id=1, replica_groups={{0,8,16,24,32,40,48,56,64,72,80,88,96,104,112,120},{128,136,144,152,160..., dimensions={0} | all-to-all | bytes 262144 | tf_op jit(solution)/shard_map/all_to_all | solution.py:313
  16.5 6.4 %shard_map.59 = (f32[4,32,896]{2,1,0:T(8,128)S(1)}, f32[4,32,896]{2,1,0:T(8,128)S(1)}) custom-call(s16[16,32,128]{2,1,0:T(8,128)(2,1)S(1)} %all_to_all.14.x_ref.refs_0_, bf16[4096,896]{1,0:T(8,128)(2,1)} %bitcast.4, bf16[64,896]{1,0:T(8,128)(2,1)} %m_ref.3), custom_call_target="tpu_custom_call" | custom-call | flops 3758096384 | bytes 7340032 | tf_op jit(solution)/shard_map/pallas_call | solution.py:153
  22.9 2.2 %collective-permute-start.1 = (f32[4,32,896]{2,1,0:T(8,128)S(1)}, f32[4,32,896]{2,1,0:T(8,128)S(1)}, u32[]{:S(2)}, u32[]{:S(2)}) collective-permute-start(f32[4,32,896]{2,1,0:T(8,128)S(1)} %get-tuple-element.19), channel_id=1, source_target_pairs={{0,1},{1,0},{2,3},{3,2},{4,5},{5,4},{6,7},{7,6},{8,9},{9,8},{10,11... | collective-permute-start | bytes 1376264 | tf_op jit(solution)/shard_map/ppermute | solution.py:321
  25.1 5.6 %collective-permute-start = (s16[16,32,128]{2,1,0:T(8,128)(2,1)S(1)}, s16[16,32,128]{2,1,0:T(8,128)(2,1)S(1)}, u32[]{:S(2)}, u32[]{:S(2)}) collective-permute-start(s16[16,32,128]{2,1,0:T(8,128)(2,1)S(1)} %all_to_all.14.x_ref.refs_0_), channel_id=1, source_target_pairs={{0,134},{1,135},{2,132},{3,133},{4,130},{5,131},{6,128},{7,129},{8... | collective-permute-start | bytes 393224 | tf_op jit(solution)/shard_map/ppermute | solution.py:314
  30.6 0.0 collective-permute-done.1.recv_ref
  30.6 0.0 slice-start
  30.7 0.1 shard_map.60
  30.7 6.5 %collective-permute-done.x_ref.refs_0_ = s16[16,32,128]{2,1,0:T(8,128)(2,1)S(1)} collective-permute-done((s16[16,32,128]{2,1,0:T(8,128)(2,1)S(1)}, s16[16,32,128]{2,1,0:T(8,128)(2,1)S(1)}, u32[]{:S(2)}, u32[]{:S(2)}) %collective-permute-start) | collective-permute-done | bytes 131104 | tf_op jit(solution)/shard_map/ppermute | solution.py:314
  37.2 0.0 slice-start.1
  37.2 6.4 %shard_map.61 = (f32[4,32,896]{2,1,0:T(8,128)S(1)}, f32[4,32,896]{2,1,0:T(8,128)S(1)}) custom-call(s16[16,32,128]{2,1,0:T(8,128)(2,1)S(1)} %collective-permute-done.x_ref.refs_0_, bf16[4096,896]{1,0:T(8,128)(2,1)} %bitcast.5, bf16[64,896]{1,0:T(8,128)(2,1)} %m_ref.3, s16[32,1024]{1,0:T(8,128)(2,1)S(1)} %get-tuple-element.20.refs_0_, ...), custom_call_target="tpu_custom_call" | custom-call | flops 3758096384 | bytes 7340032 | tf_op jit(solution)/shard_map/pallas_call | solution.py:153
  43.6 0.8 collective-permute-start.2
  44.4 0.0 collective-permute-start.13
  44.4 1.9 %collective-permute-start.14 = (s16[32,1024]{1,0:T(8,128)(2,1)S(1)}, s16[32,1024]{1,0:T(8,128)(2,1)S(1)}, u32[]{:S(2)}, u32[]{:S(2)}) collective-permute-start(s16[32,1024]{1,0:T(8,128)(2,1)S(1)} %get-tuple-element.21.refs_1_), channel_id=1, source_target_pairs={{0,4},{1,5},{2,6},{3,7},{4,0},{5,1},{6,2},{7,3},{8,12},{9,13},{10,... | collective-permute-start | bytes 196616 | tf_op jit(solution)/shard_map/ppermute | solution.py:298
  46.3 1.6 %collective-permute-start.15 = (s16[32,1024]{1,0:T(8,128)(2,1)S(1)}, s16[32,1024]{1,0:T(8,128)(2,1)S(1)}, u32[]{:S(2)}, u32[]{:S(2)}) collective-permute-start(s16[32,1024]{1,0:T(8,128)(2,1)S(1)} %get-tuple-element.22.refs_2_), channel_id=1, source_target_pairs={{0,6},{1,7},{2,4},{3,5},{4,2},{5,3},{6,0},{7,1},{8,14},{9,15},{10,... | collective-permute-start | bytes 196616 | tf_op jit(solution)/shard_map/ppermute | solution.py:298
  47.9 0.0 collective-permute-done.13.a_ref
  47.9 0.8 collective-permute-done.14.b_ref
  48.7 2.5 %collective-permute-done.15.c_ref = s16[32,1024]{1,0:T(8,128)(2,1)S(1)} collective-permute-done((s16[32,1024]{1,0:T(8,128)(2,1)S(1)}, s16[32,1024]{1,0:T(8,128)(2,1)S(1)}, u32[]{:S(2)}, u32[]{:S(2)}) %collective-permute-start.15) | collective-permute-done | bytes 65568 | tf_op jit(solution)/shard_map/ppermute | solution.py:298
  51.2 0.1 shard_map.64.refs_1_
  51.3 2.3 %collective-permute-start.16 = (s16[32,1024]{1,0:T(8,128)(2,1)S(1)}, s16[32,1024]{1,0:T(8,128)(2,1)S(1)}, u32[]{:S(2)}, u32[]{:S(2)}) collective-permute-start(s16[32,1024]{1,0:T(8,128)(2,1)S(1)} %shard_map.64.refs_1_), channel_id=1, source_target_pairs={{0,2},{1,3},{2,0},{3,1},{4,6},{5,7},{6,4},{7,5},{8,10},{9,11},{10,... | collective-permute-start | bytes 196616 | tf_op jit(solution)/shard_map/ppermute | solution.py:298
  53.6 0.5 collective-permute-start.17
  54.1 0.0 collective-permute-done.2.recv_ref
  54.1 0.1 shard_map.62
  54.2 1.5 %collective-permute-start.3 = (s16[32,1024]{1,0:T(8,128)(2,1)S(1)}, s16[32,1024]{1,0:T(8,128)(2,1)S(1)}, u32[]{:S(2)}, u32[]{:S(2)}) collective-permute-start(s16[32,1024]{1,0:T(8,128)(2,1)S(1)} %get-tuple-element.26), channel_id=1, source_target_pairs={{0,2},{1,3},{2,0},{3,1},{4,6},{5,7},{6,4},{7,5},{8,10},{9,11},{10,... | collective-permute-start | bytes 196616 | tf_op jit(solution)/shard_map/ppermute | solution.py:298
  55.7 0.6 collective-permute-start.4
  56.2 1.6 %collective-permute-start.5 = (s16[32,1024]{1,0:T(8,128)(2,1)S(1)}, s16[32,1024]{1,0:T(8,128)(2,1)S(1)}, u32[]{:S(2)}, u32[]{:S(2)}) collective-permute-start(s16[32,1024]{1,0:T(8,128)(2,1)S(1)} %get-tuple-element.28), channel_id=1, source_target_pairs={{0,6},{1,7},{2,4},{3,5},{4,2},{5,3},{6,0},{7,1},{8,14},{9,15},{10,... | collective-permute-start | bytes 196616 | tf_op jit(solution)/shard_map/ppermute | solution.py:298
  57.9 0.0 collective-permute-done.16.refs_2_
  57.9 1.6 %collective-permute-start.18 = (s16[32,1024]{1,0:T(8,128)(2,1)S(1)}, s16[32,1024]{1,0:T(8,128)(2,1)S(1)}, u32[]{:S(2)}, u32[]{:S(2)}) collective-permute-start(s16[32,1024]{1,0:T(8,128)(2,1)S(1)} %shard_map.64.refs_1_), channel_id=1, source_target_pairs={{0,6},{1,7},{2,4},{3,5},{4,2},{5,3},{6,0},{7,1},{8,14},{9,15},{10,... | collective-permute-start | bytes 196616 | tf_op jit(solution)/shard_map/ppermute | solution.py:298
  59.5 0.0 collective-permute-done.17.refs_3_
  59.5 4.6 %collective-permute-start.19 = (s16[32,1024]{1,0:T(8,128)(2,1)S(1)}, s16[32,1024]{1,0:T(8,128)(2,1)S(1)}, u32[]{:S(2)}, u32[]{:S(2)}) collective-permute-start(s16[32,1024]{1,0:T(8,128)(2,1)S(1)} %shard_map.64.refs_1_), channel_id=1, source_target_pairs={{0,1},{1,0},{2,3},{3,2},{4,5},{5,4},{6,7},{7,6},{8,9},{9,8},{10,11... | collective-permute-start | bytes 196616 | tf_op jit(solution)/shard_map/ppermute | solution.py:331
  64.1 0.0 collective-permute-done.3.a_ref
  64.1 0.0 collective-permute-start.20
  64.1 0.8 collective-permute-done.4.b_ref
  64.8 2.0 %collective-permute-start.21 = (s16[32,1024]{1,0:T(8,128)(2,1)S(1)}, s16[32,1024]{1,0:T(8,128)(2,1)S(1)}, u32[]{:S(2)}, u32[]{:S(2)}) collective-permute-start(s16[32,1024]{1,0:T(8,128)(2,1)S(1)} %collective-permute-done.17.refs_3_), channel_id=1, source_target_pairs={{0,1},{1,0},{2,3},{3,2},{4,5},{5,4},{6,7},{7,6},{8,9},{9,8},{10,11... | collective-permute-start | bytes 196616 | tf_op jit(solution)/shard_map/ppermute | solution.py:331
  66.9 0.0 collective-permute-done.5.c_ref
  66.9 0.1 shard_map.63.refs_10_.refs_1_
  67.0 0.4 collective-permute-start.6
  67.4 0.0 collective-permute-done.18.refs_4_
  67.4 1.7 %collective-permute-start.7 = (s16[32,1024]{1,0:T(8,128)(2,1)S(1)}, s16[32,1024]{1,0:T(8,128)(2,1)S(1)}, u32[]{:S(2)}, u32[]{:S(2)}) collective-permute-start(s16[32,1024]{1,0:T(8,128)(2,1)S(1)} %shard_map.63.refs_10_.refs_1_), channel_id=1, source_target_pairs={{0,4},{1,5},{2,6},{3,7},{4,0},{5,1},{6,2},{7,3},{8,12},{9,13},{10,... | collective-permute-start | bytes 196616 | tf_op jit(solution)/shard_map/ppermute | solution.py:298
  69.1 0.0 collective-permute-done.19.refs_5_
  69.1 1.6 %collective-permute-start.8 = (s16[32,1024]{1,0:T(8,128)(2,1)S(1)}, s16[32,1024]{1,0:T(8,128)(2,1)S(1)}, u32[]{:S(2)}, u32[]{:S(2)}) collective-permute-start(s16[32,1024]{1,0:T(8,128)(2,1)S(1)} %shard_map.63.refs_10_.refs_1_), channel_id=1, source_target_pairs={{0,6},{1,7},{2,4},{3,5},{4,2},{5,3},{6,0},{7,1},{8,14},{9,15},{10,... | collective-permute-start | bytes 196616 | tf_op jit(solution)/shard_map/ppermute | solution.py:298
  70.7 0.0 collective-permute-done.20.refs_6_
  70.7 1.4 %collective-permute-start.22 = (s16[32,1024]{1,0:T(8,128)(2,1)S(1)}, s16[32,1024]{1,0:T(8,128)(2,1)S(1)}, u32[]{:S(2)}, u32[]{:S(2)}) collective-permute-start(s16[32,1024]{1,0:T(8,128)(2,1)S(1)} %collective-permute-done.18.refs_4_), channel_id=1, source_target_pairs={{0,1},{1,0},{2,3},{3,2},{4,5},{5,4},{6,7},{7,6},{8,9},{9,8},{10,11... | collective-permute-start | bytes 196616 | tf_op jit(solution)/shard_map/ppermute | solution.py:331
  72.2 0.0 collective-permute-done.21.refs_7_
  72.2 0.1 collective-permute-start.9
  72.2 0.0 collective-permute-done.6.refs_2_
  72.2 0.4 collective-permute-start.10
  72.7 0.0 collective-permute-done.7.refs_3_
  72.7 3.7 %collective-permute-start.11 = (s16[32,1024]{1,0:T(8,128)(2,1)S(1)}, s16[32,1024]{1,0:T(8,128)(2,1)S(1)}, u32[]{:S(2)}, u32[]{:S(2)}) collective-permute-start(s16[32,1024]{1,0:T(8,128)(2,1)S(1)} %collective-permute-done.7.refs_3_), channel_id=1, source_target_pairs={{0,1},{1,0},{2,3},{3,2},{4,5},{5,4},{6,7},{7,6},{8,9},{9,8},{10,11... | collective-permute-start | bytes 196616 | tf_op jit(solution)/shard_map/ppermute | solution.py:331
  76.4 0.0 collective-permute-done.8.refs_4_
  76.4 0.0 collective-permute-start.12
  76.4 0.0 collective-permute-done.22.refs_8_
  76.4 0.0 slice-done
  76.4 0.0 slice-done.1
  76.4 4.8 %shard_map.65 = (f32[64,896]{1,0:T(8,128)S(1)}, f32[256,128]{1,0:T(8,128)S(1)}) custom-call(s16[16,32,128]{2,1,0:T(8,128)(2,1)S(1)} %all_to_all.14.x_ref.refs_0_, s16[32,1024]{1,0:T(8,128)(2,1)S(1)} %shard_map.64.refs_1_, s16[32,1024]{1,0:T(8,128)(2,1)S(1)} %collective-permute-done.16.refs_2_, s16[32,1024]{1,0:T(8,128)(2,1)S(1)} %collective-permute-done.17.refs_3_, ...), custom_call_target="tpu_custom_call" | custom-call | flops 3758096384 | bytes 7340032 | tf_op jit(solution)/shard_map/pallas_call | solution.py:268
  81.2 0.0 collective-permute-done.9.refs_5_
  81.3 0.0 collective-permute-done.10.refs_6_
  81.3 0.0 collective-permute-done.11.refs_7_
  81.3 0.0 collective-permute-done.12.refs_8_
  81.3 5.1 %shard_map.66 = (f32[64,896]{1,0:T(8,128)}, f32[512,128]{1,0:T(8,128)S(1)}) custom-call(s16[16,32,128]{2,1,0:T(8,128)(2,1)S(1)} %collective-permute-done.x_ref.refs_0_, s16[32,1024]{1,0:T(8,128)(2,1)S(1)} %shard_map.63.refs_10_.refs_1_, s16[32,1024]{1,0:T(8,128)(2,1)S(1)} %collective-permute-done.6.refs_2_, ...), custom_call_target="tpu_custom_call" | custom-call | flops 3758096384 | bytes 7340032 | tf_op jit(solution)/shard_map/pallas_call | solution.py:268
  86.4 23.0 %all_to_all.15 = f32[256,2,128]{2,1,0:T(2,128)S(1)} all-to-all(f32[256,2,128]{2,1,0:T(2,128)S(1)} %bitcast.3), channel_id=1, replica_groups=mesh['tgt'=32,'lat'=8] {'tgt','lat'}, dimensions={0} | all-to-all | bytes 524288 | tf_op jit(solution)/shard_map/all_to_all | solution.py:335
  109.4 0.3 reduce_sum.9
  109.7 0.1 div.12
  109.8 0.6 copy.6
  (2 shorter events, 0.0 us)
Async XLA Ops:
  22.9 7.7 %collective-permute-start.1 = (f32[4,32,896]{2,1,0:T(8,128)S(1)}, f32[4,32,896]{2,1,0:T(8,128)S(1)}, u32[]{:S(2)}, u32[]{:S(2)}) collective-permute-start(f32[4,32,896]{2,1,0:T(8,128)S(1)} %get-tuple-element.19), channel_id=1, source_target_pairs={{0,1},{1,0},{2,3},{3,2},{4,5},{5,4},{6,7},{7,6},{8,9},{9,8},{10,11... | collective-permute-start | bytes 1376264 | tf_op jit(solution)/shard_map/ppermute | solution.py:321
  25.1 12.1 %collective-permute-start = (s16[16,32,128]{2,1,0:T(8,128)(2,1)S(1)}, s16[16,32,128]{2,1,0:T(8,128)(2,1)S(1)}, u32[]{:S(2)}, u32[]{:S(2)}) collective-permute-start(s16[16,32,128]{2,1,0:T(8,128)(2,1)S(1)} %all_to_all.14.x_ref.refs_0_), channel_id=1, source_target_pairs={{0,134},{1,135},{2,132},{3,133},{4,130},{5,131},{6,128},{7,129},{8... | collective-permute-start | bytes 393224 | tf_op jit(solution)/shard_map/ppermute | solution.py:314
  30.6 45.7 %slice-start = ((s8[7340032]{0:T(1024)(128)(4,1)}), s8[4194304]{0:T(1024)(128)(4,1)S(1)}, s32[]{:S(2)}) async-start(s8[7340032]{0:T(1024)(128)(4,1)} %bitcast.6), calls=%async_computation.2 | async-start | bytes 8388608
  37.2 39.2 %slice-start.1 = ((s8[7340032]{0:T(1024)(128)(4,1)}), s8[3145728]{0:T(1024)(128)(4,1)S(1)}, s32[]{:S(2)}) async-start(s8[7340032]{0:T(1024)(128)(4,1)} %bitcast.6), calls=%async_computation.3 | async-start | bytes 6291456
  43.6 10.5 %collective-permute-start.2 = (f32[4,32,896]{2,1,0:T(8,128)S(1)}, f32[4,32,896]{2,1,0:T(8,128)S(1)}, u32[]{:S(2)}, u32[]{:S(2)}) collective-permute-start(f32[4,32,896]{2,1,0:T(8,128)S(1)} %get-tuple-element.24), channel_id=1, source_target_pairs={{0,1},{1,0},{2,3},{3,2},{4,5},{5,4},{6,7},{7,6},{8,9},{9,8},{10,11... | collective-permute-start | bytes 1376264 | tf_op jit(solution)/shard_map/ppermute | solution.py:321
  44.4 3.6 %collective-permute-start.13 = (s16[32,1024]{1,0:T(8,128)(2,1)S(1)}, s16[32,1024]{1,0:T(8,128)(2,1)S(1)}, u32[]{:S(2)}, u32[]{:S(2)}) collective-permute-start(s16[32,1024]{1,0:T(8,128)(2,1)S(1)} %get-tuple-element.20.refs_0_), channel_id=1, source_target_pairs={{0,2},{1,3},{2,0},{3,1},{4,6},{5,7},{6,4},{7,5},{8,10},{9,11},{10,... | collective-permute-start | bytes 196616 | tf_op jit(solution)/shard_map/ppermute | solution.py:298
  44.4 4.3 %collective-permute-start.14 = (s16[32,1024]{1,0:T(8,128)(2,1)S(1)}, s16[32,1024]{1,0:T(8,128)(2,1)S(1)}, u32[]{:S(2)}, u32[]{:S(2)}) collective-permute-start(s16[32,1024]{1,0:T(8,128)(2,1)S(1)} %get-tuple-element.21.refs_1_), channel_id=1, source_target_pairs={{0,4},{1,5},{2,6},{3,7},{4,0},{5,1},{6,2},{7,3},{8,12},{9,13},{10,... | collective-permute-start | bytes 196616 | tf_op jit(solution)/shard_map/ppermute | solution.py:298
  46.3 4.9 %collective-permute-start.15 = (s16[32,1024]{1,0:T(8,128)(2,1)S(1)}, s16[32,1024]{1,0:T(8,128)(2,1)S(1)}, u32[]{:S(2)}, u32[]{:S(2)}) collective-permute-start(s16[32,1024]{1,0:T(8,128)(2,1)S(1)} %get-tuple-element.22.refs_2_), channel_id=1, source_target_pairs={{0,6},{1,7},{2,4},{3,5},{4,2},{5,3},{6,0},{7,1},{8,14},{9,15},{10,... | collective-permute-start | bytes 196616 | tf_op jit(solution)/shard_map/ppermute | solution.py:298
  51.3 6.6 %collective-permute-start.16 = (s16[32,1024]{1,0:T(8,128)(2,1)S(1)}, s16[32,1024]{1,0:T(8,128)(2,1)S(1)}, u32[]{:S(2)}, u32[]{:S(2)}) collective-permute-start(s16[32,1024]{1,0:T(8,128)(2,1)S(1)} %shard_map.64.refs_1_), channel_id=1, source_target_pairs={{0,2},{1,3},{2,0},{3,1},{4,6},{5,7},{6,4},{7,5},{8,10},{9,11},{10,... | collective-permute-start | bytes 196616 | tf_op jit(solution)/shard_map/ppermute | solution.py:298
  53.6 5.9 %collective-permute-start.17 = (s16[32,1024]{1,0:T(8,128)(2,1)S(1)}, s16[32,1024]{1,0:T(8,128)(2,1)S(1)}, u32[]{:S(2)}, u32[]{:S(2)}) collective-permute-start(s16[32,1024]{1,0:T(8,128)(2,1)S(1)} %shard_map.64.refs_1_), channel_id=1, source_target_pairs={{0,4},{1,5},{2,6},{3,7},{4,0},{5,1},{6,2},{7,3},{8,12},{9,13},{10,... | collective-permute-start | bytes 196616 | tf_op jit(solution)/shard_map/ppermute | solution.py:298
  54.2 9.9 %collective-permute-start.3 = (s16[32,1024]{1,0:T(8,128)(2,1)S(1)}, s16[32,1024]{1,0:T(8,128)(2,1)S(1)}, u32[]{:S(2)}, u32[]{:S(2)}) collective-permute-start(s16[32,1024]{1,0:T(8,128)(2,1)S(1)} %get-tuple-element.26), channel_id=1, source_target_pairs={{0,2},{1,3},{2,0},{3,1},{4,6},{5,7},{6,4},{7,5},{8,10},{9,11},{10,... | collective-permute-start | bytes 196616 | tf_op jit(solution)/shard_map/ppermute | solution.py:298
  55.7 9.2 %collective-permute-start.4 = (s16[32,1024]{1,0:T(8,128)(2,1)S(1)}, s16[32,1024]{1,0:T(8,128)(2,1)S(1)}, u32[]{:S(2)}, u32[]{:S(2)}) collective-permute-start(s16[32,1024]{1,0:T(8,128)(2,1)S(1)} %get-tuple-element.27), channel_id=1, source_target_pairs={{0,4},{1,5},{2,6},{3,7},{4,0},{5,1},{6,2},{7,3},{8,12},{9,13},{10,... | collective-permute-start | bytes 196616 | tf_op jit(solution)/shard_map/ppermute | solution.py:298
  56.2 10.6 %collective-permute-start.5 = (s16[32,1024]{1,0:T(8,128)(2,1)S(1)}, s16[32,1024]{1,0:T(8,128)(2,1)S(1)}, u32[]{:S(2)}, u32[]{:S(2)}) collective-permute-start(s16[32,1024]{1,0:T(8,128)(2,1)S(1)} %get-tuple-element.28), channel_id=1, source_target_pairs={{0,6},{1,7},{2,4},{3,5},{4,2},{5,3},{6,0},{7,1},{8,14},{9,15},{10,... | collective-permute-start | bytes 196616 | tf_op jit(solution)/shard_map/ppermute | solution.py:298
  57.9 9.5 %collective-permute-start.18 = (s16[32,1024]{1,0:T(8,128)(2,1)S(1)}, s16[32,1024]{1,0:T(8,128)(2,1)S(1)}, u32[]{:S(2)}, u32[]{:S(2)}) collective-permute-start(s16[32,1024]{1,0:T(8,128)(2,1)S(1)} %shard_map.64.refs_1_), channel_id=1, source_target_pairs={{0,6},{1,7},{2,4},{3,5},{4,2},{5,3},{6,0},{7,1},{8,14},{9,15},{10,... | collective-permute-start | bytes 196616 | tf_op jit(solution)/shard_map/ppermute | solution.py:298
  59.5 9.6 %collective-permute-start.19 = (s16[32,1024]{1,0:T(8,128)(2,1)S(1)}, s16[32,1024]{1,0:T(8,128)(2,1)S(1)}, u32[]{:S(2)}, u32[]{:S(2)}) collective-permute-start(s16[32,1024]{1,0:T(8,128)(2,1)S(1)} %shard_map.64.refs_1_), channel_id=1, source_target_pairs={{0,1},{1,0},{2,3},{3,2},{4,5},{5,4},{6,7},{7,6},{8,9},{9,8},{10,11... | collective-permute-start | bytes 196616 | tf_op jit(solution)/shard_map/ppermute | solution.py:331
  64.1 6.6 %collective-permute-start.20 = (s16[32,1024]{1,0:T(8,128)(2,1)S(1)}, s16[32,1024]{1,0:T(8,128)(2,1)S(1)}, u32[]{:S(2)}, u32[]{:S(2)}) collective-permute-start(s16[32,1024]{1,0:T(8,128)(2,1)S(1)} %collective-permute-done.16.refs_2_), channel_id=1, source_target_pairs={{0,1},{1,0},{2,3},{3,2},{4,5},{5,4},{6,7},{7,6},{8,9},{9,8},{10,11... | collective-permute-start | bytes 196616 | tf_op jit(solution)/shard_map/ppermute | solution.py:331
  64.8 7.3 %collective-permute-start.21 = (s16[32,1024]{1,0:T(8,128)(2,1)S(1)}, s16[32,1024]{1,0:T(8,128)(2,1)S(1)}, u32[]{:S(2)}, u32[]{:S(2)}) collective-permute-start(s16[32,1024]{1,0:T(8,128)(2,1)S(1)} %collective-permute-done.17.refs_3_), channel_id=1, source_target_pairs={{0,1},{1,0},{2,3},{3,2},{4,5},{5,4},{6,7},{7,6},{8,9},{9,8},{10,11... | collective-permute-start | bytes 196616 | tf_op jit(solution)/shard_map/ppermute | solution.py:331
  67.0 5.3 %collective-permute-start.6 = (s16[32,1024]{1,0:T(8,128)(2,1)S(1)}, s16[32,1024]{1,0:T(8,128)(2,1)S(1)}, u32[]{:S(2)}, u32[]{:S(2)}) collective-permute-start(s16[32,1024]{1,0:T(8,128)(2,1)S(1)} %shard_map.63.refs_10_.refs_1_), channel_id=1, source_target_pairs={{0,2},{1,3},{2,0},{3,1},{4,6},{5,7},{6,4},{7,5},{8,10},{9,11},{10,... | collective-permute-start | bytes 196616 | tf_op jit(solution)/shard_map/ppermute | solution.py:298
  67.4 5.3 %collective-permute-start.7 = (s16[32,1024]{1,0:T(8,128)(2,1)S(1)}, s16[32,1024]{1,0:T(8,128)(2,1)S(1)}, u32[]{:S(2)}, u32[]{:S(2)}) collective-permute-start(s16[32,1024]{1,0:T(8,128)(2,1)S(1)} %shard_map.63.refs_10_.refs_1_), channel_id=1, source_target_pairs={{0,4},{1,5},{2,6},{3,7},{4,0},{5,1},{6,2},{7,3},{8,12},{9,13},{10,... | collective-permute-start | bytes 196616 | tf_op jit(solution)/shard_map/ppermute | solution.py:298
  69.1 7.3 %collective-permute-start.8 = (s16[32,1024]{1,0:T(8,128)(2,1)S(1)}, s16[32,1024]{1,0:T(8,128)(2,1)S(1)}, u32[]{:S(2)}, u32[]{:S(2)}) collective-permute-start(s16[32,1024]{1,0:T(8,128)(2,1)S(1)} %shard_map.63.refs_10_.refs_1_), channel_id=1, source_target_pairs={{0,6},{1,7},{2,4},{3,5},{4,2},{5,3},{6,0},{7,1},{8,14},{9,15},{10,... | collective-permute-start | bytes 196616 | tf_op jit(solution)/shard_map/ppermute | solution.py:298
  70.7 5.7 %collective-permute-start.22 = (s16[32,1024]{1,0:T(8,128)(2,1)S(1)}, s16[32,1024]{1,0:T(8,128)(2,1)S(1)}, u32[]{:S(2)}, u32[]{:S(2)}) collective-permute-start(s16[32,1024]{1,0:T(8,128)(2,1)S(1)} %collective-permute-done.18.refs_4_), channel_id=1, source_target_pairs={{0,1},{1,0},{2,3},{3,2},{4,5},{5,4},{6,7},{7,6},{8,9},{9,8},{10,11... | collective-permute-start | bytes 196616 | tf_op jit(solution)/shard_map/ppermute | solution.py:331
  72.2 9.1 %collective-permute-start.9 = (s16[32,1024]{1,0:T(8,128)(2,1)S(1)}, s16[32,1024]{1,0:T(8,128)(2,1)S(1)}, u32[]{:S(2)}, u32[]{:S(2)}) collective-permute-start(s16[32,1024]{1,0:T(8,128)(2,1)S(1)} %shard_map.63.refs_10_.refs_1_), channel_id=1, source_target_pairs={{0,1},{1,0},{2,3},{3,2},{4,5},{5,4},{6,7},{7,6},{8,9},{9,8},{10,11... | collective-permute-start | bytes 196616 | tf_op jit(solution)/shard_map/ppermute | solution.py:331
  72.2 9.0 %collective-permute-start.10 = (s16[32,1024]{1,0:T(8,128)(2,1)S(1)}, s16[32,1024]{1,0:T(8,128)(2,1)S(1)}, u32[]{:S(2)}, u32[]{:S(2)}) collective-permute-start(s16[32,1024]{1,0:T(8,128)(2,1)S(1)} %collective-permute-done.6.refs_2_), channel_id=1, source_target_pairs={{0,1},{1,0},{2,3},{3,2},{4,5},{5,4},{6,7},{7,6},{8,9},{9,8},{10,11... | collective-permute-start | bytes 196616 | tf_op jit(solution)/shard_map/ppermute | solution.py:331
  72.7 8.6 %collective-permute-start.11 = (s16[32,1024]{1,0:T(8,128)(2,1)S(1)}, s16[32,1024]{1,0:T(8,128)(2,1)S(1)}, u32[]{:S(2)}, u32[]{:S(2)}) collective-permute-start(s16[32,1024]{1,0:T(8,128)(2,1)S(1)} %collective-permute-done.7.refs_3_), channel_id=1, source_target_pairs={{0,1},{1,0},{2,3},{3,2},{4,5},{5,4},{6,7},{7,6},{8,9},{9,8},{10,11... | collective-permute-start | bytes 196616 | tf_op jit(solution)/shard_map/ppermute | solution.py:331
  76.4 4.9 %collective-permute-start.12 = (s16[32,1024]{1,0:T(8,128)(2,1)S(1)}, s16[32,1024]{1,0:T(8,128)(2,1)S(1)}, u32[]{:S(2)}, u32[]{:S(2)}) collective-permute-start(s16[32,1024]{1,0:T(8,128)(2,1)S(1)} %collective-permute-done.8.refs_4_), channel_id=1, source_target_pairs={{0,1},{1,0},{2,3},{3,2},{4,5},{5,4},{6,7},{7,6},{8,9},{9,8},{10,11... | collective-permute-start | bytes 196616 | tf_op jit(solution)/shard_map/ppermute | solution.py:331
